TPU v7x, 512 devices: a whole 4x8x8 slice. The times are simulated.
512 devices in a mesh: gx: 8 (over z), gy: 8 (over y_lo, core), gz: 8 (over y_hi, x).
Axes of the slice: x: 4, y: 8 (y_hi: 2, y_lo: 4; y = y_hi * 4 + y_lo), z: 8, core: 2. Of those that a mesh axis runs over, the one named last changes fastest.
Arguments:
- x_in: bfloat16 [3072, 5120], P(('gy', 'gx'), 'gz'), may hold values from -190 to 190
- gain: float32 [5120], P('gz'), may hold values from 0.25 to 1.75
- w_up: bfloat16 [5120, 7168], P(('gz', 'gy'), 'gx'), may hold values from -0.078125 to 0.078125
- w_down: bfloat16 [7168, 5120], P(('gx', 'gy'), 'gz'), may hold values from -0.0625 to 0.0625
- d_out: bfloat16 [3072, 5120], P(('gy', 'gx'), 'gz'), may hold values from -1.1953125 to 1.1953125
Outputs:
- d_x: bfloat16 [3072, 5120], P(('gy', 'gx'), 'gz')
- d_w_up: bfloat16 [5120, 7168], P(('gz', 'gy'), 'gx')
- d_w_down: bfloat16 [7168, 5120], P(('gx', 'gy'), 'gz')
- d_gain: float32 [5120], P('gz')
All inputs are finite; a program needn't handle non-finite values.
Results may differ from a plain program's by a relative error of at most 0.02.
Values may be sent and summed in bfloat16 or wider, within the bound.
No kernel may reach another device: no remote copies, remote signals or barrier semaphores. Data moves between devices by JAX's collectives and lax.ppermute only.
A program may use at most 64 MiB of HBM per device.

v0:
```python
import jax
import jax.numpy as jnp
from jax import lax
from jax.sharding import PartitionSpec as P


def gelu_pair(hidden):
    cdf = 0.5 * (1.0 + jax.scipy.special.erf(hidden * 0.7071067811865476))
    slope = cdf + hidden * jnp.exp(-0.5 * hidden * hidden) * 0.3989422804014327
    return (hidden * cdf, slope)


def body(x_in, gain, w_up, w_down, d_out):
    width = x_in.shape[1] * lax.axis_size("gz")
    xf = x_in.astype(jnp.float32)
    total = lax.psum(jnp.sum(xf, axis=1), "gz")
    mean = total / width
    centered = xf - mean[:, None]
    var = lax.psum(jnp.sum(centered * centered, axis=1), "gz") / width
    inv = lax.rsqrt(var + 1e-05)[:, None]
    normed = centered * inv
    z_local = (normed * gain).astype(jnp.bfloat16)
    up_full = lax.all_gather(w_up, "gy", axis=0, tiled=True)
    z_rows = lax.all_gather(z_local, "gx", axis=0, tiled=True)
    part_rows = z_rows
    hidden = lax.psum_scatter(
        jnp.dot(part_rows, up_full, preferred_element_type=jnp.float32).astype(jnp.bfloat16),
        "gz",
        scatter_dimension=0,
        tiled=True,
    ).astype(jnp.float32)
    act_f, slope = gelu_pair(hidden)
    act = act_f.astype(jnp.bfloat16)
    down_full = lax.all_gather(w_down, "gy", axis=0, tiled=True)
    out_rows = lax.all_gather(d_out, "gx", axis=0, tiled=True)
    act_rows = lax.all_gather(act, "gz", axis=0, tiled=True)
    part_rows = out_rows
    d_act = lax.psum_scatter(
        lax.dot_general(
            part_rows, down_full, (((1,), (1,)), ((), ())), preferred_element_type=jnp.float32
        ).astype(jnp.bfloat16),
        "gz",
        scatter_dimension=0,
        tiled=True,
    ).astype(jnp.float32)
    d_hidden = (d_act * slope).astype(jnp.bfloat16)
    hgrad_rows = lax.all_gather(d_hidden, "gz", axis=0, tiled=True)
    columns = act_rows
    d_w_down = lax.psum_scatter(
        lax.dot_general(
            columns, out_rows, (((0,), (0,)), ((), ())), preferred_element_type=jnp.float32
        ).astype(jnp.bfloat16),
        "gy",
        scatter_dimension=0,
        tiled=True,
    )
    columns = z_rows
    d_w_up = lax.psum_scatter(
        lax.dot_general(
            columns, hgrad_rows, (((0,), (0,)), ((), ())), preferred_element_type=jnp.float32
        ).astype(jnp.bfloat16),
        "gy",
        scatter_dimension=0,
        tiled=True,
    )
    part_rows = hgrad_rows
    d_z = lax.psum_scatter(
        lax.dot_general(
            part_rows, up_full, (((1,), (1,)), ((), ())), preferred_element_type=jnp.float32
        ).astype(jnp.bfloat16),
        "gx",
        scatter_dimension=0,
        tiled=True,
    ).astype(jnp.float32)
    d_gain = lax.psum(jnp.sum(d_z * normed, axis=0), ("gx", "gy"))
    d_scaled = d_z * gain
    scaled_sum, cross_sum = lax.psum(
        (jnp.sum(d_scaled, axis=1), jnp.sum(d_scaled * normed, axis=1)), "gz"
    )
    d_x = inv * (d_scaled - scaled_sum[:, None] / width - normed * (cross_sum[:, None] / width))
    return (d_x.astype(jnp.bfloat16), d_w_up, d_w_down, d_gain)


def solution(mesh):
    placed = (
        P(("gy", "gx"), "gz"),
        P("gz"),
        P(("gz", "gy"), "gx"),
        P(("gx", "gy"), "gz"),
        P(("gy", "gx"), "gz"),
    )
    return jax.shard_map(
        body,
        mesh=mesh,
        in_specs=placed,
        out_specs=(P(("gy", "gx"), "gz"), P(("gz", "gy"), "gx"), P(("gx", "gy"), "gz"), P("gz")),
        check_vma=False,
    )
```

profile of v0, /device:TPU:1, one launch (start us, length us, event | category | flops | bytes accessed | tf_op | source)
XLA Modules:
  0.0 543.6 jit_solution(16610349977316155122)
XLA Ops:
  7.2 0.0 all-gather.3.cloned.1.call-start
  7.2 0.7 all-gather.3.cloned.1.call-update
  7.9 0.0 all-gather.5.cloned.1.call-start
  7.9 0.7 all-gather.5.cloned.1.call-update
  8.6 0.0 reduce-scatter.6.cloned.1.call-start
  8.7 27.0 %all_gather.18 = bf16[384,640]{1,0:T(8,128)(2,1)S(1)} all-gather(bf16[48,640]{1,0:T(8,128)(2,1)} %param.9), channel_id=1, replica_groups=mesh['gx'=8,'gy'=8,'gz'=8] {'gx'}, dimensions={0}, use_global_device_ids=true | all-gather | bytes 552960 | tf_op jit(solution)/shard_map/all_gather | solution.py:35
  35.7 0.0 copy-start
  35.7 0.0 copy-start.1
  35.7 17.8 %all-gather.3.cloned.1.call-done = bf16[896,640]{1,0:T(8,128)(2,1)} async-done(((bf16[112,640]{1,0:T(8,128)(2,1)}), bf16[896,640]{1,0:T(8,128)(2,1)}) %all-gather.3.cloned.1.call-update) | async-done | bytes 1146896 | tf_op jit(solution)/shard_map/all_gather | solution.py:34
  53.5 2.9 convolution_convert_fusion.3
  56.4 0.0 reduce-scatter.6.cloned.1.call-update
  56.4 0.0 reduce-scatter.8.cloned.1.call-start
  56.5 0.0 copy-done
  56.5 0.1 convert_reduce_fusion
  56.6 26.6 %psum.35 = f32[48]{0:T(128)S(1)} all-reduce(f32[48]{0:T(128)S(1)} %convert_reduce_fusion), channel_id=1, replica_groups=mesh['gx'=8,'gy'=8,'gz'=8] {'gz'}, use_global_device_ids=true, to_apply=%region_1.0 | all-reduce | flops 48 | bytes 384 | tf_op jit(solution)/shard_map/psum | solution.py:16
  83.2 0.2 fusion.20
  83.4 20.3 %psum.36 = f32[48]{0:T(128)S(1)} all-reduce(f32[48]{0:T(128)S(1)} %fusion.20), channel_id=1, replica_groups=mesh['gx'=8,'gy'=8,'gz'=8] {'gz'}, use_global_device_ids=true, to_apply=%region_3.0 | all-reduce | flops 48 | bytes 384 | tf_op jit(solution)/shard_map/psum | solution.py:19
  103.7 0.0 copy-done.1
  103.7 0.1 fusion.16
  103.8 22.4 %all_gather.20 = bf16[384,640]{1,0:T(8,128)(2,1)S(1)} all-gather(bf16[48,640]{1,0:T(8,128)(2,1)S(1)} %fusion.16), channel_id=1, replica_groups=mesh['gx'=8,'gy'=8,'gz'=8] {'gx'}, dimensions={0}, use_global_device_ids=true | all-gather | bytes 552960 | tf_op jit(solution)/shard_map/all_gather | solution.py:24
  126.3 0.0 all-gather.5.cloned.1.call-done
  126.3 2.9 convolution_convert_fusion.2
  129.2 0.0 copy-start.2
  129.2 0.0 reduce-scatter.8.cloned.1.call-update
  129.2 0.0 reduce-scatter.10.cloned.1.call-start
  129.3 56.7 %reduce-scatter.6.cloned.1.call-done = bf16[48,896]{1,0:T(8,128)(2,1)} async-done(((bf16[384,896]{1,0:T(8,128)(2,1)}), bf16[48,896]{1,0:T(8,128)(2,1)}) %reduce-scatter.6.cloned.1.call-update) | async-done | bytes 86032 | tf_op jit(solution)/shard_map/reduce_scatter | solution.py:38
  185.9 88.3 %reduce-scatter.8.cloned.1.call-done = bf16[48,896]{1,0:T(8,128)(2,1)} async-done(((bf16[384,896]{1,0:T(8,128)(2,1)}), bf16[48,896]{1,0:T(8,128)(2,1)}) %reduce-scatter.8.cloned.1.call-update) | async-done | bytes 86032 | tf_op jit(solution)/shard_map/reduce_scatter | solution.py:26
  274.3 1.0 fusion.8
  275.3 39.4 %all_gather.22 = bf16[384,896]{1,0:T(8,128)(2,1)S(1)} all-gather(bf16[48,896]{1,0:T(8,128)(2,1)S(1)} %get-tuple-element.10), channel_id=1, replica_groups=mesh['gx'=8,'gy'=8,'gz'=8] {'gz'}, dimensions={0}, use_global_device_ids=true | all-gather | bytes 774144 | tf_op jit(solution)/shard_map/all_gather | solution.py:47
  314.7 0.0 copy-done.2
  314.7 1.6 convolution_convert_fusion.4
  316.3 0.0 reduce-scatter.10.cloned.1.call-update
  316.3 0.0 reduce-scatter.14.cloned.1.call-start
  316.4 41.4 %all_gather.23 = bf16[384,896]{1,0:T(8,128)(2,1)S(1)} all-gather(bf16[48,896]{1,0:T(8,128)(2,1)S(1)} %get-tuple-element.9), channel_id=1, replica_groups=mesh['gx'=8,'gy'=8,'gz'=8] {'gz'}, dimensions={0}, use_global_device_ids=true | all-gather | bytes 774144 | tf_op jit(solution)/shard_map/all_gather | solution.py:36
  357.8 1.9 convolution_convert_fusion
  359.7 0.0 reduce-scatter.14.cloned.1.call-update
  359.7 0.0 reduce-scatter.12.cloned.1.call-start
  359.8 1.9 convolution_convert_fusion.1
  361.6 0.0 reduce-scatter.12.cloned.1.call-update
  361.6 0.0 reduce-scatter.10.cloned.1.call-done
  361.7 1.0 fusion.22
  362.7 23.1 %all-reduce = (f32[48]{0:T(128)S(1)}, f32[48]{0:T(128)S(1)}) all-reduce(f32[48]{0:T(128)S(1)} %get-tuple-element.5, f32[48]{0:T(128)S(1)} %get-tuple-element.6), channel_id=1, replica_groups=mesh['gx'=8,'gy'=8,'gz'=8] {'gz'}, use_global_device_ids=true, to_apply=%region_10.0 | all-reduce | flops 96 | bytes 768 | tf_op jit(solution)/shard_map/psum | solution.py:77
  385.9 149.4 %psum.39 = f32[640]{0:T(1024)} all-reduce(f32[640]{0:T(1024)S(1)} %get-tuple-element.4), channel_id=1, replica_groups=mesh['gx'=8,'gy'=8,'gz'=8] {'gx','gy'}, use_global_device_ids=true, to_apply=%region_14.0 | all-reduce | flops 640 | bytes 5120 | tf_op jit(solution)/shard_map/psum | solution.py:75
  535.2 1.6 fusion.19
  536.8 0.0 reduce-scatter.14.cloned.1.call-done
  536.8 0.0 reduce-scatter.12.cloned.1.call-done
  (3 shorter events, 0.0 us)
Async XLA Ops:
  7.2 46.4 %all-gather.3.cloned.1.call-start = ((), (), s32[]{:S(2)}) async-start(), calls=%async_computation.5 | async-start | bytes 1290240 | tf_op jit(solution)/shard_map/all_gather | solution.py:34
  7.9 118.4 %all-gather.5.cloned.1.call-start = ((), (), s32[]{:S(2)}) async-start(), calls=%async_computation.7 | async-start | bytes 1290240 | tf_op jit(solution)/shard_map/all_gather | solution.py:23
  8.6 177.3 %reduce-scatter.6.cloned.1.call-start = ((), (), s32[]{:S(2)}) async-start(), calls=%async_computation.6 | async-start | bytes 774144 | tf_op jit(solution)/shard_map/reduce_scatter | solution.py:38
  35.7 20.8 %copy-start = (bf16[48,640]{1,0:T(8,128)(2,1)S(1)}, bf16[48,640]{1,0:T(8,128)(2,1)}, u32[]{:S(2)}) copy-start(bf16[48,640]{1,0:T(8,128)(2,1)} %param.5) | copy-start | bytes 184324
  35.7 68.0 %copy-start.1 = (f32[640]{0:T(1024)S(1)}, f32[640]{0:T(1024)}, u32[]{:S(2)}) copy-start(f32[640]{0:T(1024)} %param.6) | copy-start | bytes 7684
  56.4 217.8 %reduce-scatter.8.cloned.1.call-start = ((), (), s32[]{:S(2)}) async-start(), calls=%async_computation.8 | async-start | bytes 774144 | tf_op jit(solution)/shard_map/reduce_scatter | solution.py:26
  129.2 185.5 %copy-start.2 = (bf16[640,896]{1,0:T(8,128)(2,1)S(1)}, bf16[640,896]{1,0:T(8,128)(2,1)}, u32[]{:S(2)}) copy-start(bf16[640,896]{1,0:T(8,128)(2,1)} %all-gather.5.cloned.1.call-done) | copy-start | bytes 3440644
  129.2 232.5 %reduce-scatter.10.cloned.1.call-start = ((), (), s32[]{:S(2)}) async-start(), calls=%async_computation.9 | async-start | bytes 552960 | tf_op jit(solution)/shard_map/reduce_scatter | solution.py:67
  316.3 220.5 %reduce-scatter.14.cloned.1.call-start = ((), (), s32[]{:S(2)}) async-start(), calls=%async_computation.11 | async-start | bytes 1290240 | tf_op jit(solution)/shard_map/reduce_scatter | solution.py:49
  359.7 177.1 %reduce-scatter.12.cloned.1.call-start = ((), (), s32[]{:S(2)}) async-start(), calls=%async_computation.10 | async-start | bytes 1290240 | tf_op jit(solution)/shard_map/reduce_scatter | solution.py:58
Sparse Core Ops, SparseCore 0:
  10.1 43.4 all-gather.2
  55.6 39.0 all-gather.4
  99.2 86.6 reduce-scatter.5
  191.0 83.2 reduce-scatter.7
  316.5 40.0 reduce-scatter.9
  360.0 47.1 reduce-scatter.13
  410.9 39.1 reduce-scatter.11
where the time goes:
time: 544 us
  blocking collectives  350 us (64%)
  waiting for transfers between devices  164 us (30%)
  between operations  14.2 us (3%)
  matrix products  11.1 us (2%)
    psum x1, blocking collectives, body(): d_gain = lax.psum(jnp.sum(d_z * normed, axis=0), ('gx', 'gy'))  149 us
    reduce_scatter x1, waiting for transfers between devices, body(): lax.psum_scatter(jnp.dot(part_rows, up_full, preferred_element_type=jnp.f...  88.3 us
    reduce_scatter x1, waiting for transfers between devices, body(): lax.psum_scatter(lax.dot_general(part_rows, down_full, (((1,), (1,)), (()...  56.7 us
    all_gather x1, blocking collectives, body(): act_rows = lax.all_gather(act, 'gz', axis=0, tiled=True)  41.4 us
    all_gather x1, blocking collectives, body(): hgrad_rows = lax.all_gather(d_hidden, 'gz', axis=0, tiled=True)  39.4 us
    all_gather x1, blocking collectives, body(): out_rows = lax.all_gather(d_out, 'gx', axis=0, tiled=True)  27 us
    psum x1, blocking collectives, body(): total = lax.psum(jnp.sum(xf, axis=1), 'gz')  26.6 us
    psum x1, blocking collectives, body(): lax.psum((jnp.sum(d_scaled, axis=1), jnp.sum(d_scaled * normed, axis=1)),...  23.1 us
  transfers between devices with their start and end apart: 7, of which 3 were waited for; matrix products, arithmetic and copies ran while one was open for 2% of the time, Pallas kernels for 0%

commit v1 on v0

v1 whole, which is shorter than its diff:
```python
import jax
import jax.numpy as jnp
from jax import lax
from jax.sharding import PartitionSpec as P

BF, F32 = jnp.bfloat16, jnp.float32


def gelu_pair(hidden):
    cdf = 0.5 * (1.0 + jax.scipy.special.erf(hidden * 0.7071067811865476))
    slope = cdf + hidden * jnp.exp(-0.5 * hidden * hidden) * 0.3989422804014327
    return (hidden * cdf, slope)


def exchange(blocks, axis):
    return lax.all_to_all(blocks, axis, 0, 0, tiled=True)


def spread(value, axis):
    n = lax.axis_size(axis)
    return exchange(jnp.broadcast_to(value[None], (n, *value.shape)), axis)


def summed(blocks):
    return jnp.sum(blocks.astype(F32), axis=0)


def body(x_in, gain, w_up, w_down, d_out):
    rows, local = x_in.shape
    n_gx, n_gy, n_gz = (lax.axis_size(a) for a in ("gx", "gy", "gz"))
    width = local * n_gz
    hid = w_up.shape[1]
    all_rows = rows * n_gx
    block = all_rows // n_gz

    down_full = lax.all_gather(w_down, "gy", axis=0, tiled=True)
    up_full = spread(w_up, "gy").reshape(-1, hid)
    both = lax.all_gather(jnp.concatenate([x_in, d_out], axis=1), "gx", axis=0, tiled=True)
    both, up_full = lax.optimization_barrier((both, up_full))
    x_rows, out_rows = both[:, :local].astype(F32), both[:, local:]

    part_sum = jnp.sum(x_rows, axis=1)
    off = x_rows - (part_sum / local)[:, None]
    stats = spread(jnp.stack([part_sum, jnp.sum(off * off, axis=1)]), "gz")
    sums, seconds = stats[:, 0], stats[:, 1]
    mean = jnp.sum(sums, axis=0) / width
    shift = sums / local - mean
    var = (jnp.sum(seconds, axis=0) + local * jnp.sum(shift * shift, axis=0)) / width
    inv = lax.rsqrt(var + 1e-05)
    normed = (x_rows - mean[:, None]) * inv[:, None]
    z = (normed * gain).astype(BF)

    hid_part = jnp.dot(z, up_full, preferred_element_type=F32).astype(BF)
    dact_part = lax.dot_general(
        out_rows, down_full, (((1,), (1,)), ((), ())), preferred_element_type=F32
    ).astype(BF)
    pair = jnp.concatenate([hid_part, dact_part], axis=1).reshape(n_gz, block, 2 * hid)
    pair = summed(exchange(pair, "gz"))
    hidden, d_act = pair[:, :hid], pair[:, hid:]
    act_f, slope = gelu_pair(hidden)
    d_hidden = (d_act * slope).astype(BF)
    cross = jnp.sum(d_hidden.astype(F32) * hidden, axis=1)
    tilt = jnp.sum(up_full.astype(F32) * gain[:, None], axis=0)
    small = lax.all_gather(jnp.concatenate([tilt, cross]), "gz")
    acts = spread(jnp.concatenate([act_f.astype(BF), d_hidden], axis=1), "gz")
    acts, small = lax.optimization_barrier((acts, small))
    acts = acts.reshape(all_rows, 2 * hid)
    act_rows, hgrad_rows = acts[:, :hid], acts[:, hid:]
    tilt = jnp.sum(small[:, :hid], axis=0)
    cross = small[:, hid:].reshape(all_rows)

    dz_part = lax.dot_general(
        hgrad_rows, up_full, (((1,), (1,)), ((), ())), preferred_element_type=F32
    )
    level = jnp.sum(hgrad_rows.astype(F32) * tilt, axis=1)
    gain_part = jnp.sum(dz_part * normed, axis=0)
    tail = lax.psum(jnp.concatenate([level, cross, gain_part]), "gx")
    d_w_up = lax.dot_general(
        z, hgrad_rows, (((0,), (0,)), ((), ())), preferred_element_type=F32
    ).astype(BF)
    d_w_up, tail = lax.optimization_barrier((d_w_up, tail))
    d_gain = jnp.sum(lax.all_gather(tail[2 * all_rows :], "gy"), axis=0)

    d_z = summed(exchange(dz_part.astype(BF).reshape(n_gx, rows, local), "gx"))
    d_w_down = lax.psum_scatter(
        lax.dot_general(
            act_rows, out_rows, (((0,), (0,)), ((), ())), preferred_element_type=F32
        ).astype(BF),
        "gy",
        scatter_dimension=0,
        tiled=True,
    )
    d_w_up = summed(exchange(d_w_up.reshape(n_gy, -1, hid), "gy")).astype(BF)

    first = lax.axis_index("gx") * rows

    def own(values):
        return lax.dynamic_slice(values, (first,), (rows,))[:, None]

    own_inv = own(inv)
    own_normed = (x_in.astype(F32) - own(mean)) * own_inv
    scaled_sum, cross_sum = own(tail[:all_rows]), own(tail[all_rows : 2 * all_rows])
    d_x = own_inv * (d_z * gain - scaled_sum / width - own_normed * (cross_sum / width))
    return (d_x.astype(BF), d_w_up, d_w_down, d_gain)


def solution(mesh):
    placed = (
        P(("gy", "gx"), "gz"),
        P("gz"),
        P(("gz", "gy"), "gx"),
        P(("gx", "gy"), "gz"),
        P(("gy", "gx"), "gz"),
    )
    return jax.shard_map(
        body,
        mesh=mesh,
        in_specs=placed,
        out_specs=(P(("gy", "gx"), "gz"), P(("gz", "gy"), "gx"), P(("gx", "gy"), "gz"), P("gz")),
        check_vma=False,
    )
```

time: 544 us -> 274 us (0.50)
  blocking collectives: 350 us -> 163 us
  waiting for transfers between devices: 164 us -> 15.4 us
  starting transfers between devices: 0.28 us -> 59.6 us
  local copies, waits for them, and re-layouts: 0.01 us -> 6.99 us
    psum x4 -> x1, blocking collectives: 219 us -> 14.8 us  [body(): tail = lax.psum(jnp.concatenate([level, cross, gain_part]), 'gx')]
    reduce_scatter x5 -> x1, waiting for transfers between devices: 145 us -> 0.01 us  [body(): lax.psum_scatter(lax.dot_general(act_rows, out_rows, (((0,), (0,)), ((),...]
    all_gather x4 -> x2, blocking collectives: 130 us -> 64.5 us  [the longest x1 39.9 us: body(): d_gain = jnp.sum(lax.all_gather(tail[2 * all_rows:], 'gy'), axis=0)]
    all_to_all x0 -> x5, starting transfers between devices: none -> 59.6 us  [exchange(): return lax.all_to_all(blocks, axis, 0, 0, tiled=True)]
    unnamed x0 -> x1, blocking collectives: none -> 52.5 us
    all_to_all x0 -> x1, blocking collectives: none -> 30.9 us  [exchange(): return lax.all_to_all(blocks, axis, 0, 0, tiled=True)]
    all_gather x1, waiting for transfers between devices: 17.8 us -> 5.23 us  [body(): down_full = lax.all_gather(w_down, 'gy', axis=0, tiled=True)]
    all_to_all x0 -> x5, waiting for transfers between devices: none -> 9.48 us  [exchange(): return lax.all_to_all(blocks, axis, 0, 0, tiled=True)]
  transfers between devices with their start and end apart: 7 -> 7, of which waited for: 3 -> 3; matrix products, arithmetic and copies ran while one was open for 2% -> 5% of each run, Pallas kernels for 0% -> 0%
where the time goes in v1:
time: 274 us; the launch traced here: 273 us
  blocking collectives  163 us (59%)
  starting transfers between devices  59.6 us (22%)
  waiting for transfers between devices  15.4 us (6%)
  between operations  14.9 us (5%)
  matrix products  8.36 us (3%)
  local copies, waits for them, and re-layouts  6.99 us (3%)
  other arithmetic  5.06 us (2%)
    all_to_all x5, starting transfers between devices, exchange(): return lax.all_to_all(blocks, axis, 0, 0, tiled=True)  59.6 us
    unnamed x1, blocking collectives  52.5 us
    all_gather x1, blocking collectives, body(): d_gain = jnp.sum(lax.all_gather(tail[2 * all_rows:], 'gy'), axis=0)  39.9 us
    all_to_all x1, blocking collectives, exchange(): return lax.all_to_all(blocks, axis, 0, 0, tiled=True)  30.9 us
    all_gather x1, blocking collectives, body(): lax.all_gather(jnp.concatenate([x_in, d_out], axis=1), 'gx', axis=0, tile...  24.6 us
    psum x1, blocking collectives, body(): tail = lax.psum(jnp.concatenate([level, cross, gain_part]), 'gx')  14.8 us
    all_to_all x5, waiting for transfers between devices, exchange(): return lax.all_to_all(blocks, axis, 0, 0, tiled=True)  9.48 us
  transfers between devices with their start and end apart: 7, of which 3 were waited for; matrix products, arithmetic and copies ran while one was open for 5% of the time, Pallas kernels for 0%

profile of v1, /device:TPU:1, one launch (start us, length us, event | category | flops | bytes accessed | tf_op | source)
XLA Modules:
  0.0 273.1 jit_solution(461217714187254258)
XLA Ops:
  7.2 2.0 broadcast_in_dim.6
  9.2 10.5 %all-to-all-start = ((bf16[8,80,896]{2,1,0:T(8,128)(2,1)}), bf16[8,80,896]{2,1,0:T(8,128)(2,1)S(1)}, u32[]{:S(2)}, u32[]{:S(2)}) async-start(bf16[8,80,896]{2,1,0:T(8,128)(2,1)} %broadcast_in_dim.6), calls=%async_computation | async-start | bytes 2293760 | tf_op jit(solution)/shard_map/all_to_all | solution.py:16
  19.7 0.0 all-gather.5.cloned.1.call-start
  19.7 0.7 all-gather.5.cloned.1.call-update
  20.4 24.6 %all_gather.18 = bf16[384,1280]{1,0:T(8,128)(2,1)S(1)} all-gather(bf16[48,1280]{1,0:T(8,128)(2,1)S(1)} %pad_maximum_fusion.2), channel_id=1, replica_groups=mesh['gx'=8,'gy'=8,'gz'=8] {'gx'}, dimensions={0}, use_global_device_ids=true | all-gather | bytes 1105920 | tf_op jit(solution)/shard_map/all_gather | solution.py:38
  45.0 7.8 %all-to-all-done = bf16[8,80,896]{2,1,0:T(8,128)(2,1)S(1)} async-done(((bf16[8,80,896]{2,1,0:T(8,128)(2,1)}), bf16[8,80,896]{2,1,0:T(8,128)(2,1)S(1)}, u32[]{:S(2)}, u32[]{:S(2)}) %all-to-all-start) | async-done | bytes 1146912 | tf_op jit(solution)/shard_map/all_to_all | solution.py:16
  52.8 0.1 convert_reduce_fusion.1
  53.0 0.3 fusion.1
  53.3 0.0 copy-start.4
  53.3 0.6 broadcast_in_dim.7
  53.9 3.3 %all-to-all-start.1 = ((f32[8,2,384]{2,1,0:T(2,128)}), f32[8,2,384]{2,1,0:T(2,128)S(1)}, u32[]{:S(2)}, u32[]{:S(2)}) async-start(f32[8,2,384]{2,1,0:T(2,128)} %broadcast_in_dim.7), calls=%async_computation.1 | async-start | bytes 49152 | tf_op jit(solution)/shard_map/all_to_all | solution.py:16
  57.3 5.2 %all-gather.5.cloned.1.call-done = bf16[896,640]{1,0:T(8,128)(2,1)} async-done(((bf16[112,640]{1,0:T(8,128)(2,1)}), bf16[896,640]{1,0:T(8,128)(2,1)}) %all-gather.5.cloned.1.call-update) | async-done | bytes 1146896 | tf_op jit(solution)/shard_map/all_gather | solution.py:36
  62.5 2.0 convolution_convert_fusion.2
  64.5 1.7 all-to-all-done.1
  66.3 0.8 convolution_convert_fusion.3
  67.1 0.1 pad_maximum_fusion
  67.2 30.9 %all_to_all.30 = bf16[8,48,1792]{2,1,0:T(8,128)(2,1)S(1)} all-to-all(bf16[8,48,1792]{2,1,0:T(8,128)(2,1)S(1)} %bitcast.15), channel_id=1, replica_groups=mesh['gx'=8,'gy'=8,'gz'=8] {'gz'}, dimensions={0} | all-to-all | bytes 2752512 | tf_op jit(solution)/shard_map/all_to_all | solution.py:16
  98.1 0.2 convert_reduce_fusion
  98.3 0.2 multiply_reduce_fusion.2
  98.5 1.2 broadcast_in_dim.8
  99.7 3.6 %all-to-all-start.3 = ((bf16[8,48,1792]{2,1,0:T(8,128)(2,1)}), bf16[8,48,1792]{2,1,0:T(8,128)(2,1)S(1)}, u32[]{:S(2)}, u32[]{:S(2)}) async-start(bf16[8,48,1792]{2,1,0:T(8,128)(2,1)} %broadcast_in_dim.8), calls=%async_computation.3 | async-start | bytes 2752512 | tf_op jit(solution)/shard_map/all_to_all | solution.py:16
  103.3 1.3 dynamic-slice
  105.2 0.3 multiply_reduce_fusion
  105.5 0.1 maximum_dynamic-update-slice_fusion
  105.6 52.5 %all-reduce = f32[7552]{0:T(1024)} all-reduce(f32[7552]{0:T(1024)S(1)} %maximum_dynamic-update-slice_fusion), channel_id=2, replica_groups=mesh['gx'=8,'gy'=8,'gz'=8] {'gz'}, use_global_device_ids=true, to_apply=%add | all-reduce | flops 7552 | bytes 60416
  158.2 0.8 reshape.64
  159.0 0.0 all-to-all-done.3
  159.0 1.6 fusion.6
  160.6 28.5 %all-to-all-start.4 = ((bf16[8,48,640]{2,1,0:T(8,128)(2,1)}), bf16[8,48,640]{2,1,0:T(8,128)(2,1)S(1)}, u32[]{:S(2)}, u32[]{:S(2)}) async-start(bf16[8,48,640]{2,1,0:T(8,128)(2,1)} %bitcast.24), calls=%async_computation.4 | async-start | bytes 983040 | tf_op jit(solution)/shard_map/all_to_all | solution.py:16
  189.1 0.0 reduce-scatter.2.cloned.1.call-start
  189.2 0.1 reshape.62
  189.2 1.9 convolution_convert_fusion
  191.1 0.0 reduce-scatter.2.cloned.1.call-update
  191.1 0.2 multiply_reduce_fusion.1
  191.4 14.8 %psum.7 = f32[1408]{0:T(1024)S(1)} all-reduce(f32[1408]{0:T(1024)S(1)} %pad_maximum_fusion.3), channel_id=1, replica_groups=mesh['gx'=8,'gy'=8,'gz'=8] {'gx'}, use_global_device_ids=true, to_apply=%region_12.0 | all-reduce | flops 1408 | bytes 11264 | tf_op jit(solution)/shard_map/psum | solution.py:77
  206.2 2.0 convolution_convert_fusion.1
  208.2 0.0 all-to-all-done.4
  208.2 0.8 copy-done
  209.0 13.7 %all-to-all-start.5 = ((bf16[8,80,896]{2,1,0:T(8,128)(2,1)}), bf16[8,80,896]{2,1,0:T(8,128)(2,1)S(1)}, u32[]{:S(2)}, u32[]{:S(2)}) async-start(bf16[8,80,896]{2,1,0:T(8,128)(2,1)} %bitcast.23), calls=%async_computation.5 | async-start | bytes 2293760 | tf_op jit(solution)/shard_map/all_to_all | solution.py:16
  222.7 0.1 dynamic_slice.14
  222.8 0.1 dynamic_slice.12
  222.9 39.9 %all-gather.2 = f32[8,1,640]{2,1,0:T(1,128)S(1)} all-gather(f32[1,1,640]{2,1,0:T(1,128)S(1)} %reshape.69), channel_id=3, replica_groups=mesh['gx'=8,'gy'=8,'gz'=8] {'gy'}, dimensions={0}, use_global_device_ids=true | all-gather | bytes 23040 | tf_op jit(solution)/shard_map/all_gather | solution.py:82
  262.8 0.6 reduce_sum.142
  263.5 0.1 dynamic-slice_multiply_fusion
  263.5 1.1 convert_reduce_fusion.2
  264.7 0.7 multiply_convert_fusion.1
  265.4 0.0 all-to-all-done.5
  265.4 0.8 reduce_sum.141
  (26 shorter events, 0.2 us)
Async XLA Ops:
  9.2 11.2 %copy-start.1 = (bf16[48,640]{1,0:T(8,128)(2,1)S(1)}, bf16[48,640]{1,0:T(8,128)(2,1)}, u32[]{:S(2)}) copy-start(bf16[48,640]{1,0:T(8,128)(2,1)} %param.5) | copy-start | bytes 184324
  9.2 11.2 %copy-start.3 = (bf16[48,640]{1,0:T(8,128)(2,1)S(1)}, bf16[48,640]{1,0:T(8,128)(2,1)}, u32[]{:S(2)}) copy-start(bf16[48,640]{1,0:T(8,128)(2,1)} %param.9) | copy-start | bytes 184324
  9.2 43.6 %all-to-all-start = ((bf16[8,80,896]{2,1,0:T(8,128)(2,1)}), bf16[8,80,896]{2,1,0:T(8,128)(2,1)S(1)}, u32[]{:S(2)}, u32[]{:S(2)}) async-start(bf16[8,80,896]{2,1,0:T(8,128)(2,1)} %broadcast_in_dim.6), calls=%async_computation | async-start | bytes 2293760 | tf_op jit(solution)/shard_map/all_to_all | solution.py:16
  19.7 42.8 %all-gather.5.cloned.1.call-start = ((), (), s32[]{:S(2)}) async-start(), calls=%async_computation.7 | async-start | bytes 1290240 | tf_op jit(solution)/shard_map/all_gather | solution.py:36
  53.3 13.0 %copy-start.4 = (f32[640]{0:T(1024)S(1)}, f32[640]{0:T(1024)}, u32[]{:S(2)}) copy-start(f32[640]{0:T(1024)} %param.6) | copy-start | bytes 7684
  53.9 12.3 %all-to-all-start.1 = ((f32[8,2,384]{2,1,0:T(2,128)}), f32[8,2,384]{2,1,0:T(2,128)S(1)}, u32[]{:S(2)}, u32[]{:S(2)}) async-start(f32[8,2,384]{2,1,0:T(2,128)} %broadcast_in_dim.7), calls=%async_computation.1 | async-start | bytes 49152 | tf_op jit(solution)/shard_map/all_to_all | solution.py:16
  99.7 59.3 %all-to-all-start.3 = ((bf16[8,48,1792]{2,1,0:T(8,128)(2,1)}), bf16[8,48,1792]{2,1,0:T(8,128)(2,1)S(1)}, u32[]{:S(2)}, u32[]{:S(2)}) async-start(bf16[8,48,1792]{2,1,0:T(8,128)(2,1)} %broadcast_in_dim.8), calls=%async_computation.3 | async-start | bytes 2752512 | tf_op jit(solution)/shard_map/all_to_all | solution.py:16
  160.6 47.6 %all-to-all-start.4 = ((bf16[8,48,640]{2,1,0:T(8,128)(2,1)}), bf16[8,48,640]{2,1,0:T(8,128)(2,1)S(1)}, u32[]{:S(2)}, u32[]{:S(2)}) async-start(bf16[8,48,640]{2,1,0:T(8,128)(2,1)} %bitcast.24), calls=%async_computation.4 | async-start | bytes 983040 | tf_op jit(solution)/shard_map/all_to_all | solution.py:16
  189.1 77.1 %reduce-scatter.2.cloned.1.call-start = ((), (), s32[]{:S(2)}) async-start(), calls=%async_computation.8 | async-start | bytes 1290240 | tf_op jit(solution)/shard_map/reduce_scatter | solution.py:85
  208.2 0.8 copy-start
  208.2 56.4 %copy-start.2 = (bf16[48,640]{1,0:T(8,128)(2,1)S(1)}, bf16[48,640]{1,0:T(8,128)(2,1)}, u32[]{:S(2)}) copy-start(bf16[48,640]{1,0:T(8,128)(2,1)} %param.5) | copy-start | bytes 184324
  209.0 56.4 %all-to-all-start.5 = ((bf16[8,80,896]{2,1,0:T(8,128)(2,1)}), bf16[8,80,896]{2,1,0:T(8,128)(2,1)S(1)}, u32[]{:S(2)}, u32[]{:S(2)}) async-start(bf16[8,80,896]{2,1,0:T(8,128)(2,1)} %bitcast.23), calls=%async_computation.5 | async-start | bytes 2293760 | tf_op jit(solution)/shard_map/all_to_all | solution.py:16
Sparse Core Ops, SparseCore 0:
  22.6 39.8 all-gather.4
  193.3 48.6 reduce-scatter.1

commit v2 on v1

v2 whole, which is shorter than its diff:
```python
import jax
import jax.numpy as jnp
from jax import lax
from jax.sharding import Mesh
from jax.sharding import PartitionSpec as P

BF, F32 = jnp.bfloat16, jnp.float32
LANES = 128
GY, GZ = ("yl", "co"), ("yh", "xx")


def gelu_pair(hidden):
    cdf = 0.5 * (1.0 + jax.scipy.special.erf(hidden * 0.7071067811865476))
    slope = cdf + hidden * jnp.exp(-0.5 * hidden * hidden) * 0.3989422804014327
    return (hidden * cdf, slope)


def exchange(blocks, axis):
    return lax.all_to_all(blocks, axis, 0, 0, tiled=True)


def spread(value, axis):
    n = lax.axis_size(axis)
    return exchange(jnp.broadcast_to(value[None], (n, *value.shape)), axis)


def summed(blocks):
    return jnp.sum(blocks.astype(F32), axis=0)


def pieces(value):
    high = lax.reduce_precision(value, 8, 7)
    rest = value - high
    middle = lax.reduce_precision(rest, 8, 7)
    return [p.astype(BF) for p in (high, middle, rest - middle)]


def columns(values, rows):
    cols = jnp.stack([p for v in values for p in pieces(v)], axis=1)
    return jnp.pad(cols, ((0, 0), (0, LANES - cols.shape[1])))


def other_core(value):
    return lax.ppermute(value, "co", [(0, 1), (1, 0)])


def body(x_in, gain, w_up, w_down, d_out):
    rows, local = x_in.shape
    n_gx, n_yl, n_gz = (lax.axis_size(a) for a in ("gx", "yl", GZ))
    width = local * n_gz
    hid = w_up.shape[1]
    all_rows = rows * n_gx
    block = all_rows // n_gz
    core = lax.axis_index("co")

    down_full = lax.all_gather(w_down, GY, axis=0, tiled=True)
    up_mine = spread(w_up, "yl")
    both = lax.all_gather(jnp.concatenate([x_in, d_out], axis=1), "gx", axis=0, tiled=True)
    both, up_mine = lax.optimization_barrier((both, up_mine))
    up_other = other_core(up_mine)
    even = core == 0
    up_full = jnp.stack(
        [jnp.where(even, up_mine, up_other), jnp.where(even, up_other, up_mine)], axis=1
    ).reshape(local, hid)
    x_rows, out_rows = both[:, :local].astype(F32), both[:, local:]

    part_sum = jnp.sum(x_rows, axis=1)
    off = x_rows - (part_sum / local)[:, None]
    own_gain = gain.reshape(n_yl, 2, -1, 1)
    own_gain = jnp.where(even, own_gain[:, 0], own_gain[:, 1])
    tilt = jnp.sum(up_mine.astype(F32) * own_gain, axis=(0, 1))
    stats = spread(jnp.concatenate([part_sum, jnp.sum(off * off, axis=1), tilt])[None], GZ)[:, 0]
    sums, seconds = stats[:, :all_rows], stats[:, all_rows : 2 * all_rows]
    tilt = jnp.sum(stats[:, 2 * all_rows :], axis=0)
    tilt = tilt + other_core(tilt)
    mean = jnp.sum(sums, axis=0) / width
    shift = sums / local - mean
    var = (jnp.sum(seconds, axis=0) + local * jnp.sum(shift * shift, axis=0)) / width
    inv = lax.rsqrt(var + 1e-05)
    normed = (x_rows - mean[:, None]) * inv[:, None]
    z = (normed * gain).astype(BF)

    hid_part = jnp.dot(z, up_full, preferred_element_type=F32).astype(BF)
    dact_part = lax.dot_general(
        out_rows, down_full, (((1,), (1,)), ((), ())), preferred_element_type=F32
    ).astype(BF)
    pair = jnp.concatenate([hid_part, dact_part], axis=1).reshape(n_gz, block, 2 * hid)
    pair = summed(exchange(pair, GZ))
    hidden, d_act = pair[:, :hid], pair[:, hid:]
    act_f, slope = gelu_pair(hidden)
    d_hidden = (d_act * slope).astype(BF)
    cross = jnp.sum(d_hidden.astype(F32) * hidden, axis=1)
    acts = jnp.concatenate([act_f.astype(BF), d_hidden, columns([cross], block)], axis=1)
    acts = spread(acts, GZ).reshape(all_rows, -1)
    act_rows, hgrad_rows = acts[:, :hid], acts[:, hid : 2 * hid]
    cross = jnp.sum(acts[:, 2 * hid : 2 * hid + 3].astype(F32), axis=1)

    down_part = lax.dot_general(
        act_rows, out_rows, (((0,), (0,)), ((), ())), preferred_element_type=F32
    ).astype(BF)
    down_part, hgrad_rows = lax.optimization_barrier((down_part, hgrad_rows))
    d_w_down = lax.psum_scatter(down_part, GY, scatter_dimension=0, tiled=True)

    dz_part = lax.dot_general(
        hgrad_rows, up_full, (((1,), (1,)), ((), ())), preferred_element_type=F32
    )
    level = jnp.sum(hgrad_rows.astype(F32) * tilt, axis=1)
    gain_part = jnp.concatenate(
        [p.reshape(-1, LANES) for p in pieces(jnp.sum(dz_part * normed, axis=0))]
    )
    gain_rows = gain_part.shape[0]
    gain_part = jnp.pad(gain_part, ((0, rows - gain_rows), (0, 0)))
    tail = jnp.concatenate(
        [
            dz_part.astype(BF).reshape(n_gx, rows, local),
            columns([level, cross], all_rows).reshape(n_gx, rows, LANES),
            jnp.broadcast_to(gain_part, (n_gx, rows, LANES)),
        ],
        axis=2,
    )
    tail = summed(exchange(tail, "gx"))
    d_z = tail[:, :local]
    scaled_sum = jnp.sum(tail[:, local : local + 3], axis=1, keepdims=True)
    cross_sum = jnp.sum(tail[:, local + 3 : local + 6], axis=1, keepdims=True)
    gain_part = jnp.sum(tail[:gain_rows, local + LANES :].reshape(3, local), axis=0)

    d_w_up = lax.dot_general(
        z, hgrad_rows, (((0,), (0,)), ((), ())), preferred_element_type=F32
    ).astype(BF)
    d_w_up = d_w_up.reshape(n_yl, 2, -1, hid)
    keep = jnp.where(even, d_w_up[:, 0], d_w_up[:, 1])
    give = jnp.where(even, d_w_up[:, 1], d_w_up[:, 0])
    d_w_up = (keep.astype(F32) + other_core(give).astype(F32)).astype(BF)
    gain_part = jnp.pad(jnp.stack(pieces(gain_part)), ((0, 5), (0, hid - local)))
    d_w_up = jnp.concatenate(
        [d_w_up, jnp.broadcast_to(gain_part, (n_yl, *gain_part.shape))], axis=1
    )
    d_w_up = summed(exchange(d_w_up, "yl"))
    height = w_up.shape[0]
    d_gain = jnp.sum(d_w_up[height : height + 3, :local], axis=0)
    d_w_up = d_w_up[:height].astype(BF)
    d_gain = d_gain + other_core(d_gain)

    first = lax.axis_index("gx") * rows

    def own(values):
        return lax.dynamic_slice(values, (first,), (rows,))[:, None]

    d_z, d_w_down = lax.optimization_barrier((d_z, d_w_down))
    own_inv = own(inv)
    own_normed = (x_in.astype(F32) - own(mean)) * own_inv
    d_x = own_inv * (d_z * gain - scaled_sum / width - own_normed * (cross_sum / width))
    return (d_x.astype(BF), d_w_up, d_w_down, d_gain)


def solution(mesh):
    sizes = mesh.shape
    cores, x_chips = 2, sizes["gz"] // 2
    fine = Mesh(
        mesh.devices.reshape(sizes["gx"], sizes["gy"] // cores, cores, 2, x_chips),
        ("gx", *GY, *GZ),
    )
    placed = (
        P((*GY, "gx"), GZ),
        P(GZ),
        P((*GZ, *GY), "gx"),
        P(("gx", *GY), GZ),
        P((*GY, "gx"), GZ),
    )
    return jax.shard_map(
        body,
        mesh=fine,
        in_specs=placed,
        out_specs=(P((*GY, "gx"), GZ), P((*GZ, *GY), "gx"), P(("gx", *GY), GZ), P(GZ)),
        check_vma=False,
    )
```

time: 274 us -> 225 us (0.82)
  blocking collectives: 163 us -> 60.4 us
  starting transfers between devices: 59.6 us -> 101 us
  waiting for transfers between devices: 15.4 us -> 27.3 us
    unnamed x1 -> x0, blocking collectives: 52.5 us -> none
    ppermute x0 -> x4, starting transfers between devices: none -> 43.5 us  [other_core(): return lax.ppermute(value, 'co', [(0, 1), (1, 0)])]
    all_gather x1 -> x0, blocking collectives: 39.9 us -> none  [body(): d_gain = jnp.sum(lax.all_gather(tail[2 * all_rows:], 'gy'), axis=0)]
    psum x1 -> x0, blocking collectives: 14.8 us -> none  [body(): tail = lax.psum(jnp.concatenate([level, cross, gain_part]), 'gx')]
    all_to_all x5, waiting for transfers between devices: 9.48 us -> 24.1 us  [exchange(): return lax.all_to_all(blocks, axis, 0, 0, tiled=True)]
    all_gather x1, waiting for transfers between devices: 5.23 us -> 0.02 us  [body(): down_full = lax.all_gather(w_down, GY, axis=0, tiled=True)]
    all_gather x1, blocking collectives: 24.6 us -> 29.2 us  [body(): lax.all_gather(jnp.concatenate([x_in, d_out], axis=1), 'gx', axis=0, tile...]
  transfers between devices with their start and end apart: 7 -> 11, of which waited for: 3 -> 5; matrix products, arithmetic and copies ran while one was open for 5% -> 4% of each run, Pallas kernels for 0% -> 0%
where the time goes in v2:
time: 225 us; the launch traced here: 224 us
  starting transfers between devices  101 us (45%)
  blocking collectives  60.4 us (27%)
  waiting for transfers between devices  27.3 us (12%)
  between operations  14.4 us (6%)
  local copies, waits for them, and re-layouts  8.12 us (4%)
  matrix products  7.78 us (3%)
  other arithmetic  5.59 us (2%)
    all_to_all x5, starting transfers between devices, exchange(): return lax.all_to_all(blocks, axis, 0, 0, tiled=True)  57.3 us
    ppermute x4, starting transfers between devices, other_core(): return lax.ppermute(value, 'co', [(0, 1), (1, 0)])  43.5 us
    all_to_all x1, blocking collectives, exchange(): return lax.all_to_all(blocks, axis, 0, 0, tiled=True)  31.2 us
    all_gather x1, blocking collectives, body(): lax.all_gather(jnp.concatenate([x_in, d_out], axis=1), 'gx', axis=0, tile...  29.2 us
    all_to_all x5, waiting for transfers between devices, exchange(): return lax.all_to_all(blocks, axis, 0, 0, tiled=True)  24.1 us
  transfers between devices with their start and end apart: 11, of which 5 were waited for; matrix products, arithmetic and copies ran while one was open for 4% of the time, Pallas kernels for 0%

profile of v2, /device:TPU:1, one launch (start us, length us, event | category | flops | bytes accessed | tf_op | source)
XLA Modules:
  0.0 224.4 jit_solution(15777190554719748793)
XLA Ops:
  7.2 0.7 all-gather.2.cloned.1.call-update
  7.9 1.8 broadcast_in_dim.10
  9.7 5.4 %all-to-all-start = ((bf16[4,80,896]{2,1,0:T(8,128)(2,1)}), bf16[4,80,896]{2,1,0:T(8,128)(2,1)S(1)}, u32[]{:S(2)}, u32[]{:S(2)}) async-start(bf16[4,80,896]{2,1,0:T(8,128)(2,1)} %broadcast_in_dim.10), calls=%async_computation | async-start | bytes 1146880 | tf_op jit(solution)/shard_map/all_to_all | solution.py:19
  15.3 29.2 %all_gather.6 = bf16[384,1280]{1,0:T(8,128)(2,1)S(1)} all-gather(bf16[48,1280]{1,0:T(8,128)(2,1)S(1)} %pad_maximum_fusion.4), channel_id=1, replica_groups=mesh['gx'=8,'yl'=4,'co'=2,'yh'=2,'xx'=4] {'gx'}, dimensions={0}, use_global_device_ids=true | all-gather | bytes 1105920 | tf_op jit(solution)/shard_map/all_gather | solution.py:58
  44.4 0.2 multiply_reduce_fusion.1
  44.6 0.1 convert_reduce_fusion.1
  44.8 0.3 fusion.2
  45.1 0.7 broadcast_in_dim.11
  45.7 7.9 %all-to-all-start.1 = ((f32[8,1,1664]{2,1,0:T(1,128)}), f32[8,1,1664]{2,1,0:T(1,128)S(1)}, u32[]{:S(2)}, u32[]{:S(2)}) async-start(f32[8,1,1664]{2,1,0:T(1,128)} %broadcast_in_dim.11), calls=%async_computation.1 | async-start | bytes 106496 | tf_op jit(solution)/shard_map/all_to_all | solution.py:19
  53.6 6.9 %collective-permute-start = (bf16[4,80,896]{2,1,0:T(8,128)(2,1)S(1)}, bf16[4,80,896]{2,1,0:T(8,128)(2,1)S(1)}, u32[]{:S(2)}, u32[]{:S(2)}) collective-permute-start(bf16[4,80,896]{2,1,0:T(8,128)(2,1)S(1)} %all-to-all-done), channel_id=1, source_target_pairs={{0,8},{8,0},{1,9},{9,1},{2,10},{10,2},{3,11},{11,3},{4,12},{12,4},... | collective-permute-start | bytes 1720328 | tf_op jit(solution)/shard_map/ppermute | solution.py:44
  60.6 2.1 all-to-all-done.1
  62.8 0.1 select_bitcast_fusion.1
  62.9 0.1 pad_maximum_fusion.1
  63.0 1.0 copy-done
  64.0 0.8 convolution_convert_fusion.3
  64.9 2.0 convolution_convert_fusion.2
  67.0 0.1 pad_maximum_fusion
  67.1 31.2 %all_to_all.30 = bf16[8,48,1792]{2,1,0:T(8,128)(2,1)S(1)} all-to-all(bf16[8,48,1792]{2,1,0:T(8,128)(2,1)S(1)} %bitcast.56), channel_id=1, replica_groups=mesh['gx'=8,'yl'=4,'co'=2,'yh'=2,'xx'=4] {'yh','xx'}, dimensions={0} | all-to-all | bytes 2752512 | tf_op jit(solution)/shard_map/all_to_all | solution.py:19
  98.3 0.2 convert_reduce_fusion
  98.5 0.2 multiply_reduce_fusion.2
  98.7 0.1 copy.64
  98.8 1.2 broadcast_in_dim.12
  100.0 4.3 %all-to-all-start.3 = ((bf16[8,48,1920]{2,1,0:T(8,128)(2,1)}), bf16[8,48,1920]{2,1,0:T(8,128)(2,1)}, u32[]{:S(2)}, u32[]{:S(2)}) async-start(bf16[8,48,1920]{2,1,0:T(8,128)(2,1)} %broadcast_in_dim.12), calls=%async_computation.3 | async-start | bytes 2949120 | tf_op jit(solution)/shard_map/all_to_all | solution.py:19
  104.4 16.1 %collective-permute-start.1 = (f32[896]{0:T(1024)S(1)}, f32[896]{0:T(1024)S(1)}, u32[]{:S(2)}, u32[]{:S(2)}) collective-permute-start(f32[896]{0:T(1024)S(1)} %slice_reduce_fusion), channel_id=1, source_target_pairs={{0,8},{8,0},{1,9},{9,1},{2,10},{10,2},{3,11},{11,3},{4,12},{12,4},... | collective-permute-start | bytes 10760 | tf_op jit(solution)/shard_map/ppermute | solution.py:44
  120.4 0.8 collective-permute-done.1
  121.2 0.9 slice.92
  122.1 1.2 slice.90
  123.3 3.1 %convolution_convert_fusion.1 = bf16[896,640]{1,0:T(8,128)(2,1)} fusion(bf16[384,1920]{1,0:T(8,128)(2,1)} %bitcast.7, bf16[384,1280]{1,0:T(8,128)(2,1)S(1)} %all_gather.6), kind=kOutput, calls=%fused_computation.2 | convolution fusion | flops 440975360 | bytes 2326528 | tf_op jit(solution)/shard_map/dot_general | solution.py:98
  126.5 0.9 fusion.43
  127.4 0.2 multiply_reduce_fusion
  127.7 0.2 copy.65
  127.9 0.9 pad_maximum_fusion.2
  128.8 3.7 %all-to-all-start.4 = ((bf16[8,48,896]{2,1,0:T(8,128)(2,1)}), bf16[8,48,896]{2,1,0:T(8,128)(2,1)S(1)}, u32[]{:S(2)}, u32[]{:S(2)}) async-start(bf16[8,48,896]{2,1,0:T(8,128)(2,1)} %pad_maximum_fusion.2), calls=%async_computation.4 | async-start | bytes 1376256 | tf_op jit(solution)/shard_map/all_to_all | solution.py:19
  132.6 1.0 convolution_convert_fusion
  133.6 17.6 %collective-permute-start.2 = (bf16[4,80,896]{2,1,0:T(8,128)(2,1)S(1)}, bf16[4,80,896]{2,1,0:T(8,128)(2,1)S(1)}, u32[]{:S(2)}, u32[]{:S(2)}) collective-permute-start(bf16[4,80,896]{2,1,0:T(8,128)(2,1)S(1)} %fusion.9), channel_id=1, source_target_pairs={{0,8},{8,0},{1,9},{9,1},{2,10},{10,2},{3,11},{11,3},{4,12},{12,4},... | collective-permute-start | bytes 1720328 | tf_op jit(solution)/shard_map/ppermute | solution.py:44
  151.3 1.6 collective-permute-done.2
  152.9 0.2 fusion
  153.1 0.1 convert_reduce_fusion.2
  153.3 0.9 pad_maximum_fusion.3
  154.2 36.0 %all-to-all-start.5 = ((bf16[4,88,896]{2,1,0:T(8,128)(2,1)}), bf16[4,88,896]{2,1,0:T(8,128)(2,1)S(1)}, u32[]{:S(2)}, u32[]{:S(2)}) async-start(bf16[4,88,896]{2,1,0:T(8,128)(2,1)} %pad_maximum_fusion.3), calls=%async_computation.6 | async-start | bytes 1261568 | tf_op jit(solution)/shard_map/all_to_all | solution.py:19
  190.3 0.2 slice_reduce_fusion.2
  190.4 21.9 %all-to-all-done.5 = bf16[4,88,896]{2,1,0:T(8,128)(2,1)S(1)} async-done(((bf16[4,88,896]{2,1,0:T(8,128)(2,1)}), bf16[4,88,896]{2,1,0:T(8,128)(2,1)S(1)}, u32[]{:S(2)}, u32[]{:S(2)}) %all-to-all-start.5) | async-done | bytes 630816 | tf_op jit(solution)/shard_map/all_to_all | solution.py:19
  212.4 0.1 convert_reduce_fusion.3
  212.5 2.9 %collective-permute-start.3 = (f32[640]{0:T(1024)S(1)}, f32[640]{0:T(1024)S(1)}, u32[]{:S(2)}, u32[]{:S(2)}) collective-permute-start(f32[640]{0:T(1024)S(1)} %slice_reduce_fusion.5), channel_id=1, source_target_pairs={{0,8},{8,0},{1,9},{9,1},{2,10},{10,2},{3,11},{11,3},{4,12},{12,4},... | collective-permute-start | bytes 7688 | tf_op jit(solution)/shard_map/ppermute | solution.py:44
  215.4 0.7 slice.136
  216.1 0.1 collective-permute-done.3
  216.2 0.6 add.58
  216.8 0.7 multiply_convert_fusion.1
  (56 shorter events, 0.9 us)
Async XLA Ops:
  7.2 8.0 %copy-start.5 = (f32[640]{0:T(1024)S(1)}, f32[640]{0:T(1024)}, u32[]{:S(2)}) copy-start(f32[640]{0:T(1024)} %param.6) | copy-start | bytes 7684
  7.2 8.0 %copy-start.2 = (bf16[48,640]{1,0:T(8,128)(2,1)S(1)}, bf16[48,640]{1,0:T(8,128)(2,1)}, u32[]{:S(2)}) copy-start(bf16[48,640]{1,0:T(8,128)(2,1)} %param.5) | copy-start | bytes 184324
  7.2 8.0 %copy-start.4 = (bf16[48,640]{1,0:T(8,128)(2,1)S(1)}, bf16[48,640]{1,0:T(8,128)(2,1)}, u32[]{:S(2)}) copy-start(bf16[48,640]{1,0:T(8,128)(2,1)} %param.9) | copy-start | bytes 184324
  7.2 57.7 %all-gather.2.cloned.1.call-start = ((), (), s32[]{:S(2)}) async-start(), calls=%async_computation.7 | async-start | bytes 1290240 | tf_op jit(solution)/shard_map/all_gather | solution.py:56
  9.7 34.7 %all-to-all-start = ((bf16[4,80,896]{2,1,0:T(8,128)(2,1)}), bf16[4,80,896]{2,1,0:T(8,128)(2,1)S(1)}, u32[]{:S(2)}, u32[]{:S(2)}) async-start(bf16[4,80,896]{2,1,0:T(8,128)(2,1)} %broadcast_in_dim.10), calls=%async_computation | async-start | bytes 1146880 | tf_op jit(solution)/shard_map/all_to_all | solution.py:19
  45.7 17.0 %all-to-all-start.1 = ((f32[8,1,1664]{2,1,0:T(1,128)}), f32[8,1,1664]{2,1,0:T(1,128)S(1)}, u32[]{:S(2)}, u32[]{:S(2)}) async-start(f32[8,1,1664]{2,1,0:T(1,128)} %broadcast_in_dim.11), calls=%async_computation.1 | async-start | bytes 106496 | tf_op jit(solution)/shard_map/all_to_all | solution.py:19
  53.6 9.1 %collective-permute-start = (bf16[4,80,896]{2,1,0:T(8,128)(2,1)S(1)}, bf16[4,80,896]{2,1,0:T(8,128)(2,1)S(1)}, u32[]{:S(2)}, u32[]{:S(2)}) collective-permute-start(bf16[4,80,896]{2,1,0:T(8,128)(2,1)S(1)} %all-to-all-done), channel_id=1, source_target_pairs={{0,8},{8,0},{1,9},{9,1},{2,10},{10,2},{3,11},{11,3},{4,12},{12,4},... | collective-permute-start | bytes 1720328 | tf_op jit(solution)/shard_map/ppermute | solution.py:44
  63.0 1.0 copy-start
  100.0 21.2 %all-to-all-start.3 = ((bf16[8,48,1920]{2,1,0:T(8,128)(2,1)}), bf16[8,48,1920]{2,1,0:T(8,128)(2,1)}, u32[]{:S(2)}, u32[]{:S(2)}) async-start(bf16[8,48,1920]{2,1,0:T(8,128)(2,1)} %broadcast_in_dim.12), calls=%async_computation.3 | async-start | bytes 2949120 | tf_op jit(solution)/shard_map/all_to_all | solution.py:19
  104.4 16.9 %collective-permute-start.1 = (f32[896]{0:T(1024)S(1)}, f32[896]{0:T(1024)S(1)}, u32[]{:S(2)}, u32[]{:S(2)}) collective-permute-start(f32[896]{0:T(1024)S(1)} %slice_reduce_fusion), channel_id=1, source_target_pairs={{0,8},{8,0},{1,9},{9,1},{2,10},{10,2},{3,11},{11,3},{4,12},{12,4},... | collective-permute-start | bytes 10760 | tf_op jit(solution)/shard_map/ppermute | solution.py:44
  123.3 3.2 %copy-start.1 = (bf16[4,2,80,896]{3,2,1,0:T(8,128)(2,1)S(1)}, bf16[4,2,80,896]{3,2,1,0:T(8,128)(2,1)}, u32[]{:S(2)}) copy-start(bf16[4,2,80,896]{3,2,1,0:T(8,128)(2,1)} %copy-done) | copy-start | bytes 3440644
  128.8 24.2 %all-to-all-start.4 = ((bf16[8,48,896]{2,1,0:T(8,128)(2,1)}), bf16[8,48,896]{2,1,0:T(8,128)(2,1)S(1)}, u32[]{:S(2)}, u32[]{:S(2)}) async-start(bf16[8,48,896]{2,1,0:T(8,128)(2,1)} %pad_maximum_fusion.2), calls=%async_computation.4 | async-start | bytes 1376256 | tf_op jit(solution)/shard_map/all_to_all | solution.py:19
  132.5 84.3 %reduce-scatter.2.cloned.1.call-start = ((), (), s32[]{:S(2)}) async-start(), calls=%async_computation.8 | async-start | bytes 1290240 | tf_op jit(solution)/shard_map/reduce_scatter | solution.py:102
  133.6 19.2 %collective-permute-start.2 = (bf16[4,80,896]{2,1,0:T(8,128)(2,1)S(1)}, bf16[4,80,896]{2,1,0:T(8,128)(2,1)S(1)}, u32[]{:S(2)}, u32[]{:S(2)}) collective-permute-start(bf16[4,80,896]{2,1,0:T(8,128)(2,1)S(1)} %fusion.9), channel_id=1, source_target_pairs={{0,8},{8,0},{1,9},{9,1},{2,10},{10,2},{3,11},{11,3},{4,12},{12,4},... | collective-permute-start | bytes 1720328 | tf_op jit(solution)/shard_map/ppermute | solution.py:44
  154.1 62.7 %copy-start.3 = (bf16[48,640]{1,0:T(8,128)(2,1)S(1)}, bf16[48,640]{1,0:T(8,128)(2,1)}, u32[]{:S(2)}) copy-start(bf16[48,640]{1,0:T(8,128)(2,1)} %param.5) | copy-start | bytes 184324
  154.2 58.2 %all-to-all-start.5 = ((bf16[4,88,896]{2,1,0:T(8,128)(2,1)}), bf16[4,88,896]{2,1,0:T(8,128)(2,1)S(1)}, u32[]{:S(2)}, u32[]{:S(2)}) async-start(bf16[4,88,896]{2,1,0:T(8,128)(2,1)} %pad_maximum_fusion.3), calls=%async_computation.6 | async-start | bytes 1261568 | tf_op jit(solution)/shard_map/all_to_all | solution.py:19
  212.5 3.7 %collective-permute-start.3 = (f32[640]{0:T(1024)S(1)}, f32[640]{0:T(1024)S(1)}, u32[]{:S(2)}, u32[]{:S(2)}) collective-permute-start(f32[640]{0:T(1024)S(1)} %slice_reduce_fusion.5), channel_id=1, source_target_pairs={{0,8},{8,0},{1,9},{9,1},{2,10},{10,2},{3,11},{11,3},{4,12},{12,4},... | collective-permute-start | bytes 7688 | tf_op jit(solution)/shard_map/ppermute | solution.py:44
Sparse Core Ops, SparseCore 0:
  10.1 43.4 all-gather.1
  151.4 56.2 reduce-scatter.1

commit v3 on v2

v3 whole, which is shorter than its diff:
```python
import jax
import jax.numpy as jnp
from jax import lax
from jax.sharding import Mesh
from jax.sharding import PartitionSpec as P

BF, F32 = jnp.bfloat16, jnp.float32
LANES = 128
GY, GZ = ("yl", "co"), ("yh", "xx")


def gelu_pair(hidden):
    cdf = 0.5 * (1.0 + jax.scipy.special.erf(hidden * 0.7071067811865476))
    slope = cdf + hidden * jnp.exp(-0.5 * hidden * hidden) * 0.3989422804014327
    return (hidden * cdf, slope)


def exchange(blocks, axis):
    return lax.all_to_all(blocks, axis, 0, 0, tiled=True)


def spread(value, axis):
    n = lax.axis_size(axis)
    return exchange(jnp.broadcast_to(value[None], (n, *value.shape)), axis)


def summed(blocks):
    return jnp.sum(blocks.astype(F32), axis=0)


def pieces(value):
    high = lax.reduce_precision(value, 8, 7)
    rest = value - high
    middle = lax.reduce_precision(rest, 8, 7)
    return [p.astype(BF) for p in (high, middle, rest - middle)]


def columns(*values):
    return jnp.stack([p for v in values for p in pieces(v)], axis=-1)


def column(lanes, index):
    return jnp.sum(lanes[..., 3 * index : 3 * index + 3].astype(F32), axis=-1)


def other_core(value):
    return lax.ppermute(value, "co", [(0, 1), (1, 0)])


def dot(a, b, contract):
    return lax.dot_general(a, b, ((contract[:1], contract[1:]), ((), ())), preferred_element_type=F32)


def body(x_in, gain, w_up, w_down, d_out):
    rows, local = x_in.shape
    n_gx, n_yl, n_gz = (lax.axis_size(a) for a in ("gx", "yl", GZ))
    width = local * n_gz
    up_rows, hid = w_up.shape
    down_rows = w_down.shape[0]
    all_rows = rows * n_gx
    block = all_rows // n_gz
    even = lax.axis_index("co") == 0

    def by_core(mine, other):
        pair = [jnp.where(even, mine, other), jnp.where(even, other, mine)]
        return jnp.stack(pair, axis=1).reshape(-1, mine.shape[-1])

    down_full = lax.all_gather(w_down, GY, axis=0, tiled=True)
    up_mine = spread(w_up, "yl")
    both = lax.all_gather(jnp.concatenate([x_in, d_out], axis=1), "gx", axis=0, tiled=True)
    both, up_mine = lax.optimization_barrier((both, up_mine))
    up_full = by_core(up_mine, other_core(up_mine))
    x_rows, out_rows = both[:, :local].astype(F32), both[:, local:]

    part_sum = jnp.sum(x_rows, axis=1)
    off = x_rows - (part_sum / local)[:, None]
    second = jnp.sum(off * off, axis=1)
    y = (off * gain).astype(BF)
    gains = jnp.pad(jnp.stack(pieces(gain)), ((0, 5), (0, 0)))
    tilt = jnp.sum(dot(gains, up_full, (1, 0)), axis=0)
    tilt = jnp.stack(pieces(tilt)).reshape(3 * n_gz, -1)
    spare = LANES - tilt.shape[1]
    tilt = jnp.pad(tilt, ((0, block - tilt.shape[0]), (0, 0)))
    marks = columns(part_sum, second)
    extra = jnp.concatenate(
        [
            jnp.pad(marks, ((0, 0), (0, spare - marks.shape[1]))).reshape(n_gz, block, spare),
            jnp.broadcast_to(tilt, (n_gz, *tilt.shape)),
        ],
        axis=2,
    )
    pair = jnp.concatenate(
        [
            dot(y, up_full, (1, 0)).astype(BF).reshape(n_gz, block, hid),
            dot(out_rows, down_full, (1, 1)).astype(BF).reshape(n_gz, block, hid),
            extra,
        ],
        axis=2,
    )
    pair = exchange(pair, GZ)
    marks = pair[:, :, 2 * hid : 2 * hid + spare]
    tilts = pair[:, : 3 * n_gz, 2 * hid + spare :].astype(F32)
    tilts = jnp.sum(tilts.reshape(n_gz, 3, n_gz, -1), axis=1).reshape(n_gz, hid)
    means = column(marks, 0) / local
    mean = jnp.sum(means, axis=0) / n_gz
    shift = means - mean
    var = (jnp.sum(column(marks, 1), axis=0) + local * jnp.sum(shift * shift, axis=0)) / width
    inv = lax.rsqrt(var + 1e-05)
    hidden = summed(pair[:, :, :hid]) + sum(
        shift[i][:, None] * tilts[i][None] for i in range(n_gz)
    )
    hidden = hidden * inv[:, None]
    d_act = summed(pair[:, :, hid : 2 * hid])
    act_f, slope = gelu_pair(hidden)
    d_hidden = (d_act * slope).astype(BF)
    cross = jnp.sum(d_hidden.astype(F32) * hidden, axis=1)
    marks = columns(cross, mean, inv)
    marks = jnp.pad(marks, ((0, 0), (0, LANES - marks.shape[1])))
    acts = jnp.concatenate([act_f.astype(BF), d_hidden, marks], axis=1)
    acts = spread(acts, GZ).reshape(all_rows, -1)
    act_rows, hgrad_rows, marks = acts[:, :hid], acts[:, hid : 2 * hid], acts[:, 2 * hid :]
    cross, mean, inv = (column(marks, i) for i in range(3))
    normed = (x_rows - mean[:, None]) * inv[:, None]
    z = (normed * gain).astype(BF)

    dz_part = dot(hgrad_rows, up_full, (1, 1))
    d_z = lax.psum_scatter(dz_part.astype(BF), "gx", scatter_dimension=0, tiled=True)
    level = jnp.sum(hgrad_rows.astype(F32) * jnp.sum(tilts, axis=0), axis=1)
    gain_part = jnp.sum(dz_part * normed, axis=0)
    tail = jnp.concatenate(
        [
            jnp.broadcast_to(gain_part, (n_gx, local)),
            level.reshape(n_gx, rows),
            cross.reshape(n_gx, rows),
        ],
        axis=1,
    )
    tail = jnp.sum(exchange(tail[:, None], "gx")[:, 0], axis=0)
    scaled_sum = tail[local : local + rows, None] / width
    cross_sum = tail[local + rows :, None] / width

    grads = jnp.concatenate(
        [
            dot(act_rows, out_rows, (0, 0)).astype(BF).reshape(n_yl, 2, down_rows, local),
            jnp.pad(
                dot(z, hgrad_rows, (0, 0)).astype(BF).reshape(n_yl, 2, up_rows, hid),
                ((0, 0), (0, 0), (0, down_rows - up_rows), (0, 0)),
            ),
        ],
        axis=3,
    )
    keep = jnp.where(even, grads[:, 0], grads[:, 1])
    give = jnp.where(even, grads[:, 1], grads[:, 0])
    gain_part = jnp.pad(
        jnp.stack(pieces(tail[:local])),
        ((up_rows, down_rows - up_rows - 3), (local, hid - local)),
    )
    grads = (keep.astype(F32) + other_core(give).astype(F32) + gain_part.astype(F32)).astype(BF)
    grads = summed(exchange(grads, "yl"))
    d_w_down = grads[:, :local].astype(BF)
    d_w_up = grads[:up_rows, local:].astype(BF)
    d_gain = jnp.sum(grads[up_rows : up_rows + 3, local : 2 * local], axis=0)
    d_gain = d_gain + other_core(d_gain)

    first = lax.axis_index("gx") * rows

    def own(values):
        return lax.dynamic_slice(values, (first,), (rows,))[:, None]

    own_inv = own(inv)
    own_normed = (x_in.astype(F32) - own(mean)) * own_inv
    d_x = own_inv * (d_z.astype(F32) * gain - scaled_sum - own_normed * cross_sum)
    return (d_x.astype(BF), d_w_up, d_w_down, d_gain)


def solution(mesh):
    sizes = mesh.shape
    cores, x_chips = 2, sizes["gz"] // 2
    fine = Mesh(
        mesh.devices.reshape(sizes["gx"], sizes["gy"] // cores, cores, 2, x_chips),
        ("gx", *GY, *GZ),
    )
    placed = (
        P((*GY, "gx"), GZ),
        P(GZ),
        P((*GZ, *GY), "gx"),
        P(("gx", *GY), GZ),
        P((*GY, "gx"), GZ),
    )
    return jax.shard_map(
        body,
        mesh=fine,
        in_specs=placed,
        out_specs=(P((*GY, "gx"), GZ), P((*GZ, *GY), "gx"), P(("gx", *GY), GZ), P(GZ)),
        check_vma=False,
    )
```

time: 225 us -> 229 us (1.018); the launches traced: 224 us -> 225 us
  starting transfers between devices: 101 us -> 59.5 us
  waiting for transfers between devices: 27.3 us -> 50 us
  blocking collectives: 60.4 us -> 69.7 us
  other arithmetic: 5.59 us -> 10.4 us
  matrix products: 7.78 us -> 12.5 us
    all_to_all x5 -> x3, starting transfers between devices: 57.3 us -> 29.5 us  [exchange(): return lax.all_to_all(blocks, axis, 0, 0, tiled=True)]
    all_to_all x5 -> x3, waiting for transfers between devices: 24.1 us -> 47.7 us  [exchange(): return lax.all_to_all(blocks, axis, 0, 0, tiled=True)]
    ppermute x4 -> x3, starting transfers between devices: 43.5 us -> 30 us  [other_core(): return lax.ppermute(value, 'co', [(0, 1), (1, 0)])]
    all_to_all x1 -> x2, blocking collectives: 31.2 us -> 41.5 us  [exchange(): return lax.all_to_all(blocks, axis, 0, 0, tiled=True)]
    dot_general x5 -> x6, matrix products: 7.78 us -> 12.5 us  [dot(): lax.dot_general(a, b, ((contract[:1], contract[1:]), ((), ())), preferred...]
    convert_element_type x1 -> x3, other arithmetic: 0.21 us -> 3.33 us  [the longest x1 3.06 us: body(): (keep.astype(F32) + other_core(give).astype(F32) + gain_part.astype(F32))...]
  transfers between devices with their start and end apart: 11 -> 8, of which waited for: 5 -> 3; matrix products, arithmetic and copies ran while one was open for 4% -> 6% of each run, Pallas kernels for 0% -> 0%
where the time goes in v3:
time: 229 us; the launch traced here: 225 us
  blocking collectives  69.7 us (30%)
  starting transfers between devices  59.5 us (26%)
  waiting for transfers between devices  50 us (22%)
  between operations  14.5 us (6%)
  matrix products  12.5 us (5%)
  other arithmetic  10.4 us (5%)
  local copies, waits for them, and re-layouts  8.74 us (4%)
    all_to_all x3, waiting for transfers between devices, exchange(): return lax.all_to_all(blocks, axis, 0, 0, tiled=True)  47.7 us
    all_to_all x2, blocking collectives, exchange(): return lax.all_to_all(blocks, axis, 0, 0, tiled=True)  41.5 us
    ppermute x3, starting transfers between devices, other_core(): return lax.ppermute(value, 'co', [(0, 1), (1, 0)])  30 us
    all_to_all x3, starting transfers between devices, exchange(): return lax.all_to_all(blocks, axis, 0, 0, tiled=True)  29.5 us
    all_gather x1, blocking collectives, body(): lax.all_gather(jnp.concatenate([x_in, d_out], axis=1), 'gx', axis=0, tile...  28.2 us
    dot_general x6, matrix products, dot(): lax.dot_general(a, b, ((contract[:1], contract[1:]), ((), ())), preferred...  12.5 us
  transfers between devices with their start and end apart: 8, of which 3 were waited for; matrix products, arithmetic and copies ran while one was open for 6% of the time, Pallas kernels for 0%

profile of v3, /device:TPU:1, one launch (start us, length us, event | category | flops | bytes accessed | tf_op | source)
XLA Modules:
  0.0 225.4 jit_solution(13013697573153311507)
XLA Ops:
  7.2 0.7 all-gather.2.cloned.1.call-update
  7.9 1.8 broadcast_in_dim.10
  9.7 5.4 %all-to-all-start = ((bf16[4,80,896]{2,1,0:T(8,128)(2,1)}), bf16[4,80,896]{2,1,0:T(8,128)(2,1)S(1)}, u32[]{:S(2)}, u32[]{:S(2)}) async-start(bf16[4,80,896]{2,1,0:T(8,128)(2,1)} %broadcast_in_dim.10), calls=%async_computation | async-start | bytes 1146880 | tf_op jit(solution)/shard_map/all_to_all | solution.py:19
  15.2 28.2 %all_gather.6 = bf16[384,1280]{1,0:T(8,128)(2,1)S(1)} all-gather(bf16[48,1280]{1,0:T(8,128)(2,1)S(1)} %pad_maximum_fusion.1), channel_id=1, replica_groups=mesh['gx'=8,'yl'=4,'co'=2,'yh'=2,'xx'=4] {'gx'}, dimensions={0}, use_global_device_ids=true | all-gather | bytes 1105920 | tf_op jit(solution)/shard_map/all_gather | solution.py:70
  43.4 7.5 %collective-permute-start = (bf16[4,80,896]{2,1,0:T(8,128)(2,1)S(1)}, bf16[4,80,896]{2,1,0:T(8,128)(2,1)S(1)}, u32[]{:S(2)}, u32[]{:S(2)}) collective-permute-start(bf16[4,80,896]{2,1,0:T(8,128)(2,1)S(1)} %all-to-all-done), channel_id=1, source_target_pairs={{0,8},{8,0},{1,9},{9,1},{2,10},{10,2},{3,11},{11,3},{4,12},{12,4},... | collective-permute-start | bytes 1720328 | tf_op jit(solution)/shard_map/ppermute | solution.py:47
  51.0 0.1 convert_reduce_fusion.1
  51.1 0.3 fusion.9
  51.5 0.2 copy.62
  51.7 0.9 collective-permute-done
  52.6 0.1 select_bitcast_fusion.1
  52.7 0.1 pad_maximum_fusion
  52.8 0.3 convolution_reduce_fusion
  53.1 0.1 reshape.339
  53.2 1.7 convolution_convert_fusion.3
  55.0 2.9 %convolution_convert_fusion.2 = bf16[384,896]{1,0:T(8,128)(2,1)} fusion(bf16[896,640]{1,0:T(8,128)(2,1)} %all-gather.2.cloned.1.call-done, bf16[384,1280]{1,0:T(8,128)(2,1)S(1)} %all_gather.6), kind=kOutput, calls=%fused_computation.19 | convolution fusion | flops 440745984 | bytes 2326528 | tf_op jit(solution)/shard_map/dot_general | solution.py:51
  57.9 2.1 concatenate.16
  60.1 31.1 %all_to_all.25 = bf16[8,48,1920]{2,1,0:T(8,128)(2,1)S(1)} all-to-all(bf16[8,48,1920]{2,1,0:T(8,128)(2,1)S(1)} %concatenate.16), channel_id=1, replica_groups=mesh['gx'=8,'yl'=4,'co'=2,'yh'=2,'xx'=4] {'yh','xx'}, dimensions={0} | all-to-all | bytes 2949120 | tf_op jit(solution)/shard_map/all_to_all | solution.py:19
  91.2 0.2 convert_reduce_fusion.5
  92.3 0.2 convert_reduce_fusion.2
  92.5 0.2 multiply_convert_fusion
  92.7 0.2 multiply_reduce_fusion.1
  93.0 0.1 copy.63
  93.1 1.2 broadcast_in_dim.12
  94.3 3.6 %all-to-all-start.2 = ((bf16[8,48,1920]{2,1,0:T(8,128)(2,1)}), bf16[8,48,1920]{2,1,0:T(8,128)(2,1)S(1)}, u32[]{:S(2)}, u32[]{:S(2)}) async-start(bf16[8,48,1920]{2,1,0:T(8,128)(2,1)} %broadcast_in_dim.12), calls=%async_computation.2 | async-start | bytes 2949120 | tf_op jit(solution)/shard_map/all_to_all | solution.py:19
  98.0 16.3 %all-to-all-done.2 = bf16[8,48,1920]{2,1,0:T(8,128)(2,1)S(1)} async-done(((bf16[8,48,1920]{2,1,0:T(8,128)(2,1)}), bf16[8,48,1920]{2,1,0:T(8,128)(2,1)S(1)}, u32[]{:S(2)}, u32[]{:S(2)}) %all-to-all-start.2) | async-done | bytes 1474592 | tf_op jit(solution)/shard_map/all_to_all | solution.py:19
  114.3 0.1 fusion.71
  114.5 3.3 %convolution_convert_fusion.1 = bf16[896,640]{1,0:T(8,128)(2,1)} fusion(bf16[384,1920]{1,0:T(8,128)(2,1)S(1)} %bitcast.85, bf16[384,1280]{1,0:T(8,128)(2,1)} %copy-done.2), kind=kOutput, calls=%fused_computation.9 | convolution fusion | flops 440975360 | bytes 2326528 | tf_op jit(solution)/shard_map/dot_general | solution.py:51
  117.8 0.1 copy.59
  117.9 0.1 copy.58
  118.1 1.0 convolution_convert_fusion
  119.1 0.3 copy-done.4
  119.3 0.3 fusion.1
  119.6 1.2 fusion.4
  120.8 19.2 %collective-permute-start.1 = (bf16[4,112,1536]{2,1,0:T(8,128)(2,1)}, bf16[4,112,1536]{2,1,0:T(8,128)(2,1)}, u32[]{:S(2)}, u32[]{:S(2)}) collective-permute-start(bf16[4,112,1536]{2,1,0:T(8,128)(2,1)} %fusion.4), channel_id=1, source_target_pairs={{0,8},{8,0},{1,9},{9,1},{2,10},{10,2},{3,11},{11,3},{4,12},{12,4},... | collective-permute-start | bytes 4128776 | tf_op jit(solution)/shard_map/ppermute | solution.py:47
  140.1 1.3 multiply_reduce_fusion
  141.5 0.1 copy.60
  141.7 3.2 %fusion.13 = (f32[640]{0:T(1024)S(1)}, bf16[384,640]{1,0:T(8,128)(2,1)}) fusion(f32[384]{0:T(512)S(1)} %convert_reduce_fusion.9, f32[384]{0:T(512)S(1)} %convert_reduce_fusion.8, bf16[384,1280]{1,0:T(8,128)(2,1)} %copy-done.2, bf16[640,896]{1,0:T(8,128)(2,1)} %bitcast.83, bf16[384,1920]{1,0:T(8,128)(2,1)} %bitcast.88), kind=kOutput, calls=%fused_computation.34 | convolution fusion | flops 441875840 | bytes 2823680 | tf_op jit(solution)/shard_map/dot_general | solution.py:51
  145.0 10.4 %all_to_all.26 = f32[8,1,736]{2,1,0:T(1,128)S(1)} all-to-all(f32[8,1,736]{2,1,0:T(1,128)S(1)} %broadcast_in_dim.14), channel_id=1, replica_groups=mesh['gx'=8,'yl'=4,'co'=2,'yh'=2,'xx'=4] {'gx'}, dimensions={0} | all-to-all | bytes 47104 | tf_op jit(solution)/shard_map/all_to_all | solution.py:19
  155.6 3.1 %fusion.3 = bf16[4,112,1536]{2,1,0:T(8,128)(2,1)} fusion(bf16[4,112,1536]{2,1,0:T(8,128)(2,1)} %collective-permute-done.1, f32[112,1536]{1,0:T(8,128)S(1)} %fusion.32, pred[]{:T(512)S(6)} %eq.3, bf16[4,2,112,1536]{3,2,1,0:T(8,128)(2,1)S(1)} %fusion.1), kind=kLoop, calls=%fused_computation.5 | loop fusion | flops 4128768 | bytes 6193153 | tf_op jit(solution)/shard_map/convert_element_type | solution.py:158
  158.6 20.5 %all-to-all-start.4 = ((bf16[4,112,1536]{2,1,0:T(8,128)(2,1)}), bf16[4,112,1536]{2,1,0:T(8,128)(2,1)S(1)}, u32[]{:S(2)}, u32[]{:S(2)}) async-start(bf16[4,112,1536]{2,1,0:T(8,128)(2,1)} %fusion.3), calls=%async_computation.5 | async-start | bytes 2752512 | tf_op jit(solution)/shard_map/all_to_all | solution.py:19
  179.1 0.7 reduce-scatter.2.cloned.1.call-update
  180.1 31.4 %all-to-all-done.4 = bf16[4,112,1536]{2,1,0:T(8,128)(2,1)S(1)} async-done(((bf16[4,112,1536]{2,1,0:T(8,128)(2,1)}), bf16[4,112,1536]{2,1,0:T(8,128)(2,1)S(1)}, u32[]{:S(2)}, u32[]{:S(2)}) %all-to-all-start.4) | async-done | bytes 1376288 | tf_op jit(solution)/shard_map/all_to_all | solution.py:19
  211.5 0.2 convert_reduce_fusion
  211.7 3.3 %collective-permute-start.2 = (f32[640]{0:T(1024)S(1)}, f32[640]{0:T(1024)S(1)}, u32[]{:S(2)}, u32[]{:S(2)}) collective-permute-start(f32[640]{0:T(1024)S(1)} %slice_reduce_fusion), channel_id=1, source_target_pairs={{0,8},{8,0},{1,9},{9,1},{2,10},{10,2},{3,11},{11,3},{4,12},{12,4},... | collective-permute-start | bytes 7688 | tf_op jit(solution)/shard_map/ppermute | solution.py:47
  215.0 1.6 multiply_convert_fusion.1
  216.6 0.7 slice.184
  217.2 0.7 slice.183
  217.9 0.6 add.133
  (79 shorter events, 2.0 us)
Async XLA Ops:
  7.2 8.0 %copy-start.8 = (f32[640]{0:T(1024)S(1)}, f32[640]{0:T(1024)}, u32[]{:S(2)}) copy-start(f32[640]{0:T(1024)} %param.6) | copy-start | bytes 7684
  7.2 8.0 %copy-start.6 = (bf16[48,640]{1,0:T(8,128)(2,1)S(1)}, bf16[48,640]{1,0:T(8,128)(2,1)}, u32[]{:S(2)}) copy-start(bf16[48,640]{1,0:T(8,128)(2,1)} %param.5) | copy-start | bytes 184324
  7.2 8.0 %copy-start.7 = (bf16[48,640]{1,0:T(8,128)(2,1)S(1)}, bf16[48,640]{1,0:T(8,128)(2,1)}, u32[]{:S(2)}) copy-start(bf16[48,640]{1,0:T(8,128)(2,1)} %param.9) | copy-start | bytes 184324
  7.2 47.8 %all-gather.2.cloned.1.call-start = ((), (), s32[]{:S(2)}) async-start(), calls=%async_computation.6 | async-start | bytes 1290240 | tf_op jit(solution)/shard_map/all_gather | solution.py:68
  9.7 33.7 %all-to-all-start = ((bf16[4,80,896]{2,1,0:T(8,128)(2,1)}), bf16[4,80,896]{2,1,0:T(8,128)(2,1)S(1)}, u32[]{:S(2)}, u32[]{:S(2)}) async-start(bf16[4,80,896]{2,1,0:T(8,128)(2,1)} %broadcast_in_dim.10), calls=%async_computation | async-start | bytes 1146880 | tf_op jit(solution)/shard_map/all_to_all | solution.py:19
  43.4 11.5 %copy-start.2 = (bf16[384,1280]{1,0:T(8,128)(2,1)}, bf16[384,1280]{1,0:T(8,128)(2,1)S(1)}, u32[]{:S(2)}) copy-start(bf16[384,1280]{1,0:T(8,128)(2,1)S(1)} %all_gather.6) | copy-start | bytes 2949124
  43.4 9.1 %collective-permute-start = (bf16[4,80,896]{2,1,0:T(8,128)(2,1)S(1)}, bf16[4,80,896]{2,1,0:T(8,128)(2,1)S(1)}, u32[]{:S(2)}, u32[]{:S(2)}) collective-permute-start(bf16[4,80,896]{2,1,0:T(8,128)(2,1)S(1)} %all-to-all-done), channel_id=1, source_target_pairs={{0,8},{8,0},{1,9},{9,1},{2,10},{10,2},{3,11},{11,3},{4,12},{12,4},... | collective-permute-start | bytes 1720328 | tf_op jit(solution)/shard_map/ppermute | solution.py:47
  52.8 2.1 copy-start
  55.0 3.0 %copy-start.5 = (bf16[384,896]{1,0:T(8,128)(2,1)S(1)}, bf16[384,896]{1,0:T(8,128)(2,1)}, u32[]{:S(2)}) copy-start(bf16[384,896]{1,0:T(8,128)(2,1)} %convolution_convert_fusion.3) | copy-start | bytes 2064388
  94.3 20.0 %all-to-all-start.2 = ((bf16[8,48,1920]{2,1,0:T(8,128)(2,1)}), bf16[8,48,1920]{2,1,0:T(8,128)(2,1)S(1)}, u32[]{:S(2)}, u32[]{:S(2)}) async-start(bf16[8,48,1920]{2,1,0:T(8,128)(2,1)} %broadcast_in_dim.12), calls=%async_computation.2 | async-start | bytes 2949120 | tf_op jit(solution)/shard_map/all_to_all | solution.py:19
  114.3 3.7 %copy-start.1 = (bf16[8,48,1920]{2,1,0:T(8,128)(2,1)}, bf16[8,48,1920]{2,1,0:T(8,128)(2,1)S(1)}, u32[]{:S(2)}) copy-start(bf16[8,48,1920]{2,1,0:T(8,128)(2,1)S(1)} %all-to-all-done.2) | copy-start | bytes 4423684
  114.5 3.6 %copy-start.3 = (bf16[384,1280]{1,0:T(8,128)(2,1)S(1)}, bf16[384,1280]{1,0:T(8,128)(2,1)}, u32[]{:S(2)}) copy-start(bf16[384,1280]{1,0:T(8,128)(2,1)} %copy-done.2) | copy-start | bytes 2949124
  118.1 1.3 copy-start.4
  120.8 34.7 %collective-permute-start.1 = (bf16[4,112,1536]{2,1,0:T(8,128)(2,1)}, bf16[4,112,1536]{2,1,0:T(8,128)(2,1)}, u32[]{:S(2)}, u32[]{:S(2)}) collective-permute-start(bf16[4,112,1536]{2,1,0:T(8,128)(2,1)} %fusion.4), channel_id=1, source_target_pairs={{0,8},{8,0},{1,9},{9,1},{2,10},{10,2},{3,11},{11,3},{4,12},{12,4},... | collective-permute-start | bytes 4128776 | tf_op jit(solution)/shard_map/ppermute | solution.py:47
  158.6 52.8 %all-to-all-start.4 = ((bf16[4,112,1536]{2,1,0:T(8,128)(2,1)}), bf16[4,112,1536]{2,1,0:T(8,128)(2,1)S(1)}, u32[]{:S(2)}, u32[]{:S(2)}) async-start(bf16[4,112,1536]{2,1,0:T(8,128)(2,1)} %fusion.3), calls=%async_computation.5 | async-start | bytes 2752512 | tf_op jit(solution)/shard_map/all_to_all | solution.py:19
  179.1 35.9 %reduce-scatter.2.cloned.1.call-start = ((), (), s32[]{:S(2)}) async-start(), calls=%async_computation.7 | async-start | bytes 552960 | tf_op jit(solution)/shard_map/reduce_scatter | solution.py:127
  211.7 6.2 %collective-permute-start.2 = (f32[640]{0:T(1024)S(1)}, f32[640]{0:T(1024)S(1)}, u32[]{:S(2)}, u32[]{:S(2)}) collective-permute-start(f32[640]{0:T(1024)S(1)} %slice_reduce_fusion), channel_id=1, source_target_pairs={{0,8},{8,0},{1,9},{9,1},{2,10},{10,2},{3,11},{11,3},{4,12},{12,4},... | collective-permute-start | bytes 7688 | tf_op jit(solution)/shard_map/ppermute | solution.py:47
Sparse Core Ops, SparseCore 0:
  10.1 43.4 all-gather.1
  182.7 31.1 reduce-scatter.1

commit v4 on v3

--- a/solution.py
+++ b/solution.py
@@ -124,43 +124,54 @@
     z = (normed * gain).astype(BF)
 
     dz_part = dot(hgrad_rows, up_full, (1, 1))
-    d_z = lax.psum_scatter(dz_part.astype(BF), "gx", scatter_dimension=0, tiled=True)
     level = jnp.sum(hgrad_rows.astype(F32) * jnp.sum(tilts, axis=0), axis=1)
-    gain_part = jnp.sum(dz_part * normed, axis=0)
+    marks = columns(level, cross)
     tail = jnp.concatenate(
-        [
-            jnp.broadcast_to(gain_part, (n_gx, local)),
-            level.reshape(n_gx, rows),
-            cross.reshape(n_gx, rows),
-        ],
-        axis=1,
-    )
-    tail = jnp.sum(exchange(tail[:, None], "gx")[:, 0], axis=0)
-    scaled_sum = tail[local : local + rows, None] / width
-    cross_sum = tail[local + rows :, None] / width
+        [dz_part.astype(BF), jnp.pad(marks, ((0, 0), (0, LANES - marks.shape[1])))], axis=1
+    ).reshape(n_gx, rows, local + LANES)
+    gain_part = jnp.stack(pieces(jnp.sum(dz_part * normed, axis=0)))
+    gain_part = jnp.pad(gain_part, ((0, 5), (0, LANES)))
+    tail = jnp.concatenate([tail, jnp.broadcast_to(gain_part, (n_gx, *gain_part.shape))], axis=1)
+    tail, acts = lax.optimization_barrier((tail, acts))
+    act_rows, hgrad_rows = acts[:, :hid], acts[:, hid : 2 * hid]
+    tail = exchange(tail, "gx")
+
+    def chunks(value, height):
+        cut = [value[:, i : i + LANES] for i in range(0, value.shape[1], LANES)]
+        return [c.reshape(n_yl, 2, height, LANES) for c in cut]
 
     grads = jnp.concatenate(
         [
-            dot(act_rows, out_rows, (0, 0)).astype(BF).reshape(n_yl, 2, down_rows, local),
-            jnp.pad(
-                dot(z, hgrad_rows, (0, 0)).astype(BF).reshape(n_yl, 2, up_rows, hid),
-                ((0, 0), (0, 0), (0, down_rows - up_rows), (0, 0)),
-            ),
+            *chunks(dot(act_rows, out_rows, (0, 0)).astype(BF), down_rows),
+            *chunks(dot(z, hgrad_rows, (0, 0)).astype(BF), up_rows),
         ],
-        axis=3,
+        axis=2,
     )
     keep = jnp.where(even, grads[:, 0], grads[:, 1])
     give = jnp.where(even, grads[:, 1], grads[:, 0])
-    gain_part = jnp.pad(
-        jnp.stack(pieces(tail[:local])),
-        ((up_rows, down_rows - up_rows - 3), (local, hid - local)),
-    )
-    grads = (keep.astype(F32) + other_core(give).astype(F32) + gain_part.astype(F32)).astype(BF)
-    grads = summed(exchange(grads, "yl"))
-    d_w_down = grads[:, :local].astype(BF)
-    d_w_up = grads[:up_rows, local:].astype(BF)
-    d_gain = jnp.sum(grads[up_rows : up_rows + 3, local : 2 * local], axis=0)
+    swapped, tail = lax.optimization_barrier((other_core(give), tail))
+    grads = (keep.astype(F32) + swapped.astype(F32)).astype(BF)
+    d_z = summed(tail[:, :rows, :local])
+    marks = summed(tail[:, :rows, local:])
+    scaled_sum, cross_sum = (column(marks, i)[:, None] / width for i in range(2))
+    gain_part = jnp.sum(tail[:, rows : rows + 3, :local].astype(F32), axis=(0, 1))
+    gain_part = jnp.concatenate([p.reshape(-1, LANES) for p in pieces(gain_part)])
+    gain_rows = gain_part.shape[0]
+    gain_part = jnp.pad(gain_part, ((0, -gain_rows % 16), (0, 0)))
+    gain_part = jnp.broadcast_to(gain_part, (n_yl, *gain_part.shape))
+    start = grads.shape[1]
+    grads = jnp.pad(grads, ((0, 0), (0, gain_part.shape[1]), (0, 0)))
+    grads = exchange(lax.dynamic_update_slice(grads, gain_part, (0, start, 0)), "yl")
+
+    def unchunk(first, height, count):
+        cut = [grads[:, first + i * height : first + (i + 1) * height] for i in range(count)]
+        return jnp.concatenate([summed(c).astype(BF) for c in cut], axis=1)
+
+    d_gain = jnp.sum(grads[:, start : start + gain_rows].astype(F32), axis=0)
+    d_gain = jnp.sum(d_gain.reshape(3, local), axis=0)
     d_gain = d_gain + other_core(d_gain)
+    d_w_down = unchunk(0, down_rows, local // LANES)
+    d_w_up = unchunk(down_rows * (local // LANES), up_rows, hid // LANES)
 
     first = lax.axis_index("gx") * rows
 
@@ -169,7 +180,7 @@
 
     own_inv = own(inv)
     own_normed = (x_in.astype(F32) - own(mean)) * own_inv
-    d_x = own_inv * (d_z.astype(F32) * gain - scaled_sum - own_normed * cross_sum)
+    d_x = own_inv * (d_z * gain - scaled_sum - own_normed * cross_sum)
     return (d_x.astype(BF), d_w_up, d_w_down, d_gain)
 
 

time: 229 us -> 230 us (level); the launches traced: 225 us -> 230 us
  starting transfers between devices: 59.5 us -> 79.7 us
  blocking collectives: 69.7 us -> 59.3 us
  waiting for transfers between devices: 50 us -> 46.7 us
    all_to_all x3 -> x4, starting transfers between devices: 29.5 us -> 53.3 us  [exchange(): return lax.all_to_all(blocks, axis, 0, 0, tiled=True)]
    all_to_all x2 -> x1, blocking collectives: 41.5 us -> 31.1 us  [exchange(): return lax.all_to_all(blocks, axis, 0, 0, tiled=True)]
    all_to_all x3 -> x4, waiting for transfers between devices: 47.7 us -> 42.2 us  [exchange(): return lax.all_to_all(blocks, axis, 0, 0, tiled=True)]
    ppermute x3, starting transfers between devices: 30 us -> 26.4 us  [other_core(): return lax.ppermute(value, 'co', [(0, 1), (1, 0)])]
    ppermute x3, waiting for transfers between devices: 0.87 us -> 3.81 us  [other_core(): return lax.ppermute(value, 'co', [(0, 1), (1, 0)])]
  transfers between devices with their start and end apart: 8 -> 8, of which waited for: 3 -> 5; matrix products, arithmetic and copies ran while one was open for 6% -> 3% of each run, Pallas kernels for 0% -> 0%
where the time goes in v4:
time: 230 us
  starting transfers between devices  79.7 us (35%)
  blocking collectives  59.3 us (26%)
  waiting for transfers between devices  46.7 us (20%)
  between operations  14.7 us (6%)
  matrix products  11 us (5%)
  local copies, waits for them, and re-layouts  9.3 us (4%)
  other arithmetic  8.99 us (4%)
    all_to_all x4, starting transfers between devices, exchange(): return lax.all_to_all(blocks, axis, 0, 0, tiled=True)  53.3 us
    all_to_all x4, waiting for transfers between devices, exchange(): return lax.all_to_all(blocks, axis, 0, 0, tiled=True)  42.2 us
    all_to_all x1, blocking collectives, exchange(): return lax.all_to_all(blocks, axis, 0, 0, tiled=True)  31.1 us
    all_gather x1, blocking collectives, body(): lax.all_gather(jnp.concatenate([x_in, d_out], axis=1), 'gx', axis=0, tile...  28.2 us
    ppermute x3, starting transfers between devices, other_core(): return lax.ppermute(value, 'co', [(0, 1), (1, 0)])  26.4 us
    dot_general x6, matrix products, dot(): lax.dot_general(a, b, ((contract[:1], contract[1:]), ((), ())), preferred...  11 us
  transfers between devices with their start and end apart: 8, of which 5 were waited for; matrix products, arithmetic and copies ran while one was open for 3% of the time, Pallas kernels for 0%

profile of v4, /device:TPU:1, one launch (start us, length us, event | category | flops | bytes accessed | tf_op | source)
XLA Modules:
  0.0 229.6 jit_solution(10955470867620147761)
XLA Ops:
  7.2 0.7 all-gather.2.cloned.1.call-update
  7.9 1.8 broadcast_in_dim.10
  9.7 5.4 %all-to-all-start = ((bf16[4,80,896]{2,1,0:T(8,128)(2,1)}), bf16[4,80,896]{2,1,0:T(8,128)(2,1)S(1)}, u32[]{:S(2)}, u32[]{:S(2)}) async-start(bf16[4,80,896]{2,1,0:T(8,128)(2,1)} %broadcast_in_dim.10), calls=%async_computation | async-start | bytes 1146880 | tf_op jit(solution)/shard_map/all_to_all | solution.py:19
  15.2 28.2 %all_gather.6 = bf16[384,1280]{1,0:T(8,128)(2,1)S(1)} all-gather(bf16[48,1280]{1,0:T(8,128)(2,1)S(1)} %pad_maximum_fusion.3), channel_id=1, replica_groups=mesh['gx'=8,'yl'=4,'co'=2,'yh'=2,'xx'=4] {'gx'}, dimensions={0}, use_global_device_ids=true | all-gather | bytes 1105920 | tf_op jit(solution)/shard_map/all_gather | solution.py:70
  43.4 7.5 %collective-permute-start = (bf16[4,80,896]{2,1,0:T(8,128)(2,1)S(1)}, bf16[4,80,896]{2,1,0:T(8,128)(2,1)S(1)}, u32[]{:S(2)}, u32[]{:S(2)}) collective-permute-start(bf16[4,80,896]{2,1,0:T(8,128)(2,1)S(1)} %all-to-all-done), channel_id=1, source_target_pairs={{0,8},{8,0},{1,9},{9,1},{2,10},{10,2},{3,11},{11,3},{4,12},{12,4},... | collective-permute-start | bytes 1720328 | tf_op jit(solution)/shard_map/ppermute | solution.py:47
  51.0 0.1 convert_reduce_fusion
  51.1 0.3 fusion.7
  51.5 0.2 copy.87
  51.7 0.9 collective-permute-done
  52.6 0.1 select_bitcast_fusion.1
  52.7 0.1 pad_maximum_fusion.1
  52.8 0.3 convolution_reduce_fusion
  53.2 1.7 convolution_convert_fusion.3
  55.0 2.9 %convolution_convert_fusion.2 = bf16[384,896]{1,0:T(8,128)(2,1)} fusion(bf16[896,640]{1,0:T(8,128)(2,1)} %all-gather.2.cloned.1.call-done, bf16[384,1280]{1,0:T(8,128)(2,1)S(1)} %all_gather.6), kind=kOutput, calls=%fused_computation.11 | convolution fusion | flops 440745984 | bytes 2326528 | tf_op jit(solution)/shard_map/dot_general | solution.py:51
  57.9 2.4 %concatenate.29 = bf16[8,48,1920]{2,1,0:T(8,128)(2,1)S(1)} concatenate(bf16[8,48,896]{2,1,0:T(8,128)(2,1)} %bitcast.108, bf16[8,48,896]{2,1,0:T(8,128)(2,1)} %bitcast.109, bf16[8,48,16]{2,1,0:T(8,128)(2,1)S(1)} %bitcast.117, bf16[8,48,112]{2,1,0:T(8,128)(2,1)S(1)} %broadcast_in_dim.11), dimensions={2} | concatenate | bytes 2949120 | tf_op jit(solution)/shard_map/concatenate | solution.py:92
  60.2 31.1 %all_to_all.25 = bf16[8,48,1920]{2,1,0:T(8,128)(2,1)S(1)} all-to-all(bf16[8,48,1920]{2,1,0:T(8,128)(2,1)S(1)} %concatenate.29), channel_id=1, replica_groups=mesh['gx'=8,'yl'=4,'co'=2,'yh'=2,'xx'=4] {'yh','xx'}, dimensions={0} | all-to-all | bytes 2949120 | tf_op jit(solution)/shard_map/all_to_all | solution.py:19
  91.4 0.2 convert_reduce_fusion.6
  92.4 0.2 convert_reduce_fusion.1
  92.6 0.2 multiply_convert_fusion
  92.8 0.2 multiply_reduce_fusion.1
  93.1 0.1 copy.88
  93.2 1.2 broadcast_in_dim.12
  94.4 4.3 %all-to-all-start.2 = ((bf16[8,48,1920]{2,1,0:T(8,128)(2,1)}), bf16[8,48,1920]{2,1,0:T(8,128)(2,1)}, u32[]{:S(2)}, u32[]{:S(2)}) async-start(bf16[8,48,1920]{2,1,0:T(8,128)(2,1)} %broadcast_in_dim.12), calls=%async_computation.2 | async-start | bytes 2949120 | tf_op jit(solution)/shard_map/all_to_all | solution.py:19
  98.9 15.7 %all-to-all-done.2 = bf16[8,48,1920]{2,1,0:T(8,128)(2,1)} async-done(((bf16[8,48,1920]{2,1,0:T(8,128)(2,1)}), bf16[8,48,1920]{2,1,0:T(8,128)(2,1)}, u32[]{:S(2)}, u32[]{:S(2)}) %all-to-all-start.2) | async-done | bytes 1474592 | tf_op jit(solution)/shard_map/all_to_all | solution.py:19
  114.6 1.2 fusion.80
  115.8 1.3 multiply_reduce_fusion
  117.2 0.1 copy.83
  117.4 0.1 copy.85
  117.5 2.1 fusion.83
  119.7 0.2 copy.72
  119.9 0.9 pad_maximum_fusion.2
  120.8 2.1 convolution_convert_fusion
  122.9 1.9 convolution_convert_fusion.1
  124.9 8.6 %all-to-all-start.3 = ((bf16[8,56,768]{2,1,0:T(8,128)(2,1)}), bf16[8,56,768]{2,1,0:T(8,128)(2,1)S(1)}, u32[]{:S(2)}, u32[]{:S(2)}) async-start(bf16[8,56,768]{2,1,0:T(8,128)(2,1)} %pad_maximum_fusion.2), calls=%async_computation.3 | async-start | bytes 1376256 | tf_op jit(solution)/shard_map/all_to_all | solution.py:19
  133.5 0.2 fusion.81
  133.7 0.2 fusion.82
  134.3 0.1 fusion.5
  134.4 15.5 %collective-permute-start.1 = (bf16[4,1120,128]{2,1,0:T(8,128)(2,1)S(1)}, bf16[4,1120,128]{2,1,0:T(8,128)(2,1)}, u32[]{:S(2)}, u32[]{:S(2)}) collective-permute-start(bf16[4,1120,128]{2,1,0:T(8,128)(2,1)S(1)} %fusion.5), channel_id=1, source_target_pairs={{0,8},{8,0},{1,9},{9,1},{2,10},{10,2},{3,11},{11,3},{4,12},{12,4},... | collective-permute-start | bytes 3440648 | tf_op jit(solution)/shard_map/ppermute | solution.py:47
  149.9 2.5 %collective-permute-done.1 = bf16[4,1120,128]{2,1,0:T(8,128)(2,1)} collective-permute-done((bf16[4,1120,128]{2,1,0:T(8,128)(2,1)S(1)}, bf16[4,1120,128]{2,1,0:T(8,128)(2,1)}, u32[]{:S(2)}, u32[]{:S(2)}) %collective-permute-start.1) | collective-permute-done | bytes 1146912 | tf_op jit(solution)/shard_map/ppermute | solution.py:47
  152.4 1.7 fusion
  154.2 1.1 pad_maximum_fusion
  155.3 35.0 %all-to-all-start.4 = ((bf16[4,1136,128]{2,1,0:T(8,128)(2,1)}), bf16[4,1136,128]{2,1,0:T(8,128)(2,1)S(1)}, u32[]{:S(2)}, u32[]{:S(2)}) async-start(bf16[4,1136,128]{2,1,0:T(8,128)(2,1)} %pad_maximum_fusion), calls=%async_computation.4 | async-start | bytes 2326528 | tf_op jit(solution)/shard_map/all_to_all | solution.py:19
  190.5 0.2 slice_reduce_fusion.13
  190.7 0.7 multiply_convert_fusion.1
  191.5 26.5 %all-to-all-done.4 = bf16[4,1136,128]{2,1,0:T(8,128)(2,1)S(1)} async-done(((bf16[4,1136,128]{2,1,0:T(8,128)(2,1)}), bf16[4,1136,128]{2,1,0:T(8,128)(2,1)S(1)}, u32[]{:S(2)}, u32[]{:S(2)}) %all-to-all-start.4) | async-done | bytes 1163296 | tf_op jit(solution)/shard_map/all_to_all | solution.py:19
  218.0 3.3 %collective-permute-start.2 = (f32[640]{0:T(1024)S(1)}, f32[640]{0:T(1024)S(1)}, u32[]{:S(2)}, u32[]{:S(2)}) collective-permute-start(f32[640]{0:T(1024)S(1)} %reduce_sum.432), channel_id=1, source_target_pairs={{0,8},{8,0},{1,9},{9,1},{2,10},{10,2},{3,11},{11,3},{4,12},{12,4},... | collective-permute-start | bytes 7688 | tf_op jit(solution)/shard_map/ppermute | solution.py:47
  221.8 0.4 collective-permute-done.2
  222.2 0.6 add.123
  (109 shorter events, 2.7 us)
Async XLA Ops:
  7.2 8.0 %copy-start.6 = (f32[640]{0:T(1024)S(1)}, f32[640]{0:T(1024)}, u32[]{:S(2)}) copy-start(f32[640]{0:T(1024)} %param.6) | copy-start | bytes 7684
  7.2 8.0 %copy-start.4 = (bf16[48,640]{1,0:T(8,128)(2,1)S(1)}, bf16[48,640]{1,0:T(8,128)(2,1)}, u32[]{:S(2)}) copy-start(bf16[48,640]{1,0:T(8,128)(2,1)} %param.5) | copy-start | bytes 184324
  7.2 8.0 %copy-start.5 = (bf16[48,640]{1,0:T(8,128)(2,1)S(1)}, bf16[48,640]{1,0:T(8,128)(2,1)}, u32[]{:S(2)}) copy-start(bf16[48,640]{1,0:T(8,128)(2,1)} %param.9) | copy-start | bytes 184324
  7.2 47.8 %all-gather.2.cloned.1.call-start = ((), (), s32[]{:S(2)}) async-start(), calls=%async_computation.5 | async-start | bytes 1290240 | tf_op jit(solution)/shard_map/all_gather | solution.py:68
  9.7 33.7 %all-to-all-start = ((bf16[4,80,896]{2,1,0:T(8,128)(2,1)}), bf16[4,80,896]{2,1,0:T(8,128)(2,1)S(1)}, u32[]{:S(2)}, u32[]{:S(2)}) async-start(bf16[4,80,896]{2,1,0:T(8,128)(2,1)} %broadcast_in_dim.10), calls=%async_computation | async-start | bytes 1146880 | tf_op jit(solution)/shard_map/all_to_all | solution.py:19
  43.4 11.5 %copy-start.2 = (bf16[384,1280]{1,0:T(8,128)(2,1)}, bf16[384,1280]{1,0:T(8,128)(2,1)S(1)}, u32[]{:S(2)}) copy-start(bf16[384,1280]{1,0:T(8,128)(2,1)S(1)} %all_gather.6) | copy-start | bytes 2949124
  43.4 9.1 %collective-permute-start = (bf16[4,80,896]{2,1,0:T(8,128)(2,1)S(1)}, bf16[4,80,896]{2,1,0:T(8,128)(2,1)S(1)}, u32[]{:S(2)}, u32[]{:S(2)}) collective-permute-start(bf16[4,80,896]{2,1,0:T(8,128)(2,1)S(1)} %all-to-all-done), channel_id=1, source_target_pairs={{0,8},{8,0},{1,9},{9,1},{2,10},{10,2},{3,11},{11,3},{4,12},{12,4},... | collective-permute-start | bytes 1720328 | tf_op jit(solution)/shard_map/ppermute | solution.py:47
  52.8 2.2 copy-start
  94.4 20.1 %all-to-all-start.2 = ((bf16[8,48,1920]{2,1,0:T(8,128)(2,1)}), bf16[8,48,1920]{2,1,0:T(8,128)(2,1)}, u32[]{:S(2)}, u32[]{:S(2)}) async-start(bf16[8,48,1920]{2,1,0:T(8,128)(2,1)} %broadcast_in_dim.12), calls=%async_computation.2 | async-start | bytes 2949120 | tf_op jit(solution)/shard_map/all_to_all | solution.py:19
  98.7 18.8 %copy-start.1 = (bf16[4,2,80,896]{3,2,1,0:T(8,128)(2,1)S(1)}, bf16[4,2,80,896]{3,2,1,0:T(8,128)(2,1)}, u32[]{:S(2)}) copy-start(bf16[4,2,80,896]{3,2,1,0:T(8,128)(2,1)} %copy-done) | copy-start | bytes 3440644
  119.6 1.3 copy-start.3
  124.9 27.5 %all-to-all-start.3 = ((bf16[8,56,768]{2,1,0:T(8,128)(2,1)}), bf16[8,56,768]{2,1,0:T(8,128)(2,1)S(1)}, u32[]{:S(2)}, u32[]{:S(2)}) async-start(bf16[8,56,768]{2,1,0:T(8,128)(2,1)} %pad_maximum_fusion.2), calls=%async_computation.3 | async-start | bytes 1376256 | tf_op jit(solution)/shard_map/all_to_all | solution.py:19
  134.4 18.0 %collective-permute-start.1 = (bf16[4,1120,128]{2,1,0:T(8,128)(2,1)S(1)}, bf16[4,1120,128]{2,1,0:T(8,128)(2,1)}, u32[]{:S(2)}, u32[]{:S(2)}) collective-permute-start(bf16[4,1120,128]{2,1,0:T(8,128)(2,1)S(1)} %fusion.5), channel_id=1, source_target_pairs={{0,8},{8,0},{1,9},{9,1},{2,10},{10,2},{3,11},{11,3},{4,12},{12,4},... | collective-permute-start | bytes 3440648 | tf_op jit(solution)/shard_map/ppermute | solution.py:47
  155.3 62.7 %all-to-all-start.4 = ((bf16[4,1136,128]{2,1,0:T(8,128)(2,1)}), bf16[4,1136,128]{2,1,0:T(8,128)(2,1)S(1)}, u32[]{:S(2)}, u32[]{:S(2)}) async-start(bf16[4,1136,128]{2,1,0:T(8,128)(2,1)} %pad_maximum_fusion), calls=%async_computation.4 | async-start | bytes 2326528 | tf_op jit(solution)/shard_map/all_to_all | solution.py:19
  218.0 4.1 %collective-permute-start.2 = (f32[640]{0:T(1024)S(1)}, f32[640]{0:T(1024)S(1)}, u32[]{:S(2)}, u32[]{:S(2)}) collective-permute-start(f32[640]{0:T(1024)S(1)} %reduce_sum.432), channel_id=1, source_target_pairs={{0,8},{8,0},{1,9},{9,1},{2,10},{10,2},{3,11},{11,3},{4,12},{12,4},... | collective-permute-start | bytes 7688 | tf_op jit(solution)/shard_map/ppermute | solution.py:47
  221.7 1.0 copy-start.7
  221.8 1.0 copy-start.8
Sparse Core Ops, SparseCore 0:
  10.1 43.4 all-gather.1

commit v5 on v4

--- a/solution.py
+++ b/solution.py
@@ -43,8 +43,12 @@
     return jnp.sum(lanes[..., 3 * index : 3 * index + 3].astype(F32), axis=-1)
 
 
+def swap(value, axis, bits):
+    return lax.ppermute(value, axis, [(i, i ^ bits) for i in range(lax.axis_size(axis))])
+
+
 def other_core(value):
-    return lax.ppermute(value, "co", [(0, 1), (1, 0)])
+    return swap(value, "co", 1)
 
 
 def dot(a, b, contract):
@@ -149,27 +153,25 @@
     )
     keep = jnp.where(even, grads[:, 0], grads[:, 1])
     give = jnp.where(even, grads[:, 1], grads[:, 0])
-    swapped, tail = lax.optimization_barrier((other_core(give), tail))
-    grads = (keep.astype(F32) + swapped.astype(F32)).astype(BF)
+    grads = (keep.astype(F32) + other_core(give).astype(F32)).astype(BF)
+    place = lax.axis_index("yl")
+
+    def part(index):
+        return lax.dynamic_index_in_dim(grads, index, keepdims=False)
+
+    grads = [part(place)] + [swap(part(place ^ k), "yl", k) for k in range(1, n_yl)]
     d_z = summed(tail[:, :rows, :local])
     marks = summed(tail[:, :rows, local:])
     scaled_sum, cross_sum = (column(marks, i)[:, None] / width for i in range(2))
-    gain_part = jnp.sum(tail[:, rows : rows + 3, :local].astype(F32), axis=(0, 1))
-    gain_part = jnp.concatenate([p.reshape(-1, LANES) for p in pieces(gain_part)])
-    gain_rows = gain_part.shape[0]
-    gain_part = jnp.pad(gain_part, ((0, -gain_rows % 16), (0, 0)))
-    gain_part = jnp.broadcast_to(gain_part, (n_yl, *gain_part.shape))
-    start = grads.shape[1]
-    grads = jnp.pad(grads, ((0, 0), (0, gain_part.shape[1]), (0, 0)))
-    grads = exchange(lax.dynamic_update_slice(grads, gain_part, (0, start, 0)), "yl")
+    d_gain = jnp.sum(tail[:, rows : rows + 3, :local].astype(F32), axis=(0, 1))
+    for axis, bits in (("yl", 1), ("yl", 2), ("co", 1)):
+        d_gain = d_gain + swap(d_gain, axis, bits)
 
     def unchunk(first, height, count):
-        cut = [grads[:, first + i * height : first + (i + 1) * height] for i in range(count)]
-        return jnp.concatenate([summed(c).astype(BF) for c in cut], axis=1)
-
-    d_gain = jnp.sum(grads[:, start : start + gain_rows].astype(F32), axis=0)
-    d_gain = jnp.sum(d_gain.reshape(3, local), axis=0)
-    d_gain = d_gain + other_core(d_gain)
+        cut = [slice(first + i * height, first + (i + 1) * height) for i in range(count)]
+        cut = [sum(g[c].astype(F32) for g in grads) for c in cut]
+        return jnp.concatenate([c.astype(BF) for c in cut], axis=1)
+
     d_w_down = unchunk(0, down_rows, local // LANES)
     d_w_up = unchunk(down_rows * (local // LANES), up_rows, hid // LANES)
 

time: 230 us -> 214 us (0.930)
  waiting for transfers between devices: 46.7 us -> 20.4 us
  starting transfers between devices: 79.7 us -> 86.4 us
    ppermute x3 -> x8, starting transfers between devices: 26.4 us -> 72.5 us  [swap(): lax.ppermute(value, axis, [(i, i ^ bits) for i in range(lax.axis_size(axi...]
    all_to_all x4 -> x3, starting transfers between devices: 53.3 us -> 13.9 us  [exchange(): return lax.all_to_all(blocks, axis, 0, 0, tiled=True)]
    all_to_all x4 -> x3, waiting for transfers between devices: 42.2 us -> 15.7 us  [exchange(): return lax.all_to_all(blocks, axis, 0, 0, tiled=True)]
  transfers between devices with their start and end apart: 8 -> 12, of which waited for: 5 -> 4; matrix products, arithmetic and copies ran while one was open for 3% -> 5% of each run, Pallas kernels for 0% -> 0%
where the time goes in v5:
time: 214 us; the launch traced here: 213 us
  starting transfers between devices  86.4 us (40%)
  blocking collectives  59.3 us (28%)
  waiting for transfers between devices  20.4 us (10%)
  between operations  14.7 us (7%)
  matrix products  11 us (5%)
  other arithmetic  10.9 us (5%)
  local copies, waits for them, and re-layouts  10.2 us (5%)
    ppermute x8, starting transfers between devices, swap(): lax.ppermute(value, axis, [(i, i ^ bits) for i in range(lax.axis_size(axi...  72.5 us
    all_to_all x1, blocking collectives, exchange(): return lax.all_to_all(blocks, axis, 0, 0, tiled=True)  31.1 us
    all_gather x1, blocking collectives, body(): lax.all_gather(jnp.concatenate([x_in, d_out], axis=1), 'gx', axis=0, tile...  28.2 us
    all_to_all x3, waiting for transfers between devices, exchange(): return lax.all_to_all(blocks, axis, 0, 0, tiled=True)  15.7 us
    all_to_all x3, starting transfers between devices, exchange(): return lax.all_to_all(blocks, axis, 0, 0, tiled=True)  13.9 us
    dot_general x6, matrix products, dot(): lax.dot_general(a, b, ((contract[:1], contract[1:]), ((), ())), preferred...  11 us
  transfers between devices with their start and end apart: 12, of which 4 were waited for; matrix products, arithmetic and copies ran while one was open for 5% of the time, Pallas kernels for 0%

profile of v5, /device:TPU:1, one launch (start us, length us, event | category | flops | bytes accessed | tf_op | source)
XLA Modules:
  0.0 213.0 jit_solution(7166205176979230896)
XLA Ops:
  7.2 0.7 all-gather.2.cloned.1.call-update
  7.9 1.8 broadcast_in_dim.8
  9.7 5.4 %all-to-all-start = ((bf16[4,80,896]{2,1,0:T(8,128)(2,1)}), bf16[4,80,896]{2,1,0:T(8,128)(2,1)S(1)}, u32[]{:S(2)}, u32[]{:S(2)}) async-start(bf16[4,80,896]{2,1,0:T(8,128)(2,1)} %broadcast_in_dim.8), calls=%async_computation | async-start | bytes 1146880 | tf_op jit(solution)/shard_map/all_to_all | solution.py:19
  15.2 28.2 %all_gather.6 = bf16[384,1280]{1,0:T(8,128)(2,1)S(1)} all-gather(bf16[48,1280]{1,0:T(8,128)(2,1)S(1)} %pad_maximum_fusion.2), channel_id=1, replica_groups=mesh['gx'=8,'yl'=4,'co'=2,'yh'=2,'xx'=4] {'gx'}, dimensions={0}, use_global_device_ids=true | all-gather | bytes 1105920 | tf_op jit(solution)/shard_map/all_gather | solution.py:74
  43.4 7.5 %collective-permute-start = (bf16[4,80,896]{2,1,0:T(8,128)(2,1)S(1)}, bf16[4,80,896]{2,1,0:T(8,128)(2,1)S(1)}, u32[]{:S(2)}, u32[]{:S(2)}) collective-permute-start(bf16[4,80,896]{2,1,0:T(8,128)(2,1)S(1)} %all-to-all-done), channel_id=1, source_target_pairs={{0,8},{8,0},{1,9},{9,1},{2,10},{10,2},{3,11},{11,3},{4,12},{12,4},... | collective-permute-start | bytes 1720328 | tf_op jit(solution)/shard_map/ppermute | solution.py:47
  51.0 0.1 convert_reduce_fusion
  51.1 0.3 fusion.5
  51.5 0.2 copy.145
  51.7 0.9 collective-permute-done
  52.8 0.3 convolution_reduce_fusion
  53.2 1.7 convolution_convert_fusion.3
  55.0 2.9 %convolution_convert_fusion.2 = bf16[384,896]{1,0:T(8,128)(2,1)} fusion(bf16[896,640]{1,0:T(8,128)(2,1)} %all-gather.2.cloned.1.call-done, bf16[384,1280]{1,0:T(8,128)(2,1)S(1)} %all_gather.6), kind=kOutput, calls=%fused_computation.10 | convolution fusion | flops 440745984 | bytes 2326528 | tf_op jit(solution)/shard_map/dot_general | solution.py:55
  57.9 2.1 %concatenate.25 = bf16[8,48,1920]{2,1,0:T(8,128)(2,1)S(1)} concatenate(bf16[8,48,896]{2,1,0:T(8,128)(2,1)S(1)} %bitcast.163, bf16[8,48,896]{2,1,0:T(8,128)(2,1)} %bitcast.164, bf16[8,48,16]{2,1,0:T(8,128)(2,1)S(1)} %bitcast.172, bf16[8,48,112]{2,1,0:T(8,128)(2,1)S(1)} %broadcast_in_dim.9), dimensions={2} | concatenate | bytes 2949120 | tf_op jit(solution)/shard_map/concatenate | solution.py:96
  60.1 31.1 %all_to_all.20 = bf16[8,48,1920]{2,1,0:T(8,128)(2,1)S(1)} all-to-all(bf16[8,48,1920]{2,1,0:T(8,128)(2,1)S(1)} %concatenate.25), channel_id=1, replica_groups=mesh['gx'=8,'yl'=4,'co'=2,'yh'=2,'xx'=4] {'yh','xx'}, dimensions={0} | all-to-all | bytes 2949120 | tf_op jit(solution)/shard_map/all_to_all | solution.py:19
  91.2 0.2 convert_reduce_fusion.6
  92.3 0.2 convert_reduce_fusion.1
  92.5 0.2 multiply_convert_fusion
  92.7 0.2 multiply_reduce_fusion.1
  93.1 1.2 broadcast_in_dim.10
  94.3 4.3 %all-to-all-start.2 = ((bf16[8,48,1920]{2,1,0:T(8,128)(2,1)}), bf16[8,48,1920]{2,1,0:T(8,128)(2,1)}, u32[]{:S(2)}, u32[]{:S(2)}) async-start(bf16[8,48,1920]{2,1,0:T(8,128)(2,1)} %broadcast_in_dim.10), calls=%async_computation.2 | async-start | bytes 2949120 | tf_op jit(solution)/shard_map/all_to_all | solution.py:19
  98.8 15.7 %all-to-all-done.2 = bf16[8,48,1920]{2,1,0:T(8,128)(2,1)} async-done(((bf16[8,48,1920]{2,1,0:T(8,128)(2,1)}), bf16[8,48,1920]{2,1,0:T(8,128)(2,1)}, u32[]{:S(2)}, u32[]{:S(2)}) %all-to-all-start.2) | async-done | bytes 1474592 | tf_op jit(solution)/shard_map/all_to_all | solution.py:19
  114.4 1.2 fusion.108
  115.6 1.3 multiply_reduce_fusion
  117.4 2.1 fusion.111
  119.5 0.2 copy.120
  119.8 0.9 pad_maximum_fusion.1
  120.7 2.1 convolution_convert_fusion
  122.8 1.9 convolution_convert_fusion.1
  124.8 0.2 fusion.109
  125.0 0.2 fusion.110
  125.7 19.9 %collective-permute-start.1 = (bf16[4,1120,128]{2,1,0:T(8,128)(2,1)S(1)}, bf16[4,1120,128]{2,1,0:T(8,128)(2,1)}, u32[]{:S(2)}, u32[]{:S(2)}) collective-permute-start(bf16[4,1120,128]{2,1,0:T(8,128)(2,1)S(1)} %select_bitcast_fusion), channel_id=1, source_target_pairs={{0,8},{8,0},{1,9},{9,1},{2,10},{10,2},{3,11},{11,3},{4,12},{12,4},... | collective-permute-start | bytes 3440648 | tf_op jit(solution)/shard_map/ppermute | solution.py:47
  145.6 4.2 %all-to-all-start.3 = ((bf16[8,56,768]{2,1,0:T(8,128)(2,1)}), bf16[8,56,768]{2,1,0:T(8,128)(2,1)}, u32[]{:S(2)}, u32[]{:S(2)}) async-start(bf16[8,56,768]{2,1,0:T(8,128)(2,1)} %pad_maximum_fusion.1), calls=%async_computation.3 | async-start | bytes 1376256 | tf_op jit(solution)/shard_map/all_to_all | solution.py:19
  150.0 1.7 fusion
  151.8 20.0 %collective-permute-start.2 = (bf16[1120,128]{1,0:T(8,128)(2,1)S(1)}, bf16[1120,128]{1,0:T(8,128)(2,1)S(1)}, u32[]{:S(2)}, u32[]{:S(2)}) collective-permute-start(bf16[1120,128]{1,0:T(8,128)(2,1)S(1)} %get-tuple-element.29), channel_id=1, source_target_pairs={{0,16},{16,0},{32,48},{48,32},{1,17},{17,1},{33,49},{49,33},{2,18}... | collective-permute-start | bytes 860168 | tf_op jit(solution)/shard_map/ppermute | solution.py:47
  171.8 2.0 collective-permute-start.4
  173.8 3.0 %collective-permute-start.3 = (bf16[1120,128]{1,0:T(8,128)(2,1)S(1)}, bf16[1120,128]{1,0:T(8,128)(2,1)S(1)}, u32[]{:S(2)}, u32[]{:S(2)}) collective-permute-start(bf16[1120,128]{1,0:T(8,128)(2,1)S(1)} %get-tuple-element.31), channel_id=1, source_target_pairs={{0,32},{16,48},{32,0},{48,16},{1,33},{17,49},{33,1},{49,17},{2,34}... | collective-permute-start | bytes 860168 | tf_op jit(solution)/shard_map/ppermute | solution.py:47
  176.8 0.9 convert_reduce_fusion.8
  177.7 14.6 %collective-permute-start.5 = (f32[640]{0:T(1024)S(1)}, f32[640]{0:T(1024)S(1)}, u32[]{:S(2)}, u32[]{:S(2)}) collective-permute-start(f32[640]{0:T(1024)S(1)} %convert_reduce_fusion.8), channel_id=1, source_target_pairs={{0,16},{16,0},{32,48},{48,32},{1,17},{17,1},{33,49},{49,33},{2,18}... | collective-permute-start | bytes 7688 | tf_op jit(solution)/shard_map/ppermute | solution.py:47
  192.3 0.9 convert_reduce_fusion.4
  193.2 0.2 slice_reduce_fusion.1
  193.5 2.5 %collective-permute-start.6 = (f32[640]{0:T(1024)S(1)}, f32[640]{0:T(1024)S(1)}, u32[]{:S(2)}, u32[]{:S(2)}) collective-permute-start(f32[640]{0:T(1024)S(1)} %add.288), channel_id=1, source_target_pairs={{0,32},{16,48},{32,0},{48,16},{1,33},{17,49},{33,1},{49,17},{2,34}... | collective-permute-start | bytes 7688 | tf_op jit(solution)/shard_map/ppermute | solution.py:47
  195.9 1.1 convert_reduce_fusion.3
  197.0 3.0 %collective-permute-done.6 = f32[640]{0:T(1024)S(1)} collective-permute-done((f32[640]{0:T(1024)S(1)}, f32[640]{0:T(1024)S(1)}, u32[]{:S(2)}, u32[]{:S(2)}) %collective-permute-start.6) | collective-permute-done | bytes 2592 | tf_op jit(solution)/shard_map/ppermute | solution.py:47
  200.1 3.0 %collective-permute-start.7 = (f32[640]{0:T(1024)S(1)}, f32[640]{0:T(1024)S(1)}, u32[]{:S(2)}, u32[]{:S(2)}) collective-permute-start(f32[640]{0:T(1024)S(1)} %add.289), channel_id=1, source_target_pairs={{0,8},{8,0},{1,9},{9,1},{2,10},{10,2},{3,11},{11,3},{4,12},{12,4},... | collective-permute-start | bytes 7688 | tf_op jit(solution)/shard_map/ppermute | solution.py:47
  203.1 0.7 multiply_convert_fusion.1
  203.9 0.6 add.290
  205.0 0.5 copy-done.9
  205.5 0.7 copy-done.8
  (113 shorter events, 3.4 us)
Async XLA Ops:
  7.2 8.0 %copy-start.7 = (f32[640]{0:T(1024)S(1)}, f32[640]{0:T(1024)}, u32[]{:S(2)}) copy-start(f32[640]{0:T(1024)} %param.6) | copy-start | bytes 7684
  7.2 8.0 %copy-start.5 = (bf16[48,640]{1,0:T(8,128)(2,1)S(1)}, bf16[48,640]{1,0:T(8,128)(2,1)}, u32[]{:S(2)}) copy-start(bf16[48,640]{1,0:T(8,128)(2,1)} %param.5) | copy-start | bytes 184324
  7.2 8.0 %copy-start.6 = (bf16[48,640]{1,0:T(8,128)(2,1)S(1)}, bf16[48,640]{1,0:T(8,128)(2,1)}, u32[]{:S(2)}) copy-start(bf16[48,640]{1,0:T(8,128)(2,1)} %param.9) | copy-start | bytes 184324
  7.2 47.8 %all-gather.2.cloned.1.call-start = ((), (), s32[]{:S(2)}) async-start(), calls=%async_computation.4 | async-start | bytes 1290240 | tf_op jit(solution)/shard_map/all_gather | solution.py:72
  9.7 33.7 %all-to-all-start = ((bf16[4,80,896]{2,1,0:T(8,128)(2,1)}), bf16[4,80,896]{2,1,0:T(8,128)(2,1)S(1)}, u32[]{:S(2)}, u32[]{:S(2)}) async-start(bf16[4,80,896]{2,1,0:T(8,128)(2,1)} %broadcast_in_dim.8), calls=%async_computation | async-start | bytes 1146880 | tf_op jit(solution)/shard_map/all_to_all | solution.py:19
  43.4 11.5 %copy-start.2 = (bf16[384,1280]{1,0:T(8,128)(2,1)}, bf16[384,1280]{1,0:T(8,128)(2,1)S(1)}, u32[]{:S(2)}) copy-start(bf16[384,1280]{1,0:T(8,128)(2,1)S(1)} %all_gather.6) | copy-start | bytes 2949124
  43.4 9.1 %collective-permute-start = (bf16[4,80,896]{2,1,0:T(8,128)(2,1)S(1)}, bf16[4,80,896]{2,1,0:T(8,128)(2,1)S(1)}, u32[]{:S(2)}, u32[]{:S(2)}) collective-permute-start(bf16[4,80,896]{2,1,0:T(8,128)(2,1)S(1)} %all-to-all-done), channel_id=1, source_target_pairs={{0,8},{8,0},{1,9},{9,1},{2,10},{10,2},{3,11},{11,3},{4,12},{12,4},... | collective-permute-start | bytes 1720328 | tf_op jit(solution)/shard_map/ppermute | solution.py:47
  52.8 2.2 %copy-start = (bf16[4,2,80,896]{3,2,1,0:T(8,128)(2,1)}, bf16[4,2,80,896]{3,2,1,0:T(8,128)(2,1)S(1)}, u32[]{:S(2)}) copy-start(bf16[4,2,80,896]{3,2,1,0:T(8,128)(2,1)S(1)} %pad_maximum_fusion) | copy-start | bytes 3440644
  55.0 3.0 %copy-start.4 = (bf16[384,896]{1,0:T(8,128)(2,1)S(1)}, bf16[384,896]{1,0:T(8,128)(2,1)}, u32[]{:S(2)}) copy-start(bf16[384,896]{1,0:T(8,128)(2,1)} %convolution_convert_fusion.3) | copy-start | bytes 2064388
  94.3 20.2 %all-to-all-start.2 = ((bf16[8,48,1920]{2,1,0:T(8,128)(2,1)}), bf16[8,48,1920]{2,1,0:T(8,128)(2,1)}, u32[]{:S(2)}, u32[]{:S(2)}) async-start(bf16[8,48,1920]{2,1,0:T(8,128)(2,1)} %broadcast_in_dim.10), calls=%async_computation.2 | async-start | bytes 2949120 | tf_op jit(solution)/shard_map/all_to_all | solution.py:19
  98.6 18.8 %copy-start.1 = (bf16[4,2,80,896]{3,2,1,0:T(8,128)(2,1)S(1)}, bf16[4,2,80,896]{3,2,1,0:T(8,128)(2,1)}, u32[]{:S(2)}) copy-start(bf16[4,2,80,896]{3,2,1,0:T(8,128)(2,1)} %copy-done) | copy-start | bytes 3440644
  119.5 1.2 copy-start.3
  125.7 24.3 %collective-permute-start.1 = (bf16[4,1120,128]{2,1,0:T(8,128)(2,1)S(1)}, bf16[4,1120,128]{2,1,0:T(8,128)(2,1)}, u32[]{:S(2)}, u32[]{:S(2)}) collective-permute-start(bf16[4,1120,128]{2,1,0:T(8,128)(2,1)S(1)} %select_bitcast_fusion), channel_id=1, source_target_pairs={{0,8},{8,0},{1,9},{9,1},{2,10},{10,2},{3,11},{11,3},{4,12},{12,4},... | collective-permute-start | bytes 3440648 | tf_op jit(solution)/shard_map/ppermute | solution.py:47
  145.6 31.2 %all-to-all-start.3 = ((bf16[8,56,768]{2,1,0:T(8,128)(2,1)}), bf16[8,56,768]{2,1,0:T(8,128)(2,1)}, u32[]{:S(2)}, u32[]{:S(2)}) async-start(bf16[8,56,768]{2,1,0:T(8,128)(2,1)} %pad_maximum_fusion.1), calls=%async_computation.3 | async-start | bytes 1376256 | tf_op jit(solution)/shard_map/all_to_all | solution.py:19
  151.8 52.7 %collective-permute-start.2 = (bf16[1120,128]{1,0:T(8,128)(2,1)S(1)}, bf16[1120,128]{1,0:T(8,128)(2,1)S(1)}, u32[]{:S(2)}, u32[]{:S(2)}) collective-permute-start(bf16[1120,128]{1,0:T(8,128)(2,1)S(1)} %get-tuple-element.29), channel_id=1, source_target_pairs={{0,16},{16,0},{32,48},{48,32},{1,17},{17,1},{33,49},{49,33},{2,18}... | collective-permute-start | bytes 860168 | tf_op jit(solution)/shard_map/ppermute | solution.py:47
  171.8 32.7 %collective-permute-start.4 = (bf16[1120,128]{1,0:T(8,128)(2,1)S(1)}, bf16[1120,128]{1,0:T(8,128)(2,1)S(1)}, u32[]{:S(2)}, u32[]{:S(2)}) collective-permute-start(bf16[1120,128]{1,0:T(8,128)(2,1)S(1)} %get-tuple-element.30), channel_id=1, source_target_pairs={{0,48},{16,32},{32,16},{48,0},{1,49},{17,33},{33,17},{49,1},{2,50}... | collective-permute-start | bytes 860168 | tf_op jit(solution)/shard_map/ppermute | solution.py:47
  173.8 30.7 %collective-permute-start.3 = (bf16[1120,128]{1,0:T(8,128)(2,1)S(1)}, bf16[1120,128]{1,0:T(8,128)(2,1)S(1)}, u32[]{:S(2)}, u32[]{:S(2)}) collective-permute-start(bf16[1120,128]{1,0:T(8,128)(2,1)S(1)} %get-tuple-element.31), channel_id=1, source_target_pairs={{0,32},{16,48},{32,0},{48,16},{1,33},{17,49},{33,1},{49,17},{2,34}... | collective-permute-start | bytes 860168 | tf_op jit(solution)/shard_map/ppermute | solution.py:47
  177.7 15.7 %collective-permute-start.5 = (f32[640]{0:T(1024)S(1)}, f32[640]{0:T(1024)S(1)}, u32[]{:S(2)}, u32[]{:S(2)}) collective-permute-start(f32[640]{0:T(1024)S(1)} %convert_reduce_fusion.8), channel_id=1, source_target_pairs={{0,16},{16,0},{32,48},{48,32},{1,17},{17,1},{33,49},{49,33},{2,18}... | collective-permute-start | bytes 7688 | tf_op jit(solution)/shard_map/ppermute | solution.py:47
  193.5 6.6 %collective-permute-start.6 = (f32[640]{0:T(1024)S(1)}, f32[640]{0:T(1024)S(1)}, u32[]{:S(2)}, u32[]{:S(2)}) collective-permute-start(f32[640]{0:T(1024)S(1)} %add.288), channel_id=1, source_target_pairs={{0,32},{16,48},{32,0},{48,16},{1,33},{17,49},{33,1},{49,17},{2,34}... | collective-permute-start | bytes 7688 | tf_op jit(solution)/shard_map/ppermute | solution.py:47
  200.1 3.8 %collective-permute-start.7 = (f32[640]{0:T(1024)S(1)}, f32[640]{0:T(1024)S(1)}, u32[]{:S(2)}, u32[]{:S(2)}) collective-permute-start(f32[640]{0:T(1024)S(1)} %add.289), channel_id=1, source_target_pairs={{0,8},{8,0},{1,9},{9,1},{2,10},{10,2},{3,11},{11,3},{4,12},{12,4},... | collective-permute-start | bytes 7688 | tf_op jit(solution)/shard_map/ppermute | solution.py:47
  204.8 0.7 copy-start.9
  205.5 0.7 copy-start.8
Sparse Core Ops, SparseCore 0:
  10.1 43.4 all-gather.1

commit v6 on v5

--- a/solution.py
+++ b/solution.py
@@ -1,6 +1,8 @@
 import jax
 import jax.numpy as jnp
 from jax import lax
+from jax.experimental import pallas as pl
+from jax.experimental.pallas import tpu as pltpu
 from jax.sharding import Mesh
 from jax.sharding import PartitionSpec as P
 
@@ -53,6 +55,105 @@
 
 def dot(a, b, contract):
     return lax.dot_general(a, b, ((contract[:1], contract[1:]), ((), ())), preferred_element_type=F32)
+
+
+VMEM = pl.BlockSpec(memory_space=pltpu.VMEM)
+
+
+def local_call(kernel, out, *args, scratch=(), scalar=False):
+    specs = [VMEM] * len(args)
+    if scalar:
+        specs[0] = pl.BlockSpec(memory_space=pltpu.SMEM)
+    return pl.pallas_call(
+        kernel,
+        out_shape=out,
+        in_specs=specs,
+        out_specs=jax.tree.map(lambda _: VMEM, out),
+        scratch_shapes=scratch,
+        compiler_params=pltpu.CompilerParams(vmem_limit_bytes=40 * 1024 * 1024),
+    )(*args)
+
+
+def fill_kernel(y_ref, both_ref, up_ref, down_ref, extra_ref, out_ref):
+    n, block, _ = out_ref.shape
+    local, hid = up_ref.shape
+    part = jnp.dot(y_ref[...], up_ref[...], preferred_element_type=F32).astype(BF)
+    out_ref[:, :, :hid] = part.reshape(n, block, hid)
+    part = dot(both_ref[:, local:], down_ref[...], (1, 1)).astype(BF)
+    out_ref[:, :, hid : 2 * hid] = part.reshape(n, block, hid)
+    out_ref[:, :, 2 * hid :] = extra_ref[...]
+
+
+def lane_pieces(values, lane):
+    out = jnp.zeros(lane.shape, F32)
+    for i, value in enumerate(values):
+        for j in range(3):
+            piece = value.astype(BF).astype(F32)
+            out = jnp.where(lane == 3 * i + j, piece, out)
+            value = value - piece
+    return out
+
+
+def tokens_kernel(acts_ref, both_ref, up_ref, tilt_ref, gain_ref, tail_ref, z_ref):
+    n, high, _ = tail_ref.shape
+    local, hid = up_ref.shape
+    tall = acts_ref.shape[0]
+    rows = tall // n
+    grad = acts_ref[:, hid : 2 * hid]
+    marks = acts_ref[:, 2 * hid :].astype(F32)
+    lane = lax.broadcasted_iota(jnp.int32, marks.shape, 1)
+
+    def taken(index):
+        mine = (lane >= 3 * index) & (lane < 3 * index + 3)
+        return jnp.sum(jnp.where(mine, marks, 0.0), axis=1, keepdims=True)
+
+    cross, mean, inv = (taken(i) for i in range(3))
+    normed = (both_ref[:, :local].astype(F32) - mean) * inv
+    z_ref[...] = (normed * gain_ref[...]).astype(BF)
+    d_z = dot(grad, up_ref[...], (1, 1))
+    level = jnp.sum(grad.astype(F32) * tilt_ref[...], axis=1, keepdims=True)
+    tail_ref[:, :rows, :local] = d_z.astype(BF).reshape(n, rows, local)
+    sums = lane_pieces((level, cross), lane).astype(BF)
+    tail_ref[:, :rows, local:] = sums.reshape(n, rows, LANES)
+    rest = jnp.sum(d_z * normed, axis=0, keepdims=True)
+    row = lax.broadcasted_iota(jnp.int32, (high - rows, local), 0)
+    gains = jnp.zeros(row.shape, F32)
+    for j in range(3):
+        piece = rest.astype(BF).astype(F32)
+        gains = jnp.where(row == j, piece, gains)
+        rest = rest - piece
+    gains = gains.astype(BF)
+    for i in range(n):
+        tail_ref[i, rows:, :local] = gains
+        tail_ref[i, rows:, local:] = jnp.zeros((high - rows, LANES), BF)
+
+
+def grads_kernel(core_ref, acts_ref, both_ref, z_ref, keep_ref, give_ref, down_ref, up_ref):
+    hid, local = down_ref.shape
+    down_ref[...] = dot(acts_ref[:, :hid], both_ref[:, local:], (0, 0)).astype(BF)
+    up_ref[...] = dot(z_ref[...], acts_ref[:, hid : 2 * hid], (0, 0)).astype(BF)
+    core = core_ref[0]
+    n = keep_ref.shape[0]
+    for ref, which in ((keep_ref, core), (give_ref, 1 - core)):
+        for j in range(n):
+            first = 0
+            for whole in (down_ref, up_ref):
+                height = whole.shape[0] // (2 * n)
+                start = pl.multiple_of((2 * j + which) * height, 16)
+                for i in range(0, whole.shape[1], LANES):
+                    ref[j, first : first + height, :] = whole[pl.ds(start, height), i : i + LANES]
+                    first += height
+
+
+def merge_kernel(*refs):
+    *parts, down_ref, up_ref = refs
+    first = 0
+    for out in (down_ref, up_ref):
+        height = out.shape[0]
+        for i in range(0, out.shape[1], LANES):
+            total = sum(p[first : first + height, :].astype(F32) for p in parts)
+            out[:, i : i + LANES] = total.astype(BF)
+            first += height
 
 
 def body(x_in, gain, w_up, w_down, d_out):
@@ -74,7 +175,7 @@
     both = lax.all_gather(jnp.concatenate([x_in, d_out], axis=1), "gx", axis=0, tiled=True)
     both, up_mine = lax.optimization_barrier((both, up_mine))
     up_full = by_core(up_mine, other_core(up_mine))
-    x_rows, out_rows = both[:, :local].astype(F32), both[:, local:]
+    x_rows = both[:, :local].astype(F32)
 
     part_sum = jnp.sum(x_rows, axis=1)
     off = x_rows - (part_sum / local)[:, None]
@@ -93,13 +194,10 @@
         ],
         axis=2,
     )
-    pair = jnp.concatenate(
-        [
-            dot(y, up_full, (1, 0)).astype(BF).reshape(n_gz, block, hid),
-            dot(out_rows, down_full, (1, 1)).astype(BF).reshape(n_gz, block, hid),
-            extra,
-        ],
-        axis=2,
+    pair = local_call(
+        fill_kernel,
+        jax.ShapeDtypeStruct((n_gz, block, 2 * hid + LANES), BF),
+        *(y, both, up_full, down_full, extra),
     )
     pair = exchange(pair, GZ)
     marks = pair[:, :, 2 * hid : 2 * hid + spare]
@@ -122,37 +220,26 @@
     marks = jnp.pad(marks, ((0, 0), (0, LANES - marks.shape[1])))
     acts = jnp.concatenate([act_f.astype(BF), d_hidden, marks], axis=1)
     acts = spread(acts, GZ).reshape(all_rows, -1)
-    act_rows, hgrad_rows, marks = acts[:, :hid], acts[:, hid : 2 * hid], acts[:, 2 * hid :]
-    cross, mean, inv = (column(marks, i) for i in range(3))
-    normed = (x_rows - mean[:, None]) * inv[:, None]
-    z = (normed * gain).astype(BF)
-
-    dz_part = dot(hgrad_rows, up_full, (1, 1))
-    level = jnp.sum(hgrad_rows.astype(F32) * jnp.sum(tilts, axis=0), axis=1)
-    marks = columns(level, cross)
-    tail = jnp.concatenate(
-        [dz_part.astype(BF), jnp.pad(marks, ((0, 0), (0, LANES - marks.shape[1])))], axis=1
-    ).reshape(n_gx, rows, local + LANES)
-    gain_part = jnp.stack(pieces(jnp.sum(dz_part * normed, axis=0)))
-    gain_part = jnp.pad(gain_part, ((0, 5), (0, LANES)))
-    tail = jnp.concatenate([tail, jnp.broadcast_to(gain_part, (n_gx, *gain_part.shape))], axis=1)
-    tail, acts = lax.optimization_barrier((tail, acts))
-    act_rows, hgrad_rows = acts[:, :hid], acts[:, hid : 2 * hid]
+    _, mean, inv = (column(acts[:, 2 * hid :], i) for i in range(3))
+
+    tail, z = local_call(
+        tokens_kernel,
+        (
+            jax.ShapeDtypeStruct((n_gx, rows + 8, local + LANES), BF),
+            jax.ShapeDtypeStruct((all_rows, local), BF),
+        ),
+        *(acts, both, up_full, jnp.sum(tilts, axis=0)[None], gain[None]),
+    )
     tail = exchange(tail, "gx")
 
-    def chunks(value, height):
-        cut = [value[:, i : i + LANES] for i in range(0, value.shape[1], LANES)]
-        return [c.reshape(n_yl, 2, height, LANES) for c in cut]
-
-    grads = jnp.concatenate(
-        [
-            *chunks(dot(act_rows, out_rows, (0, 0)).astype(BF), down_rows),
-            *chunks(dot(z, hgrad_rows, (0, 0)).astype(BF), up_rows),
-        ],
-        axis=2,
-    )
-    keep = jnp.where(even, grads[:, 0], grads[:, 1])
-    give = jnp.where(even, grads[:, 1], grads[:, 0])
+    packed = down_rows * (local // LANES) + up_rows * (hid // LANES)
+    keep, give = local_call(
+        grads_kernel,
+        (jax.ShapeDtypeStruct((n_yl, packed, LANES), BF),) * 2,
+        *(lax.axis_index("co")[None], acts, both, z),
+        scratch=(pltpu.VMEM((hid, local), BF), pltpu.VMEM((local, hid), BF)),
+        scalar=True,
+    )
     grads = (keep.astype(F32) + other_core(give).astype(F32)).astype(BF)
     place = lax.axis_index("yl")
 
@@ -167,13 +254,14 @@
     for axis, bits in (("yl", 1), ("yl", 2), ("co", 1)):
         d_gain = d_gain + swap(d_gain, axis, bits)
 
-    def unchunk(first, height, count):
-        cut = [slice(first + i * height, first + (i + 1) * height) for i in range(count)]
-        cut = [sum(g[c].astype(F32) for g in grads) for c in cut]
-        return jnp.concatenate([c.astype(BF) for c in cut], axis=1)
-
-    d_w_down = unchunk(0, down_rows, local // LANES)
-    d_w_up = unchunk(down_rows * (local // LANES), up_rows, hid // LANES)
+    d_w_down, d_w_up = local_call(
+        merge_kernel,
+        (
+            jax.ShapeDtypeStruct((down_rows, local), BF),
+            jax.ShapeDtypeStruct((up_rows, hid), BF),
+        ),
+        *grads,
+    )
 
     first = lax.axis_index("gx") * rows
 

time: 214 us -> 207 us (0.967)
  matrix products: 11 us -> 0.28 us
  Pallas kernels: 0 us -> 8.53 us
  local copies, waits for them, and re-layouts: 10.2 us -> 6.54 us
    ppermute x8, starting transfers between devices: 72.5 us -> 59 us  [swap(): lax.ppermute(value, axis, [(i, i ^ bits) for i in range(lax.axis_size(axi...]
    all_to_all x3, starting transfers between devices: 13.9 us -> 26.7 us  [exchange(): return lax.all_to_all(blocks, axis, 0, 0, tiled=True)]
    dot_general x6 -> x1, matrix products: 11 us -> 0.28 us  [dot(): lax.dot_general(a, b, ((contract[:1], contract[1:]), ((), ())), preferred...]
    pallas_call x0 -> x4, Pallas kernels: none -> 8.53 us  [local_call(): pl.pallas_call(kernel, out_shape=out, in_specs=specs, out_specs=jax.tree....]
    all_to_all x3, waiting for transfers between devices: 15.7 us -> 18.7 us  [exchange(): return lax.all_to_all(blocks, axis, 0, 0, tiled=True)]
    ppermute x8, waiting for transfers between devices: 3.99 us -> 1.66 us  [swap(): lax.ppermute(value, axis, [(i, i ^ bits) for i in range(lax.axis_size(axi...]
    concatenate x2 -> x0, local copies, waits for them, and re-layouts: 2.17 us -> none  [the longest x1 2.15 us: body(): jnp.concatenate([dot(y, up_full, (1, 0)).astype(BF).reshape(n_gz, block,...]
  transfers between devices with their start and end apart: 12 -> 12, of which waited for: 4 -> 6; matrix products, arithmetic and copies ran while one was open for 5% -> 6% of each run, Pallas kernels for 0% -> 0%
where the time goes in v6:
time: 207 us; the launch traced here: 206 us
  starting transfers between devices  85.7 us (41%)
  blocking collectives  58 us (28%)
  waiting for transfers between devices  21.2 us (10%)
  between operations  14.4 us (7%)
  other arithmetic  11.4 us (6%)
  Pallas kernels  8.53 us (4%)
  local copies, waits for them, and re-layouts  6.54 us (3%)
    ppermute x8, starting transfers between devices, swap(): lax.ppermute(value, axis, [(i, i ^ bits) for i in range(lax.axis_size(axi...  59 us
    all_to_all x1, blocking collectives, exchange(): return lax.all_to_all(blocks, axis, 0, 0, tiled=True)  29.8 us
    all_gather x1, blocking collectives, body(): lax.all_gather(jnp.concatenate([x_in, d_out], axis=1), 'gx', axis=0, tile...  28.2 us
    all_to_all x3, starting transfers between devices, exchange(): return lax.all_to_all(blocks, axis, 0, 0, tiled=True)  26.7 us
    all_to_all x3, waiting for transfers between devices, exchange(): return lax.all_to_all(blocks, axis, 0, 0, tiled=True)  18.7 us
    pallas_call x4, Pallas kernels, local_call(): pl.pallas_call(kernel, out_shape=out, in_specs=specs, out_specs=jax.tree....  8.53 us
  transfers between devices with their start and end apart: 12, of which 6 were waited for; matrix products, arithmetic and copies ran while one was open for 6% of the time, Pallas kernels for 0%

profile of v6, /device:TPU:1, one launch (start us, length us, event | category | flops | bytes accessed | tf_op | source)
XLA Modules:
  0.0 206.0 jit_solution(4654611426114896168)
XLA Ops:
  7.2 0.7 all-gather.2.cloned.1.call-update
  7.9 1.8 broadcast_in_dim.12
  9.7 5.4 %all-to-all-start = ((bf16[4,80,896]{2,1,0:T(8,128)(2,1)}), bf16[4,80,896]{2,1,0:T(8,128)(2,1)S(1)}, u32[]{:S(2)}, u32[]{:S(2)}) async-start(bf16[4,80,896]{2,1,0:T(8,128)(2,1)} %broadcast_in_dim.12), calls=%async_computation | async-start | bytes 1146880 | tf_op jit(solution)/shard_map/all_to_all | solution.py:21
  15.2 28.2 %all_gather.6.both_ref = bf16[384,1280]{1,0:T(8,128)(2,1)S(1)} all-gather(bf16[48,1280]{1,0:T(8,128)(2,1)S(1)} %pad_maximum_fusion.1), channel_id=1, replica_groups=mesh['gx'=8,'yl'=4,'co'=2,'yh'=2,'xx'=4] {'gx'}, dimensions={0}, use_global_device_ids=true | all-gather | bytes 1105920 | tf_op jit(solution)/shard_map/all_gather | solution.py:175
  43.4 7.5 %collective-permute-start = (bf16[4,80,896]{2,1,0:T(8,128)(2,1)S(1)}, bf16[4,80,896]{2,1,0:T(8,128)(2,1)S(1)}, u32[]{:S(2)}, u32[]{:S(2)}) collective-permute-start(bf16[4,80,896]{2,1,0:T(8,128)(2,1)S(1)} %all-to-all-done), channel_id=1, source_target_pairs={{0,8},{8,0},{1,9},{9,1},{2,10},{10,2},{3,11},{11,3},{4,12},{12,4},... | collective-permute-start | bytes 1720328 | tf_op jit(solution)/shard_map/ppermute | solution.py:49
  51.0 0.1 convert_reduce_fusion.2
  51.1 0.3 fusion.3
  51.5 0.2 copy.24
  51.7 0.8 collective-permute-done
  52.6 0.1 select_bitcast_fusion.1
  52.7 0.1 pad_maximum_fusion
  52.8 0.3 convolution_reduce_fusion
  53.3 0.1 pad_maximum_fusion.2.extra_ref
  53.4 0.2 all-gather.2.cloned.1.call-done.down_ref
  53.6 1.3 copy-done
  54.8 1.4 shard_map.84
  56.2 29.8 %all_to_all.20 = bf16[8,48,1920]{2,1,0:T(8,128)(2,1)S(1)} all-to-all(bf16[8,48,1920]{2,1,0:T(8,128)(2,1)S(1)} %shard_map.84), channel_id=1, replica_groups=mesh['gx'=8,'yl'=4,'co'=2,'yh'=2,'xx'=4] {'yh','xx'}, dimensions={0} | all-to-all | bytes 2949120 | tf_op jit(solution)/shard_map/all_to_all | solution.py:21
  86.0 0.2 convert_reduce_fusion.8
  86.3 0.8 copy-done.1
  87.8 1.5 convert_reduce_fusion
  89.3 0.2 multiply_convert_fusion
  89.5 0.2 multiply_reduce_fusion
  89.8 0.1 copy.25
  89.9 1.2 broadcast_in_dim.14
  91.2 4.3 %all-to-all-start.2 = ((bf16[8,48,1920]{2,1,0:T(8,128)(2,1)}), bf16[8,48,1920]{2,1,0:T(8,128)(2,1)}, u32[]{:S(2)}, u32[]{:S(2)}) async-start(bf16[8,48,1920]{2,1,0:T(8,128)(2,1)} %broadcast_in_dim.14), calls=%async_computation.2 | async-start | bytes 2949120 | tf_op jit(solution)/shard_map/all_to_all | solution.py:21
  95.5 0.9 convert_reduce_fusion.9
  96.5 14.0 %all-to-all-done.2 = bf16[8,48,1920]{2,1,0:T(8,128)(2,1)} async-done(((bf16[8,48,1920]{2,1,0:T(8,128)(2,1)}), bf16[8,48,1920]{2,1,0:T(8,128)(2,1)}, u32[]{:S(2)}, u32[]{:S(2)}) %all-to-all-start.2) | async-done | bytes 1474592 | tf_op jit(solution)/shard_map/all_to_all | solution.py:21
  110.5 3.1 %shard_map.85 = (bf16[8,56,768]{2,1,0:T(8,128)(2,1)}, bf16[384,640]{1,0:T(8,128)(2,1)S(1)}) custom-call(bf16[384,1920]{1,0:T(8,128)(2,1)} %bitcast.17.acts_ref, bf16[384,1280]{1,0:T(8,128)(2,1)S(1)} %all_gather.6.both_ref, bf16[640,896]{1,0:T(8,128)(2,1)S(1)} %bitcast.64, f32[1,896]{1,0:T(1,128)S(1)} %broadcast_in_dim.15.tilt_ref, ...), custom_call_target="tpu_custom_call" | custom-call | tf_op jit(solution)/shard_map/pallas_call | solution.py:67
  113.6 3.3 %shard_map.86 = (bf16[4,1120,128]{2,1,0:T(8,128)(2,1)S(1)}, bf16[4,1120,128]{2,1,0:T(8,128)(2,1)S(1)}) custom-call(s32[1]{0:T(128)} %bitcast.19.core_ref, bf16[384,1920]{1,0:T(8,128)(2,1)} %bitcast.17.acts_ref, bf16[384,1280]{1,0:T(8,128)(2,1)S(1)} %all_gather.6.both_ref, bf16[384,640]{1,0:T(8,128)(2,1)S(1)} %get-tuple-element.15.z_ref), custom_call_target="tpu_custom_call" | custom-call | tf_op jit(solution)/shard_map/pallas_call | solution.py:67
  116.9 21.9 %collective-permute-start.1 = (bf16[4,1120,128]{2,1,0:T(8,128)(2,1)S(1)}, bf16[4,1120,128]{2,1,0:T(8,128)(2,1)}, u32[]{:S(2)}, u32[]{:S(2)}) collective-permute-start(bf16[4,1120,128]{2,1,0:T(8,128)(2,1)S(1)} %get-tuple-element.17), channel_id=1, source_target_pairs={{0,8},{8,0},{1,9},{9,1},{2,10},{10,2},{3,11},{11,3},{4,12},{12,4},... | collective-permute-start | bytes 3440648 | tf_op jit(solution)/shard_map/ppermute | solution.py:49
  138.7 17.0 %all-to-all-start.3 = ((bf16[8,56,768]{2,1,0:T(8,128)(2,1)}), bf16[8,56,768]{2,1,0:T(8,128)(2,1)}, u32[]{:S(2)}, u32[]{:S(2)}) async-start(bf16[8,56,768]{2,1,0:T(8,128)(2,1)} %get-tuple-element.14), calls=%async_computation.3 | async-start | bytes 1376256 | tf_op jit(solution)/shard_map/all_to_all | solution.py:21
  155.7 1.2 convert_reduce_fusion.6
  157.1 1.6 add_convert_fusion
  158.7 9.8 %collective-permute-start.4 = (bf16[1120,128]{1,0:T(8,128)(2,1)S(1)}, bf16[1120,128]{1,0:T(8,128)(2,1)S(1)}, u32[]{:S(2)}, u32[]{:S(2)}) collective-permute-start(bf16[1120,128]{1,0:T(8,128)(2,1)S(1)} %get-tuple-element.36), channel_id=1, source_target_pairs={{0,48},{16,32},{32,16},{48,0},{1,49},{17,33},{33,17},{49,1},{2,50}... | collective-permute-start | bytes 860168 | tf_op jit(solution)/shard_map/ppermute | solution.py:49
  168.5 1.9 collective-permute-start.3
  170.5 2.2 %collective-permute-start.2 = (bf16[1120,128]{1,0:T(8,128)(2,1)S(1)}, bf16[1120,128]{1,0:T(8,128)(2,1)S(1)}, u32[]{:S(2)}, u32[]{:S(2)}) collective-permute-start(bf16[1120,128]{1,0:T(8,128)(2,1)S(1)} %get-tuple-element.38), channel_id=1, source_target_pairs={{0,16},{16,0},{32,48},{48,32},{1,17},{17,1},{33,49},{49,33},{2,18}... | collective-permute-start | bytes 860168 | tf_op jit(solution)/shard_map/ppermute | solution.py:49
  172.7 4.7 %all-to-all-done.3 = bf16[8,56,768]{2,1,0:T(8,128)(2,1)} async-done(((bf16[8,56,768]{2,1,0:T(8,128)(2,1)}), bf16[8,56,768]{2,1,0:T(8,128)(2,1)}, u32[]{:S(2)}, u32[]{:S(2)}) %all-to-all-start.3) | async-done | bytes 688160 | tf_op jit(solution)/shard_map/all_to_all | solution.py:21
  177.3 0.9 convert_reduce_fusion.10
  178.2 8.0 %collective-permute-start.5 = (f32[640]{0:T(1024)S(1)}, f32[640]{0:T(1024)S(1)}, u32[]{:S(2)}, u32[]{:S(2)}) collective-permute-start(f32[640]{0:T(1024)S(1)} %convert_reduce_fusion.10), channel_id=1, source_target_pairs={{0,16},{16,0},{32,48},{48,32},{1,17},{17,1},{33,49},{49,33},{2,18}... | collective-permute-start | bytes 7688 | tf_op jit(solution)/shard_map/ppermute | solution.py:49
  186.3 0.9 convert_reduce_fusion.5
  187.2 0.2 slice_reduce_fusion.1
  187.4 3.9 %collective-permute-start.6 = (f32[640]{0:T(1024)S(1)}, f32[640]{0:T(1024)S(1)}, u32[]{:S(2)}, u32[]{:S(2)}) collective-permute-start(f32[640]{0:T(1024)S(1)} %add.140), channel_id=1, source_target_pairs={{0,32},{16,48},{32,0},{48,16},{1,33},{17,49},{33,1},{49,17},{2,34}... | collective-permute-start | bytes 7688 | tf_op jit(solution)/shard_map/ppermute | solution.py:49
  191.3 1.1 convert_reduce_fusion.3
  192.4 0.8 collective-permute-done.6
  193.2 3.8 %collective-permute-start.7 = (f32[640]{0:T(1024)S(1)}, f32[640]{0:T(1024)S(1)}, u32[]{:S(2)}, u32[]{:S(2)}) collective-permute-start(f32[640]{0:T(1024)S(1)} %add.141), channel_id=1, source_target_pairs={{0,8},{8,0},{1,9},{9,1},{2,10},{10,2},{3,11},{11,3},{4,12},{12,4},... | collective-permute-start | bytes 7688 | tf_op jit(solution)/shard_map/ppermute | solution.py:49
  196.9 0.7 multiply_convert_fusion.1
  197.7 0.6 add.142
  198.3 0.8 shard_map.87
  (60 shorter events, 1.6 us)
Async XLA Ops:
  7.2 8.0 %copy-start.3 = (f32[640]{0:T(1024)S(1)}, f32[640]{0:T(1024)}, u32[]{:S(2)}) copy-start(f32[640]{0:T(1024)} %param.6) | copy-start | bytes 7684
  7.2 8.0 %copy-start.2 = (bf16[48,640]{1,0:T(8,128)(2,1)S(1)}, bf16[48,640]{1,0:T(8,128)(2,1)}, u32[]{:S(2)}) copy-start(bf16[48,640]{1,0:T(8,128)(2,1)} %param.5) | copy-start | bytes 184324
  7.2 8.0 %copy-start.4 = (bf16[48,640]{1,0:T(8,128)(2,1)S(1)}, bf16[48,640]{1,0:T(8,128)(2,1)}, u32[]{:S(2)}) copy-start(bf16[48,640]{1,0:T(8,128)(2,1)} %param.9) | copy-start | bytes 184324
  7.2 46.4 %all-gather.2.cloned.1.call-start = ((), (), s32[]{:S(2)}) async-start(), calls=%async_computation.4 | async-start | bytes 1290240 | tf_op jit(solution)/shard_map/all_gather | solution.py:173
  9.7 33.7 %all-to-all-start = ((bf16[4,80,896]{2,1,0:T(8,128)(2,1)}), bf16[4,80,896]{2,1,0:T(8,128)(2,1)S(1)}, u32[]{:S(2)}, u32[]{:S(2)}) async-start(bf16[4,80,896]{2,1,0:T(8,128)(2,1)} %broadcast_in_dim.12), calls=%async_computation | async-start | bytes 1146880 | tf_op jit(solution)/shard_map/all_to_all | solution.py:21
  43.4 9.1 %collective-permute-start = (bf16[4,80,896]{2,1,0:T(8,128)(2,1)S(1)}, bf16[4,80,896]{2,1,0:T(8,128)(2,1)S(1)}, u32[]{:S(2)}, u32[]{:S(2)}) collective-permute-start(bf16[4,80,896]{2,1,0:T(8,128)(2,1)S(1)} %all-to-all-done), channel_id=1, source_target_pairs={{0,8},{8,0},{1,9},{9,1},{2,10},{10,2},{3,11},{11,3},{4,12},{12,4},... | collective-permute-start | bytes 1720328 | tf_op jit(solution)/shard_map/ppermute | solution.py:49
  53.6 1.3 copy-start
  86.0 1.1 copy-start.1
  91.2 19.3 %all-to-all-start.2 = ((bf16[8,48,1920]{2,1,0:T(8,128)(2,1)}), bf16[8,48,1920]{2,1,0:T(8,128)(2,1)}, u32[]{:S(2)}, u32[]{:S(2)}) async-start(bf16[8,48,1920]{2,1,0:T(8,128)(2,1)} %broadcast_in_dim.14), calls=%async_computation.2 | async-start | bytes 2949120 | tf_op jit(solution)/shard_map/all_to_all | solution.py:21
  116.9 40.2 %collective-permute-start.1 = (bf16[4,1120,128]{2,1,0:T(8,128)(2,1)S(1)}, bf16[4,1120,128]{2,1,0:T(8,128)(2,1)}, u32[]{:S(2)}, u32[]{:S(2)}) collective-permute-start(bf16[4,1120,128]{2,1,0:T(8,128)(2,1)S(1)} %get-tuple-element.17), channel_id=1, source_target_pairs={{0,8},{8,0},{1,9},{9,1},{2,10},{10,2},{3,11},{11,3},{4,12},{12,4},... | collective-permute-start | bytes 3440648 | tf_op jit(solution)/shard_map/ppermute | solution.py:49
  138.7 38.6 %all-to-all-start.3 = ((bf16[8,56,768]{2,1,0:T(8,128)(2,1)}), bf16[8,56,768]{2,1,0:T(8,128)(2,1)}, u32[]{:S(2)}, u32[]{:S(2)}) async-start(bf16[8,56,768]{2,1,0:T(8,128)(2,1)} %get-tuple-element.14), calls=%async_computation.3 | async-start | bytes 1376256 | tf_op jit(solution)/shard_map/all_to_all | solution.py:21
  158.7 39.6 %collective-permute-start.4 = (bf16[1120,128]{1,0:T(8,128)(2,1)S(1)}, bf16[1120,128]{1,0:T(8,128)(2,1)S(1)}, u32[]{:S(2)}, u32[]{:S(2)}) collective-permute-start(bf16[1120,128]{1,0:T(8,128)(2,1)S(1)} %get-tuple-element.36), channel_id=1, source_target_pairs={{0,48},{16,32},{32,16},{48,0},{1,49},{17,33},{33,17},{49,1},{2,50}... | collective-permute-start | bytes 860168 | tf_op jit(solution)/shard_map/ppermute | solution.py:49
  168.5 29.8 %collective-permute-start.3 = (bf16[1120,128]{1,0:T(8,128)(2,1)S(1)}, bf16[1120,128]{1,0:T(8,128)(2,1)S(1)}, u32[]{:S(2)}, u32[]{:S(2)}) collective-permute-start(bf16[1120,128]{1,0:T(8,128)(2,1)S(1)} %get-tuple-element.37), channel_id=1, source_target_pairs={{0,32},{16,48},{32,0},{48,16},{1,33},{17,49},{33,1},{49,17},{2,34}... | collective-permute-start | bytes 860168 | tf_op jit(solution)/shard_map/ppermute | solution.py:49
  170.5 27.9 %collective-permute-start.2 = (bf16[1120,128]{1,0:T(8,128)(2,1)S(1)}, bf16[1120,128]{1,0:T(8,128)(2,1)S(1)}, u32[]{:S(2)}, u32[]{:S(2)}) collective-permute-start(bf16[1120,128]{1,0:T(8,128)(2,1)S(1)} %get-tuple-element.38), channel_id=1, source_target_pairs={{0,16},{16,0},{32,48},{48,32},{1,17},{17,1},{33,49},{49,33},{2,18}... | collective-permute-start | bytes 860168 | tf_op jit(solution)/shard_map/ppermute | solution.py:49
  178.2 9.2 %collective-permute-start.5 = (f32[640]{0:T(1024)S(1)}, f32[640]{0:T(1024)S(1)}, u32[]{:S(2)}, u32[]{:S(2)}) collective-permute-start(f32[640]{0:T(1024)S(1)} %convert_reduce_fusion.10), channel_id=1, source_target_pairs={{0,16},{16,0},{32,48},{48,32},{1,17},{17,1},{33,49},{49,33},{2,18}... | collective-permute-start | bytes 7688 | tf_op jit(solution)/shard_map/ppermute | solution.py:49
  187.4 5.7 %collective-permute-start.6 = (f32[640]{0:T(1024)S(1)}, f32[640]{0:T(1024)S(1)}, u32[]{:S(2)}, u32[]{:S(2)}) collective-permute-start(f32[640]{0:T(1024)S(1)} %add.140), channel_id=1, source_target_pairs={{0,32},{16,48},{32,0},{48,16},{1,33},{17,49},{33,1},{49,17},{2,34}... | collective-permute-start | bytes 7688 | tf_op jit(solution)/shard_map/ppermute | solution.py:49
  193.2 4.6 %collective-permute-start.7 = (f32[640]{0:T(1024)S(1)}, f32[640]{0:T(1024)S(1)}, u32[]{:S(2)}, u32[]{:S(2)}) collective-permute-start(f32[640]{0:T(1024)S(1)} %add.141), channel_id=1, source_target_pairs={{0,8},{8,0},{1,9},{9,1},{2,10},{10,2},{3,11},{11,3},{4,12},{12,4},... | collective-permute-start | bytes 7688 | tf_op jit(solution)/shard_map/ppermute | solution.py:49
Sparse Core Ops, SparseCore 0:
  10.1 43.4 all-gather.1

commit v7 on v6

--- a/solution.py
+++ b/solution.py
@@ -94,28 +94,39 @@
     return out
 
 
-def tokens_kernel(acts_ref, both_ref, up_ref, tilt_ref, gain_ref, tail_ref, z_ref):
+def halves(index, own_ref, peer_ref):
+    tall = own_ref.shape[0]
+    for ref, which in ((own_ref, index), (peer_ref, 1 - index)):
+        yield ref, which, pl.ds(pl.multiple_of(which * tall, 16), tall)
+
+
+def tokens_kernel(
+    place_ref, own_ref, peer_ref, both_ref, up_ref, tilt_ref, gain_ref, tail_ref, z_ref, stats_ref
+):
     n, high, _ = tail_ref.shape
     local, hid = up_ref.shape
-    tall = acts_ref.shape[0]
-    rows = tall // n
-    grad = acts_ref[:, hid : 2 * hid]
-    marks = acts_ref[:, 2 * hid :].astype(F32)
-    lane = lax.broadcasted_iota(jnp.int32, marks.shape, 1)
-
-    def taken(index):
-        mine = (lane >= 3 * index) & (lane < 3 * index + 3)
-        return jnp.sum(jnp.where(mine, marks, 0.0), axis=1, keepdims=True)
-
-    cross, mean, inv = (taken(i) for i in range(3))
-    normed = (both_ref[:, :local].astype(F32) - mean) * inv
-    z_ref[...] = (normed * gain_ref[...]).astype(BF)
-    d_z = dot(grad, up_ref[...], (1, 1))
-    level = jnp.sum(grad.astype(F32) * tilt_ref[...], axis=1, keepdims=True)
-    tail_ref[:, :rows, :local] = d_z.astype(BF).reshape(n, rows, local)
-    sums = lane_pieces((level, cross), lane).astype(BF)
-    tail_ref[:, :rows, local:] = sums.reshape(n, rows, LANES)
-    rest = jnp.sum(d_z * normed, axis=0, keepdims=True)
+    rows = both_ref.shape[0] // n
+    rest = 0.0
+    for ref, which, span in halves(place_ref[1], own_ref, peer_ref):
+        grad = ref[:, hid : 2 * hid]
+        marks = ref[:, 2 * hid :].astype(F32)
+        lane = lax.broadcasted_iota(jnp.int32, marks.shape, 1)
+
+        def taken(index):
+            mine = (lane >= 3 * index) & (lane < 3 * index + 3)
+            return jnp.sum(jnp.where(mine, marks, 0.0), axis=1, keepdims=True)
+
+        cross, mean, inv = (taken(i) for i in range(3))
+        stats_ref[span, :] = jnp.where(lane == 0, mean, inv)
+        normed = (both_ref[span, :local].astype(F32) - mean) * inv
+        z_ref[span, :] = (normed * gain_ref[...]).astype(BF)
+        d_z = dot(grad, up_ref[...], (1, 1))
+        level = jnp.sum(grad.astype(F32) * tilt_ref[...], axis=1, keepdims=True)
+        blocks = pl.ds(which * (n // 2), n // 2)
+        tail_ref[blocks, :rows, :local] = d_z.astype(BF).reshape(n // 2, rows, local)
+        sums = lane_pieces((level, cross), lane).astype(BF)
+        tail_ref[blocks, :rows, local:] = sums.reshape(n // 2, rows, LANES)
+        rest = rest + jnp.sum(d_z * normed, axis=0, keepdims=True)
     row = lax.broadcasted_iota(jnp.int32, (high - rows, local), 0)
     gains = jnp.zeros(row.shape, F32)
     for j in range(3):
@@ -128,11 +139,17 @@
         tail_ref[i, rows:, local:] = jnp.zeros((high - rows, LANES), BF)
 
 
-def grads_kernel(core_ref, acts_ref, both_ref, z_ref, keep_ref, give_ref, down_ref, up_ref):
+def grads_kernel(
+    place_ref, own_ref, peer_ref, both_ref, z_ref, keep_ref, give_ref, down_ref, up_ref
+):
     hid, local = down_ref.shape
-    down_ref[...] = dot(acts_ref[:, :hid], both_ref[:, local:], (0, 0)).astype(BF)
-    up_ref[...] = dot(z_ref[...], acts_ref[:, hid : 2 * hid], (0, 0)).astype(BF)
-    core = core_ref[0]
+    down, up = 0.0, 0.0
+    for ref, _, span in halves(place_ref[1], own_ref, peer_ref):
+        down = down + dot(ref[:, :hid], both_ref[span, local:], (0, 0))
+        up = up + dot(z_ref[span, :], ref[:, hid : 2 * hid], (0, 0))
+    down_ref[...] = down.astype(BF)
+    up_ref[...] = up.astype(BF)
+    core = place_ref[0]
     n = keep_ref.shape[0]
     for ref, which in ((keep_ref, core), (give_ref, 1 - core)):
         for j in range(n):
@@ -219,16 +236,21 @@
     marks = columns(cross, mean, inv)
     marks = jnp.pad(marks, ((0, 0), (0, LANES - marks.shape[1])))
     acts = jnp.concatenate([act_f.astype(BF), d_hidden, marks], axis=1)
-    acts = spread(acts, GZ).reshape(all_rows, -1)
-    _, mean, inv = (column(acts[:, 2 * hid :], i) for i in range(3))
-
-    tail, z = local_call(
+    peer = swap(acts, "yh", 1)
+    own = spread(acts, "xx")
+    own, peer = lax.optimization_barrier((own, peer))
+    own, peer = (v.reshape(all_rows // 2, -1) for v in (own, spread(peer, "xx")))
+
+    place = jnp.stack([lax.axis_index("co"), lax.axis_index("yh")])
+    tail, z, stats = local_call(
         tokens_kernel,
         (
             jax.ShapeDtypeStruct((n_gx, rows + 8, local + LANES), BF),
             jax.ShapeDtypeStruct((all_rows, local), BF),
+            jax.ShapeDtypeStruct((all_rows, LANES), F32),
         ),
-        *(acts, both, up_full, jnp.sum(tilts, axis=0)[None], gain[None]),
+        *(place, own, peer, both, up_full, jnp.sum(tilts, axis=0)[None], gain[None]),
+        scalar=True,
     )
     tail = exchange(tail, "gx")
 
@@ -236,17 +258,17 @@
     keep, give = local_call(
         grads_kernel,
         (jax.ShapeDtypeStruct((n_yl, packed, LANES), BF),) * 2,
-        *(lax.axis_index("co")[None], acts, both, z),
+        *(place, own, peer, both, z),
         scratch=(pltpu.VMEM((hid, local), BF), pltpu.VMEM((local, hid), BF)),
         scalar=True,
     )
     grads = (keep.astype(F32) + other_core(give).astype(F32)).astype(BF)
-    place = lax.axis_index("yl")
+    turn = lax.axis_index("yl")
 
     def part(index):
         return lax.dynamic_index_in_dim(grads, index, keepdims=False)
 
-    grads = [part(place)] + [swap(part(place ^ k), "yl", k) for k in range(1, n_yl)]
+    grads = [part(turn)] + [swap(part(turn ^ k), "yl", k) for k in range(1, n_yl)]
     d_z = summed(tail[:, :rows, :local])
     marks = summed(tail[:, :rows, local:])
     scaled_sum, cross_sum = (column(marks, i)[:, None] / width for i in range(2))
@@ -265,11 +287,9 @@
 
     first = lax.axis_index("gx") * rows
 
-    def own(values):
-        return lax.dynamic_slice(values, (first,), (rows,))[:, None]
-
-    own_inv = own(inv)
-    own_normed = (x_in.astype(F32) - own(mean)) * own_inv
+    stats = lax.dynamic_slice(stats, (first, 0), (rows, 2))
+    own_inv = stats[:, 1:]
+    own_normed = (x_in.astype(F32) - stats[:, :1]) * own_inv
     d_x = own_inv * (d_z * gain - scaled_sum - own_normed * cross_sum)
     return (d_x.astype(BF), d_w_up, d_w_down, d_gain)
 

time: 207 us -> 207 us (level)
  starting transfers between devices: 85.7 us -> 58 us
  waiting for transfers between devices: 21.2 us -> 38.9 us
  blocking collectives: 58 us -> 70.6 us
  other arithmetic: 11.4 us -> 7.39 us
    ppermute x8 -> x9, starting transfers between devices: 59 us -> 37.5 us  [swap(): lax.ppermute(value, axis, [(i, i ^ bits) for i in range(lax.axis_size(axi...]
    all_to_all x1, blocking collectives: 29.8 us -> 42.9 us  [exchange(): return lax.all_to_all(blocks, axis, 0, 0, tiled=True)]
    ppermute x8 -> x9, waiting for transfers between devices: 1.66 us -> 14.2 us  [swap(): lax.ppermute(value, axis, [(i, i ^ bits) for i in range(lax.axis_size(axi...]
    all_to_all x3 -> x4, starting transfers between devices: 26.7 us -> 20.5 us  [exchange(): return lax.all_to_all(blocks, axis, 0, 0, tiled=True)]
    all_gather x1, waiting for transfers between devices: 0.21 us -> 5.67 us  [body(): down_full = lax.all_gather(w_down, GY, axis=0, tiled=True)]
    all_to_all x3 -> x4, waiting for transfers between devices: 18.7 us -> 18.4 us  [exchange(): return lax.all_to_all(blocks, axis, 0, 0, tiled=True)]
  transfers between devices with their start and end apart: 12 -> 14, of which waited for: 6 -> 8; matrix products, arithmetic and copies ran while one was open for 6% -> 3% of each run, Pallas kernels for 0% -> 0%
where the time goes in v7:
time: 207 us; the launch traced here: 206 us
  blocking collectives  70.6 us (34%)
  starting transfers between devices  58 us (28%)
  waiting for transfers between devices  38.9 us (19%)
  between operations  14.4 us (7%)
  Pallas kernels  9.24 us (4%)
  other arithmetic  7.39 us (4%)
  local copies, waits for them, and re-layouts  7.31 us (4%)
    all_to_all x1, blocking collectives, exchange(): return lax.all_to_all(blocks, axis, 0, 0, tiled=True)  42.9 us
    ppermute x9, starting transfers between devices, swap(): lax.ppermute(value, axis, [(i, i ^ bits) for i in range(lax.axis_size(axi...  37.5 us
    all_gather x1, blocking collectives, body(): lax.all_gather(jnp.concatenate([x_in, d_out], axis=1), 'gx', axis=0, tile...  27.6 us
    all_to_all x4, starting transfers between devices, exchange(): return lax.all_to_all(blocks, axis, 0, 0, tiled=True)  20.5 us
    all_to_all x4, waiting for transfers between devices, exchange(): return lax.all_to_all(blocks, axis, 0, 0, tiled=True)  18.4 us
    ppermute x9, waiting for transfers between devices, swap(): lax.ppermute(value, axis, [(i, i ^ bits) for i in range(lax.axis_size(axi...  14.2 us
    pallas_call x4, Pallas kernels, local_call(): pl.pallas_call(kernel, out_shape=out, in_specs=specs, out_specs=jax.tree....  9.24 us
    all_gather x1, waiting for transfers between devices, body(): down_full = lax.all_gather(w_down, GY, axis=0, tiled=True)  5.67 us
  transfers between devices with their start and end apart: 14, of which 8 were waited for; matrix products, arithmetic and copies ran while one was open for 3% of the time, Pallas kernels for 0%

profile of v7, /device:TPU:1, one launch (start us, length us, event | category | flops | bytes accessed | tf_op | source)
XLA Modules:
  0.0 206.1 jit_solution(7669669052005181661)
XLA Ops:
  7.2 1.8 broadcast_in_dim.12
  9.0 5.4 %all-to-all-start = ((bf16[4,80,896]{2,1,0:T(8,128)(2,1)}), bf16[4,80,896]{2,1,0:T(8,128)(2,1)S(1)}, u32[]{:S(2)}, u32[]{:S(2)}) async-start(bf16[4,80,896]{2,1,0:T(8,128)(2,1)} %broadcast_in_dim.12), calls=%async_computation | async-start | bytes 1146880 | tf_op jit(solution)/shard_map/all_to_all | solution.py:21
  14.4 0.7 all-gather.2.cloned.1.call-update
  15.3 27.6 %all_gather.6.both_ref = bf16[384,1280]{1,0:T(8,128)(2,1)S(1)} all-gather(bf16[48,1280]{1,0:T(8,128)(2,1)S(1)} %pad_maximum_fusion.1), channel_id=1, replica_groups=mesh['gx'=8,'yl'=4,'co'=2,'yh'=2,'xx'=4] {'gx'}, dimensions={0}, use_global_device_ids=true | all-gather | bytes 1105920 | tf_op jit(solution)/shard_map/all_gather | solution.py:192
  42.9 8.3 %collective-permute-start = (bf16[4,80,896]{2,1,0:T(8,128)(2,1)S(1)}, bf16[4,80,896]{2,1,0:T(8,128)(2,1)S(1)}, u32[]{:S(2)}, u32[]{:S(2)}) collective-permute-start(bf16[4,80,896]{2,1,0:T(8,128)(2,1)S(1)} %all-to-all-done), channel_id=1, source_target_pairs={{0,8},{8,0},{1,9},{9,1},{2,10},{10,2},{3,11},{11,3},{4,12},{12,4},... | collective-permute-start | bytes 1720328 | tf_op jit(solution)/shard_map/ppermute | solution.py:49
  51.2 0.1 convert_reduce_fusion.2
  51.3 0.3 fusion.3
  51.7 0.2 copy.24
  52.0 0.8 collective-permute-done
  52.8 0.1 select_bitcast_fusion.1
  52.9 0.1 pad_maximum_fusion
  53.0 0.3 convolution_reduce_fusion
  53.6 5.7 %all-gather.2.cloned.1.call-done.down_ref = bf16[896,640]{1,0:T(8,128)(2,1)} async-done(((bf16[112,640]{1,0:T(8,128)(2,1)}), bf16[896,640]{1,0:T(8,128)(2,1)}) %all-gather.2.cloned.1.call-update) | async-done | bytes 1146896 | tf_op jit(solution)/shard_map/all_gather | solution.py:190
  59.2 1.3 copy-done
  60.5 1.4 shard_map.84
  61.8 42.9 %all_to_all.25 = bf16[8,48,1920]{2,1,0:T(8,128)(2,1)S(1)} all-to-all(bf16[8,48,1920]{2,1,0:T(8,128)(2,1)S(1)} %shard_map.84), channel_id=1, replica_groups=mesh['gx'=8,'yl'=4,'co'=2,'yh'=2,'xx'=4] {'yh','xx'}, dimensions={0} | all-to-all | bytes 2949120 | tf_op jit(solution)/shard_map/all_to_all | solution.py:21
  104.8 0.2 convert_reduce_fusion.6
  105.1 0.9 copy-done.1
  106.7 1.5 convert_reduce_fusion
  108.2 0.2 multiply_convert_fusion
  108.4 0.2 multiply_reduce_fusion
  108.8 0.9 broadcast_in_dim.14
  109.8 3.5 %all-to-all-start.2 = ((bf16[4,48,1920]{2,1,0:T(8,128)(2,1)}), bf16[4,48,1920]{2,1,0:T(8,128)(2,1)S(1)}, u32[]{:S(2)}, u32[]{:S(2)}) async-start(bf16[4,48,1920]{2,1,0:T(8,128)(2,1)} %broadcast_in_dim.14), calls=%async_computation.2 | async-start | bytes 1474560 | tf_op jit(solution)/shard_map/all_to_all | solution.py:21
  113.3 6.0 %collective-permute-start.1 = (bf16[48,1920]{1,0:T(8,128)(2,1)S(1)}, bf16[48,1920]{1,0:T(8,128)(2,1)S(1)}, u32[]{:S(2)}, u32[]{:S(2)}) collective-permute-start(bf16[48,1920]{1,0:T(8,128)(2,1)S(1)} %fusion.5), channel_id=1, source_target_pairs={{0,4},{4,0},{1,5},{5,1},{2,6},{6,2},{3,7},{7,3},{8,12},{12,8},{9,1... | collective-permute-start | bytes 552968 | tf_op jit(solution)/shard_map/ppermute | solution.py:49
  119.3 6.1 %collective-permute-done.1 = bf16[48,1920]{1,0:T(8,128)(2,1)S(1)} collective-permute-done((bf16[48,1920]{1,0:T(8,128)(2,1)S(1)}, bf16[48,1920]{1,0:T(8,128)(2,1)S(1)}, u32[]{:S(2)}, u32[]{:S(2)}) %collective-permute-start.1) | collective-permute-done | bytes 184352 | tf_op jit(solution)/shard_map/ppermute | solution.py:49
  125.4 0.9 broadcast_in_dim.15
  126.3 4.2 %all-to-all-start.3 = ((bf16[4,48,1920]{2,1,0:T(8,128)(2,1)}), bf16[4,48,1920]{2,1,0:T(8,128)(2,1)}, u32[]{:S(2)}, u32[]{:S(2)}) async-start(bf16[4,48,1920]{2,1,0:T(8,128)(2,1)} %broadcast_in_dim.15), calls=%async_computation.3 | async-start | bytes 1474560 | tf_op jit(solution)/shard_map/all_to_all | solution.py:21
  130.6 0.9 convert_reduce_fusion.7
  131.6 8.0 %all-to-all-done.3 = bf16[4,48,1920]{2,1,0:T(8,128)(2,1)} async-done(((bf16[4,48,1920]{2,1,0:T(8,128)(2,1)}), bf16[4,48,1920]{2,1,0:T(8,128)(2,1)}, u32[]{:S(2)}, u32[]{:S(2)}) %all-to-all-start.3) | async-done | bytes 737312 | tf_op jit(solution)/shard_map/all_to_all | solution.py:21
  139.6 3.0 %shard_map.85 = (bf16[8,56,768]{2,1,0:T(8,128)(2,1)}, bf16[384,640]{1,0:T(8,128)(2,1)S(1)}, f32[384,128]{1,0:T(8,128)S(1)}) custom-call(s32[2]{0:T(128)S(1)} %pad_add_fusion.place_ref, bf16[192,1920]{1,0:T(8,128)(2,1)S(1)} %bitcast.67, bf16[192,1920]{1,0:T(8,128)(2,1)} %bitcast.20.peer_ref, bf16[384,1280]{1,0:T(8,128)(2,1)S(1)} %all_gather.6.both_ref, ...), custom_call_target="tpu_custom_call" | custom-call | tf_op jit(solution)/shard_map/pallas_call | solution.py:67
  142.6 4.1 %shard_map.86 = (bf16[4,1120,128]{2,1,0:T(8,128)(2,1)S(1)}, bf16[4,1120,128]{2,1,0:T(8,128)(2,1)}) custom-call(s32[2]{0:T(128)S(1)} %pad_add_fusion.place_ref, bf16[192,1920]{1,0:T(8,128)(2,1)S(1)} %bitcast.68, bf16[192,1920]{1,0:T(8,128)(2,1)} %bitcast.20.peer_ref, bf16[384,1280]{1,0:T(8,128)(2,1)S(1)} %all_gather.6.both_ref, ...), custom_call_target="tpu_custom_call" | custom-call | tf_op jit(solution)/shard_map/pallas_call | solution.py:67
  146.6 5.6 %collective-permute-start.2 = (bf16[4,1120,128]{2,1,0:T(8,128)(2,1)}, bf16[4,1120,128]{2,1,0:T(8,128)(2,1)}, u32[]{:S(2)}, u32[]{:S(2)}) collective-permute-start(bf16[4,1120,128]{2,1,0:T(8,128)(2,1)} %get-tuple-element.23), channel_id=1, source_target_pairs={{0,8},{8,0},{1,9},{9,1},{2,10},{10,2},{3,11},{11,3},{4,12},{12,4},... | collective-permute-start | bytes 3440648 | tf_op jit(solution)/shard_map/ppermute | solution.py:49
  152.2 7.4 %all-to-all-start.4 = ((bf16[8,56,768]{2,1,0:T(8,128)(2,1)}), bf16[8,56,768]{2,1,0:T(8,128)(2,1)S(1)}, u32[]{:S(2)}, u32[]{:S(2)}) async-start(bf16[8,56,768]{2,1,0:T(8,128)(2,1)} %get-tuple-element.20), calls=%async_computation.4 | async-start | bytes 1376256 | tf_op jit(solution)/shard_map/all_to_all | solution.py:21
  159.7 0.2 dynamic-slice_reduce_fusion.1
  159.9 1.6 add_convert_fusion
  161.5 1.9 collective-permute-start.3
  163.5 5.3 %collective-permute-start.4 = (bf16[1120,128]{1,0:T(8,128)(2,1)S(1)}, bf16[1120,128]{1,0:T(8,128)(2,1)S(1)}, u32[]{:S(2)}, u32[]{:S(2)}) collective-permute-start(bf16[1120,128]{1,0:T(8,128)(2,1)S(1)} %get-tuple-element.43), channel_id=1, source_target_pairs={{0,32},{16,48},{32,0},{48,16},{1,33},{17,49},{33,1},{49,17},{2,34}... | collective-permute-start | bytes 860168 | tf_op jit(solution)/shard_map/ppermute | solution.py:49
  168.7 2.1 %collective-permute-start.5 = (bf16[1120,128]{1,0:T(8,128)(2,1)S(1)}, bf16[1120,128]{1,0:T(8,128)(2,1)S(1)}, u32[]{:S(2)}, u32[]{:S(2)}) collective-permute-start(bf16[1120,128]{1,0:T(8,128)(2,1)S(1)} %get-tuple-element.42), channel_id=1, source_target_pairs={{0,48},{16,32},{32,16},{48,0},{1,49},{17,33},{33,17},{49,1},{2,50}... | collective-permute-start | bytes 860168 | tf_op jit(solution)/shard_map/ppermute | solution.py:49
  170.8 10.4 %all-to-all-done.4 = bf16[8,56,768]{2,1,0:T(8,128)(2,1)S(1)} async-done(((bf16[8,56,768]{2,1,0:T(8,128)(2,1)}), bf16[8,56,768]{2,1,0:T(8,128)(2,1)S(1)}, u32[]{:S(2)}, u32[]{:S(2)}) %all-to-all-start.4) | async-done | bytes 688160 | tf_op jit(solution)/shard_map/all_to_all | solution.py:21
  181.2 0.2 slice_reduce_fusion.1
  181.4 1.9 collective-permute-start.6
  183.4 3.1 %collective-permute-done.6 = f32[640]{0:T(1024)S(1)} collective-permute-done((f32[640]{0:T(1024)S(1)}, f32[640]{0:T(1024)S(1)}, u32[]{:S(2)}, u32[]{:S(2)}) %collective-permute-start.6) | collective-permute-done | bytes 2592 | tf_op jit(solution)/shard_map/ppermute | solution.py:49
  186.5 3.1 %collective-permute-start.7 = (f32[640]{0:T(1024)S(1)}, f32[640]{0:T(1024)S(1)}, u32[]{:S(2)}, u32[]{:S(2)}) collective-permute-start(f32[640]{0:T(1024)S(1)} %add.139), channel_id=1, source_target_pairs={{0,32},{16,48},{32,0},{48,16},{1,33},{17,49},{33,1},{49,17},{2,34}... | collective-permute-start | bytes 7688 | tf_op jit(solution)/shard_map/ppermute | solution.py:49
  189.7 4.1 %collective-permute-done.7 = f32[640]{0:T(1024)S(1)} collective-permute-done((f32[640]{0:T(1024)S(1)}, f32[640]{0:T(1024)S(1)}, u32[]{:S(2)}, u32[]{:S(2)}) %collective-permute-start.7) | collective-permute-done | bytes 2592 | tf_op jit(solution)/shard_map/ppermute | solution.py:49
  193.7 3.3 %collective-permute-start.8 = (f32[640]{0:T(1024)S(1)}, f32[640]{0:T(1024)S(1)}, u32[]{:S(2)}, u32[]{:S(2)}) collective-permute-start(f32[640]{0:T(1024)S(1)} %add.140), channel_id=1, source_target_pairs={{0,8},{8,0},{1,9},{9,1},{2,10},{10,2},{3,11},{11,3},{4,12},{12,4},... | collective-permute-start | bytes 7688 | tf_op jit(solution)/shard_map/ppermute | solution.py:49
  197.1 0.7 multiply_convert_fusion.1
  197.9 0.6 add.141
  198.5 0.8 shard_map.87
  (64 shorter events, 1.8 us)
Async XLA Ops:
  7.2 8.0 %copy-start.3 = (f32[640]{0:T(1024)S(1)}, f32[640]{0:T(1024)}, u32[]{:S(2)}) copy-start(f32[640]{0:T(1024)} %param.6) | copy-start | bytes 7684
  7.2 8.0 %copy-start.2 = (bf16[48,640]{1,0:T(8,128)(2,1)S(1)}, bf16[48,640]{1,0:T(8,128)(2,1)}, u32[]{:S(2)}) copy-start(bf16[48,640]{1,0:T(8,128)(2,1)} %param.5) | copy-start | bytes 184324
  7.2 8.0 %copy-start.4 = (bf16[48,640]{1,0:T(8,128)(2,1)S(1)}, bf16[48,640]{1,0:T(8,128)(2,1)}, u32[]{:S(2)}) copy-start(bf16[48,640]{1,0:T(8,128)(2,1)} %param.9) | copy-start | bytes 184324
  9.0 33.9 %all-to-all-start = ((bf16[4,80,896]{2,1,0:T(8,128)(2,1)}), bf16[4,80,896]{2,1,0:T(8,128)(2,1)S(1)}, u32[]{:S(2)}, u32[]{:S(2)}) async-start(bf16[4,80,896]{2,1,0:T(8,128)(2,1)} %broadcast_in_dim.12), calls=%async_computation | async-start | bytes 1146880 | tf_op jit(solution)/shard_map/all_to_all | solution.py:21
  14.4 44.8 %all-gather.2.cloned.1.call-start = ((), (), s32[]{:S(2)}) async-start(), calls=%async_computation.5 | async-start | bytes 1290240 | tf_op jit(solution)/shard_map/all_gather | solution.py:190
  42.9 9.9 %collective-permute-start = (bf16[4,80,896]{2,1,0:T(8,128)(2,1)S(1)}, bf16[4,80,896]{2,1,0:T(8,128)(2,1)S(1)}, u32[]{:S(2)}, u32[]{:S(2)}) collective-permute-start(bf16[4,80,896]{2,1,0:T(8,128)(2,1)S(1)} %all-to-all-done), channel_id=1, source_target_pairs={{0,8},{8,0},{1,9},{9,1},{2,10},{10,2},{3,11},{11,3},{4,12},{12,4},... | collective-permute-start | bytes 1720328 | tf_op jit(solution)/shard_map/ppermute | solution.py:49
  59.2 1.3 copy-start
  104.8 1.1 copy-start.1
  109.8 15.6 %all-to-all-start.2 = ((bf16[4,48,1920]{2,1,0:T(8,128)(2,1)}), bf16[4,48,1920]{2,1,0:T(8,128)(2,1)S(1)}, u32[]{:S(2)}, u32[]{:S(2)}) async-start(bf16[4,48,1920]{2,1,0:T(8,128)(2,1)} %broadcast_in_dim.14), calls=%async_computation.2 | async-start | bytes 1474560 | tf_op jit(solution)/shard_map/all_to_all | solution.py:21
  113.3 12.1 %collective-permute-start.1 = (bf16[48,1920]{1,0:T(8,128)(2,1)S(1)}, bf16[48,1920]{1,0:T(8,128)(2,1)S(1)}, u32[]{:S(2)}, u32[]{:S(2)}) collective-permute-start(bf16[48,1920]{1,0:T(8,128)(2,1)S(1)} %fusion.5), channel_id=1, source_target_pairs={{0,4},{4,0},{1,5},{5,1},{2,6},{6,2},{3,7},{7,3},{8,12},{12,8},{9,1... | collective-permute-start | bytes 552968 | tf_op jit(solution)/shard_map/ppermute | solution.py:49
  126.3 13.3 %all-to-all-start.3 = ((bf16[4,48,1920]{2,1,0:T(8,128)(2,1)}), bf16[4,48,1920]{2,1,0:T(8,128)(2,1)}, u32[]{:S(2)}, u32[]{:S(2)}) async-start(bf16[4,48,1920]{2,1,0:T(8,128)(2,1)} %broadcast_in_dim.15), calls=%async_computation.3 | async-start | bytes 1474560 | tf_op jit(solution)/shard_map/all_to_all | solution.py:21
  146.6 13.2 %collective-permute-start.2 = (bf16[4,1120,128]{2,1,0:T(8,128)(2,1)}, bf16[4,1120,128]{2,1,0:T(8,128)(2,1)}, u32[]{:S(2)}, u32[]{:S(2)}) collective-permute-start(bf16[4,1120,128]{2,1,0:T(8,128)(2,1)} %get-tuple-element.23), channel_id=1, source_target_pairs={{0,8},{8,0},{1,9},{9,1},{2,10},{10,2},{3,11},{11,3},{4,12},{12,4},... | collective-permute-start | bytes 3440648 | tf_op jit(solution)/shard_map/ppermute | solution.py:49
  152.2 28.9 %all-to-all-start.4 = ((bf16[8,56,768]{2,1,0:T(8,128)(2,1)}), bf16[8,56,768]{2,1,0:T(8,128)(2,1)S(1)}, u32[]{:S(2)}, u32[]{:S(2)}) async-start(bf16[8,56,768]{2,1,0:T(8,128)(2,1)} %get-tuple-element.20), calls=%async_computation.4 | async-start | bytes 1376256 | tf_op jit(solution)/shard_map/all_to_all | solution.py:21
  161.5 36.9 %collective-permute-start.3 = (bf16[1120,128]{1,0:T(8,128)(2,1)S(1)}, bf16[1120,128]{1,0:T(8,128)(2,1)S(1)}, u32[]{:S(2)}, u32[]{:S(2)}) collective-permute-start(bf16[1120,128]{1,0:T(8,128)(2,1)S(1)} %get-tuple-element.44), channel_id=1, source_target_pairs={{0,16},{16,0},{32,48},{48,32},{1,17},{17,1},{33,49},{49,33},{2,18}... | collective-permute-start | bytes 860168 | tf_op jit(solution)/shard_map/ppermute | solution.py:49
  163.5 35.0 %collective-permute-start.4 = (bf16[1120,128]{1,0:T(8,128)(2,1)S(1)}, bf16[1120,128]{1,0:T(8,128)(2,1)S(1)}, u32[]{:S(2)}, u32[]{:S(2)}) collective-permute-start(bf16[1120,128]{1,0:T(8,128)(2,1)S(1)} %get-tuple-element.43), channel_id=1, source_target_pairs={{0,32},{16,48},{32,0},{48,16},{1,33},{17,49},{33,1},{49,17},{2,34}... | collective-permute-start | bytes 860168 | tf_op jit(solution)/shard_map/ppermute | solution.py:49
  168.7 29.7 %collective-permute-start.5 = (bf16[1120,128]{1,0:T(8,128)(2,1)S(1)}, bf16[1120,128]{1,0:T(8,128)(2,1)S(1)}, u32[]{:S(2)}, u32[]{:S(2)}) collective-permute-start(bf16[1120,128]{1,0:T(8,128)(2,1)S(1)} %get-tuple-element.42), channel_id=1, source_target_pairs={{0,48},{16,32},{32,16},{48,0},{1,49},{17,33},{33,17},{49,1},{2,50}... | collective-permute-start | bytes 860168 | tf_op jit(solution)/shard_map/ppermute | solution.py:49
  181.4 5.1 %collective-permute-start.6 = (f32[640]{0:T(1024)S(1)}, f32[640]{0:T(1024)S(1)}, u32[]{:S(2)}, u32[]{:S(2)}) collective-permute-start(f32[640]{0:T(1024)S(1)} %convert_reduce_fusion.8), channel_id=1, source_target_pairs={{0,16},{16,0},{32,48},{48,32},{1,17},{17,1},{33,49},{49,33},{2,18}... | collective-permute-start | bytes 7688 | tf_op jit(solution)/shard_map/ppermute | solution.py:49
  186.5 7.3 %collective-permute-start.7 = (f32[640]{0:T(1024)S(1)}, f32[640]{0:T(1024)S(1)}, u32[]{:S(2)}, u32[]{:S(2)}) collective-permute-start(f32[640]{0:T(1024)S(1)} %add.139), channel_id=1, source_target_pairs={{0,32},{16,48},{32,0},{48,16},{1,33},{17,49},{33,1},{49,17},{2,34}... | collective-permute-start | bytes 7688 | tf_op jit(solution)/shard_map/ppermute | solution.py:49
  193.7 4.1 %collective-permute-start.8 = (f32[640]{0:T(1024)S(1)}, f32[640]{0:T(1024)S(1)}, u32[]{:S(2)}, u32[]{:S(2)}) collective-permute-start(f32[640]{0:T(1024)S(1)} %add.140), channel_id=1, source_target_pairs={{0,8},{8,0},{1,9},{9,1},{2,10},{10,2},{3,11},{11,3},{4,12},{12,4},... | collective-permute-start | bytes 7688 | tf_op jit(solution)/shard_map/ppermute | solution.py:49
Sparse Core Ops, SparseCore 0:
  17.3 41.8 all-gather.1

commit v8 on v7

--- a/solution.py
+++ b/solution.py
@@ -273,8 +273,7 @@
     marks = summed(tail[:, :rows, local:])
     scaled_sum, cross_sum = (column(marks, i)[:, None] / width for i in range(2))
     d_gain = jnp.sum(tail[:, rows : rows + 3, :local].astype(F32), axis=(0, 1))
-    for axis, bits in (("yl", 1), ("yl", 2), ("co", 1)):
-        d_gain = d_gain + swap(d_gain, axis, bits)
+    d_gain = jnp.sum(lax.all_gather(d_gain.reshape(-1, LANES), GY), axis=0).reshape(-1)
 
     d_w_down, d_w_up = local_call(
         merge_kernel,

time: 207 us -> 212 us (1.024)
  blocking collectives: 70.6 us -> 91.1 us
  starting transfers between devices: 58 us -> 49.7 us
  waiting for transfers between devices: 38.9 us -> 31.7 us
    all_gather x0 -> x1, blocking collectives: none -> 20.5 us  [body(): lax.all_gather(d_gain.reshape(-1, LANES), GY)]
    ppermute x9 -> x6, starting transfers between devices: 37.5 us -> 29.1 us  [swap(): lax.ppermute(value, axis, [(i, i ^ bits) for i in range(lax.axis_size(axi...]
    ppermute x9 -> x6, waiting for transfers between devices: 14.2 us -> 6.91 us  [swap(): lax.ppermute(value, axis, [(i, i ^ bits) for i in range(lax.axis_size(axi...]
  transfers between devices with their start and end apart: 14 -> 11, of which waited for: 8 -> 5; matrix products, arithmetic and copies ran while one was open for 3% -> 3% of each run, Pallas kernels for 0% -> 0%
where the time goes in v8:
time: 212 us; the launch traced here: 211 us
  blocking collectives  91.1 us (43%)
  starting transfers between devices  49.7 us (23%)
  waiting for transfers between devices  31.7 us (15%)
  between operations  14.4 us (7%)
  Pallas kernels  9.24 us (4%)
  other arithmetic  7.39 us (3%)
  local copies, waits for them, and re-layouts  7.31 us (3%)
    all_to_all x1, blocking collectives, exchange(): return lax.all_to_all(blocks, axis, 0, 0, tiled=True)  42.9 us
    ppermute x6, starting transfers between devices, swap(): lax.ppermute(value, axis, [(i, i ^ bits) for i in range(lax.axis_size(axi...  29.1 us
    all_gather x1, blocking collectives, body(): lax.all_gather(jnp.concatenate([x_in, d_out], axis=1), 'gx', axis=0, tile...  27.6 us
    all_to_all x4, starting transfers between devices, exchange(): return lax.all_to_all(blocks, axis, 0, 0, tiled=True)  20.5 us
    all_gather x1, blocking collectives, body(): lax.all_gather(d_gain.reshape(-1, LANES), GY)  20.5 us
    all_to_all x4, waiting for transfers between devices, exchange(): return lax.all_to_all(blocks, axis, 0, 0, tiled=True)  18.4 us
    pallas_call x4, Pallas kernels, local_call(): pl.pallas_call(kernel, out_shape=out, in_specs=specs, out_specs=jax.tree....  9.24 us
    ppermute x6, waiting for transfers between devices, swap(): lax.ppermute(value, axis, [(i, i ^ bits) for i in range(lax.axis_size(axi...  6.91 us
  transfers between devices with their start and end apart: 11, of which 5 were waited for; matrix products, arithmetic and copies ran while one was open for 3% of the time, Pallas kernels for 0%

profile of v8, /device:TPU:1, one launch (start us, length us, event | category | flops | bytes accessed | tf_op | source)
XLA Modules:
  0.0 211.0 jit_solution(2454747941397952289)
XLA Ops:
  7.2 1.8 broadcast_in_dim.12
  9.0 5.4 %all-to-all-start = ((bf16[4,80,896]{2,1,0:T(8,128)(2,1)}), bf16[4,80,896]{2,1,0:T(8,128)(2,1)S(1)}, u32[]{:S(2)}, u32[]{:S(2)}) async-start(bf16[4,80,896]{2,1,0:T(8,128)(2,1)} %broadcast_in_dim.12), calls=%async_computation | async-start | bytes 1146880 | tf_op jit(solution)/shard_map/all_to_all | solution.py:21
  14.4 0.7 all-gather.2.cloned.1.call-update
  15.3 27.6 %all_gather.9.both_ref = bf16[384,1280]{1,0:T(8,128)(2,1)S(1)} all-gather(bf16[48,1280]{1,0:T(8,128)(2,1)S(1)} %pad_maximum_fusion.1), channel_id=1, replica_groups=mesh['gx'=8,'yl'=4,'co'=2,'yh'=2,'xx'=4] {'gx'}, dimensions={0}, use_global_device_ids=true | all-gather | bytes 1105920 | tf_op jit(solution)/shard_map/all_gather | solution.py:192
  42.9 8.3 %collective-permute-start = (bf16[4,80,896]{2,1,0:T(8,128)(2,1)S(1)}, bf16[4,80,896]{2,1,0:T(8,128)(2,1)S(1)}, u32[]{:S(2)}, u32[]{:S(2)}) collective-permute-start(bf16[4,80,896]{2,1,0:T(8,128)(2,1)S(1)} %all-to-all-done), channel_id=1, source_target_pairs={{0,8},{8,0},{1,9},{9,1},{2,10},{10,2},{3,11},{11,3},{4,12},{12,4},... | collective-permute-start | bytes 1720328 | tf_op jit(solution)/shard_map/ppermute | solution.py:49
  51.2 0.1 convert_reduce_fusion.2
  51.3 0.3 fusion.3
  51.7 0.2 copy.27
  52.0 0.8 collective-permute-done
  52.8 0.1 select_bitcast_fusion.1
  52.9 0.1 pad_maximum_fusion
  53.0 0.3 convolution_reduce_fusion
  53.3 0.1 reshape.318
  53.5 0.1 pad_maximum_fusion.2.extra_ref
  53.6 5.7 %all-gather.2.cloned.1.call-done.down_ref = bf16[896,640]{1,0:T(8,128)(2,1)} async-done(((bf16[112,640]{1,0:T(8,128)(2,1)}), bf16[896,640]{1,0:T(8,128)(2,1)}) %all-gather.2.cloned.1.call-update) | async-done | bytes 1146896 | tf_op jit(solution)/shard_map/all_gather | solution.py:190
  59.2 1.3 copy-done
  60.5 1.4 shard_map.84
  61.8 42.9 %all_to_all.25 = bf16[8,48,1920]{2,1,0:T(8,128)(2,1)S(1)} all-to-all(bf16[8,48,1920]{2,1,0:T(8,128)(2,1)S(1)} %shard_map.84), channel_id=1, replica_groups=mesh['gx'=8,'yl'=4,'co'=2,'yh'=2,'xx'=4] {'yh','xx'}, dimensions={0} | all-to-all | bytes 2949120 | tf_op jit(solution)/shard_map/all_to_all | solution.py:21
  104.8 0.2 convert_reduce_fusion.6
  105.1 0.9 copy-done.1
  106.7 1.5 convert_reduce_fusion
  108.2 0.2 multiply_convert_fusion
  108.4 0.2 multiply_reduce_fusion
  108.7 0.1 copy.28
  108.8 0.9 broadcast_in_dim.14
  109.8 3.5 %all-to-all-start.2 = ((bf16[4,48,1920]{2,1,0:T(8,128)(2,1)}), bf16[4,48,1920]{2,1,0:T(8,128)(2,1)S(1)}, u32[]{:S(2)}, u32[]{:S(2)}) async-start(bf16[4,48,1920]{2,1,0:T(8,128)(2,1)} %broadcast_in_dim.14), calls=%async_computation.2 | async-start | bytes 1474560 | tf_op jit(solution)/shard_map/all_to_all | solution.py:21
  113.3 6.0 %collective-permute-start.1 = (bf16[48,1920]{1,0:T(8,128)(2,1)S(1)}, bf16[48,1920]{1,0:T(8,128)(2,1)S(1)}, u32[]{:S(2)}, u32[]{:S(2)}) collective-permute-start(bf16[48,1920]{1,0:T(8,128)(2,1)S(1)} %fusion.5), channel_id=1, source_target_pairs={{0,4},{4,0},{1,5},{5,1},{2,6},{6,2},{3,7},{7,3},{8,12},{12,8},{9,1... | collective-permute-start | bytes 552968 | tf_op jit(solution)/shard_map/ppermute | solution.py:49
  119.3 6.1 %collective-permute-done.1 = bf16[48,1920]{1,0:T(8,128)(2,1)S(1)} collective-permute-done((bf16[48,1920]{1,0:T(8,128)(2,1)S(1)}, bf16[48,1920]{1,0:T(8,128)(2,1)S(1)}, u32[]{:S(2)}, u32[]{:S(2)}) %collective-permute-start.1) | collective-permute-done | bytes 184352 | tf_op jit(solution)/shard_map/ppermute | solution.py:49
  125.4 0.9 broadcast_in_dim.15
  126.3 4.2 %all-to-all-start.3 = ((bf16[4,48,1920]{2,1,0:T(8,128)(2,1)}), bf16[4,48,1920]{2,1,0:T(8,128)(2,1)}, u32[]{:S(2)}, u32[]{:S(2)}) async-start(bf16[4,48,1920]{2,1,0:T(8,128)(2,1)} %broadcast_in_dim.15), calls=%async_computation.3 | async-start | bytes 1474560 | tf_op jit(solution)/shard_map/all_to_all | solution.py:21
  130.6 0.9 convert_reduce_fusion.7
  131.6 8.0 %all-to-all-done.3 = bf16[4,48,1920]{2,1,0:T(8,128)(2,1)} async-done(((bf16[4,48,1920]{2,1,0:T(8,128)(2,1)}), bf16[4,48,1920]{2,1,0:T(8,128)(2,1)}, u32[]{:S(2)}, u32[]{:S(2)}) %all-to-all-start.3) | async-done | bytes 737312 | tf_op jit(solution)/shard_map/all_to_all | solution.py:21
  139.6 3.0 %shard_map.85 = (bf16[8,56,768]{2,1,0:T(8,128)(2,1)}, bf16[384,640]{1,0:T(8,128)(2,1)S(1)}, f32[384,128]{1,0:T(8,128)S(1)}) custom-call(s32[2]{0:T(128)S(1)} %pad_add_fusion.place_ref, bf16[192,1920]{1,0:T(8,128)(2,1)S(1)} %bitcast.69, bf16[192,1920]{1,0:T(8,128)(2,1)} %bitcast.20.peer_ref, bf16[384,1280]{1,0:T(8,128)(2,1)S(1)} %all_gather.9.both_ref, ...), custom_call_target="tpu_custom_call" | custom-call | tf_op jit(solution)/shard_map/pallas_call | solution.py:67
  142.6 4.1 %shard_map.86 = (bf16[4,1120,128]{2,1,0:T(8,128)(2,1)S(1)}, bf16[4,1120,128]{2,1,0:T(8,128)(2,1)}) custom-call(s32[2]{0:T(128)S(1)} %pad_add_fusion.place_ref, bf16[192,1920]{1,0:T(8,128)(2,1)S(1)} %bitcast.70, bf16[192,1920]{1,0:T(8,128)(2,1)} %bitcast.20.peer_ref, bf16[384,1280]{1,0:T(8,128)(2,1)S(1)} %all_gather.9.both_ref, ...), custom_call_target="tpu_custom_call" | custom-call | tf_op jit(solution)/shard_map/pallas_call | solution.py:67
  146.6 5.6 %collective-permute-start.2 = (bf16[4,1120,128]{2,1,0:T(8,128)(2,1)}, bf16[4,1120,128]{2,1,0:T(8,128)(2,1)}, u32[]{:S(2)}, u32[]{:S(2)}) collective-permute-start(bf16[4,1120,128]{2,1,0:T(8,128)(2,1)} %get-tuple-element.23), channel_id=1, source_target_pairs={{0,8},{8,0},{1,9},{9,1},{2,10},{10,2},{3,11},{11,3},{4,12},{12,4},... | collective-permute-start | bytes 3440648 | tf_op jit(solution)/shard_map/ppermute | solution.py:49
  152.2 7.4 %all-to-all-start.4 = ((bf16[8,56,768]{2,1,0:T(8,128)(2,1)}), bf16[8,56,768]{2,1,0:T(8,128)(2,1)S(1)}, u32[]{:S(2)}, u32[]{:S(2)}) async-start(bf16[8,56,768]{2,1,0:T(8,128)(2,1)} %get-tuple-element.20), calls=%async_computation.4 | async-start | bytes 1376256 | tf_op jit(solution)/shard_map/all_to_all | solution.py:21
  159.7 0.2 dynamic-slice_reduce_fusion.1
  159.9 1.6 add_convert_fusion
  161.4 0.1 dynamic-slice_bitcast_fusion
  161.5 1.9 collective-permute-start.3
  163.5 5.3 %collective-permute-start.4 = (bf16[1120,128]{1,0:T(8,128)(2,1)S(1)}, bf16[1120,128]{1,0:T(8,128)(2,1)S(1)}, u32[]{:S(2)}, u32[]{:S(2)}) collective-permute-start(bf16[1120,128]{1,0:T(8,128)(2,1)S(1)} %get-tuple-element.43), channel_id=1, source_target_pairs={{0,32},{16,48},{32,0},{48,16},{1,33},{17,49},{33,1},{49,17},{2,34}... | collective-permute-start | bytes 860168 | tf_op jit(solution)/shard_map/ppermute | solution.py:49
  168.7 2.1 collective-permute-start.5
  170.8 10.4 %all-to-all-done.4 = bf16[8,56,768]{2,1,0:T(8,128)(2,1)S(1)} async-done(((bf16[8,56,768]{2,1,0:T(8,128)(2,1)}), bf16[8,56,768]{2,1,0:T(8,128)(2,1)S(1)}, u32[]{:S(2)}, u32[]{:S(2)}) %all-to-all-start.4) | async-done | bytes 688160 | tf_op jit(solution)/shard_map/all_to_all | solution.py:21
  181.2 0.2 slice_reduce_fusion.1
  181.5 20.5 %all_gather.11 = f32[8,5,128]{2,1,0:T(8,128)S(1)} all-gather(f32[1,5,128]{2,1,0:T(8,128)S(1)} %bitcast.72), channel_id=1, replica_groups=mesh['gx'=8,'yl'=4,'co'=2,'yh'=2,'xx'=4] {'yl','co'}, dimensions={0}, use_global_device_ids=true | all-gather | bytes 23040 | tf_op jit(solution)/shard_map/all_gather | solution.py:276
  202.0 0.6 reduce_sum.204
  202.6 0.7 multiply_convert_fusion.1
  203.3 0.8 shard_map.87
  (57 shorter events, 1.4 us)
Async XLA Ops:
  7.2 8.0 %copy-start.3 = (f32[640]{0:T(1024)S(1)}, f32[640]{0:T(1024)}, u32[]{:S(2)}) copy-start(f32[640]{0:T(1024)} %param.6) | copy-start | bytes 7684
  7.2 8.0 %copy-start.2 = (bf16[48,640]{1,0:T(8,128)(2,1)S(1)}, bf16[48,640]{1,0:T(8,128)(2,1)}, u32[]{:S(2)}) copy-start(bf16[48,640]{1,0:T(8,128)(2,1)} %param.5) | copy-start | bytes 184324
  7.2 8.0 %copy-start.4 = (bf16[48,640]{1,0:T(8,128)(2,1)S(1)}, bf16[48,640]{1,0:T(8,128)(2,1)}, u32[]{:S(2)}) copy-start(bf16[48,640]{1,0:T(8,128)(2,1)} %param.9) | copy-start | bytes 184324
  9.0 33.9 %all-to-all-start = ((bf16[4,80,896]{2,1,0:T(8,128)(2,1)}), bf16[4,80,896]{2,1,0:T(8,128)(2,1)S(1)}, u32[]{:S(2)}, u32[]{:S(2)}) async-start(bf16[4,80,896]{2,1,0:T(8,128)(2,1)} %broadcast_in_dim.12), calls=%async_computation | async-start | bytes 1146880 | tf_op jit(solution)/shard_map/all_to_all | solution.py:21
  14.4 44.8 %all-gather.2.cloned.1.call-start = ((), (), s32[]{:S(2)}) async-start(), calls=%async_computation.5 | async-start | bytes 1290240 | tf_op jit(solution)/shard_map/all_gather | solution.py:190
  42.9 9.9 %collective-permute-start = (bf16[4,80,896]{2,1,0:T(8,128)(2,1)S(1)}, bf16[4,80,896]{2,1,0:T(8,128)(2,1)S(1)}, u32[]{:S(2)}, u32[]{:S(2)}) collective-permute-start(bf16[4,80,896]{2,1,0:T(8,128)(2,1)S(1)} %all-to-all-done), channel_id=1, source_target_pairs={{0,8},{8,0},{1,9},{9,1},{2,10},{10,2},{3,11},{11,3},{4,12},{12,4},... | collective-permute-start | bytes 1720328 | tf_op jit(solution)/shard_map/ppermute | solution.py:49
  59.2 1.3 copy-start
  104.8 1.1 copy-start.1
  109.8 15.6 %all-to-all-start.2 = ((bf16[4,48,1920]{2,1,0:T(8,128)(2,1)}), bf16[4,48,1920]{2,1,0:T(8,128)(2,1)S(1)}, u32[]{:S(2)}, u32[]{:S(2)}) async-start(bf16[4,48,1920]{2,1,0:T(8,128)(2,1)} %broadcast_in_dim.14), calls=%async_computation.2 | async-start | bytes 1474560 | tf_op jit(solution)/shard_map/all_to_all | solution.py:21
  113.3 12.1 %collective-permute-start.1 = (bf16[48,1920]{1,0:T(8,128)(2,1)S(1)}, bf16[48,1920]{1,0:T(8,128)(2,1)S(1)}, u32[]{:S(2)}, u32[]{:S(2)}) collective-permute-start(bf16[48,1920]{1,0:T(8,128)(2,1)S(1)} %fusion.5), channel_id=1, source_target_pairs={{0,4},{4,0},{1,5},{5,1},{2,6},{6,2},{3,7},{7,3},{8,12},{12,8},{9,1... | collective-permute-start | bytes 552968 | tf_op jit(solution)/shard_map/ppermute | solution.py:49
  126.3 13.3 %all-to-all-start.3 = ((bf16[4,48,1920]{2,1,0:T(8,128)(2,1)}), bf16[4,48,1920]{2,1,0:T(8,128)(2,1)}, u32[]{:S(2)}, u32[]{:S(2)}) async-start(bf16[4,48,1920]{2,1,0:T(8,128)(2,1)} %broadcast_in_dim.15), calls=%async_computation.3 | async-start | bytes 1474560 | tf_op jit(solution)/shard_map/all_to_all | solution.py:21
  146.6 13.2 %collective-permute-start.2 = (bf16[4,1120,128]{2,1,0:T(8,128)(2,1)}, bf16[4,1120,128]{2,1,0:T(8,128)(2,1)}, u32[]{:S(2)}, u32[]{:S(2)}) collective-permute-start(bf16[4,1120,128]{2,1,0:T(8,128)(2,1)} %get-tuple-element.23), channel_id=1, source_target_pairs={{0,8},{8,0},{1,9},{9,1},{2,10},{10,2},{3,11},{11,3},{4,12},{12,4},... | collective-permute-start | bytes 3440648 | tf_op jit(solution)/shard_map/ppermute | solution.py:49
  152.2 28.9 %all-to-all-start.4 = ((bf16[8,56,768]{2,1,0:T(8,128)(2,1)}), bf16[8,56,768]{2,1,0:T(8,128)(2,1)S(1)}, u32[]{:S(2)}, u32[]{:S(2)}) async-start(bf16[8,56,768]{2,1,0:T(8,128)(2,1)} %get-tuple-element.20), calls=%async_computation.4 | async-start | bytes 1376256 | tf_op jit(solution)/shard_map/all_to_all | solution.py:21
  161.5 41.8 %collective-permute-start.3 = (bf16[1120,128]{1,0:T(8,128)(2,1)S(1)}, bf16[1120,128]{1,0:T(8,128)(2,1)S(1)}, u32[]{:S(2)}, u32[]{:S(2)}) collective-permute-start(bf16[1120,128]{1,0:T(8,128)(2,1)S(1)} %get-tuple-element.44), channel_id=1, source_target_pairs={{0,16},{16,0},{32,48},{48,32},{1,17},{17,1},{33,49},{49,33},{2,18}... | collective-permute-start | bytes 860168 | tf_op jit(solution)/shard_map/ppermute | solution.py:49
  163.5 39.9 %collective-permute-start.4 = (bf16[1120,128]{1,0:T(8,128)(2,1)S(1)}, bf16[1120,128]{1,0:T(8,128)(2,1)S(1)}, u32[]{:S(2)}, u32[]{:S(2)}) collective-permute-start(bf16[1120,128]{1,0:T(8,128)(2,1)S(1)} %get-tuple-element.43), channel_id=1, source_target_pairs={{0,32},{16,48},{32,0},{48,16},{1,33},{17,49},{33,1},{49,17},{2,34}... | collective-permute-start | bytes 860168 | tf_op jit(solution)/shard_map/ppermute | solution.py:49
  168.7 34.6 %collective-permute-start.5 = (bf16[1120,128]{1,0:T(8,128)(2,1)S(1)}, bf16[1120,128]{1,0:T(8,128)(2,1)S(1)}, u32[]{:S(2)}, u32[]{:S(2)}) collective-permute-start(bf16[1120,128]{1,0:T(8,128)(2,1)S(1)} %get-tuple-element.42), channel_id=1, source_target_pairs={{0,48},{16,32},{32,16},{48,0},{1,49},{17,33},{33,17},{49,1},{2,50}... | collective-permute-start | bytes 860168 | tf_op jit(solution)/shard_map/ppermute | solution.py:49
Sparse Core Ops, SparseCore 0:
  17.3 41.8 all-gather.1

commit v9 on v7

--- a/solution.py
+++ b/solution.py
@@ -101,7 +101,7 @@
 
 
 def tokens_kernel(
-    place_ref, own_ref, peer_ref, both_ref, up_ref, tilt_ref, gain_ref, tail_ref, z_ref, stats_ref
+    place_ref, own_ref, peer_ref, both_ref, up_ref, tilt_ref, gain_ref, tail_ref, z_ref
 ):
     n, high, _ = tail_ref.shape
     local, hid = up_ref.shape
@@ -117,7 +117,6 @@
             return jnp.sum(jnp.where(mine, marks, 0.0), axis=1, keepdims=True)
 
         cross, mean, inv = (taken(i) for i in range(3))
-        stats_ref[span, :] = jnp.where(lane == 0, mean, inv)
         normed = (both_ref[span, :local].astype(F32) - mean) * inv
         z_ref[span, :] = (normed * gain_ref[...]).astype(BF)
         d_z = dot(grad, up_ref[...], (1, 1))
@@ -242,12 +241,11 @@
     own, peer = (v.reshape(all_rows // 2, -1) for v in (own, spread(peer, "xx")))
 
     place = jnp.stack([lax.axis_index("co"), lax.axis_index("yh")])
-    tail, z, stats = local_call(
+    tail, z = local_call(
         tokens_kernel,
         (
             jax.ShapeDtypeStruct((n_gx, rows + 8, local + LANES), BF),
             jax.ShapeDtypeStruct((all_rows, local), BF),
-            jax.ShapeDtypeStruct((all_rows, LANES), F32),
         ),
         *(place, own, peer, both, up_full, jnp.sum(tilts, axis=0)[None], gain[None]),
         scalar=True,
@@ -287,9 +285,12 @@
 
     first = lax.axis_index("gx") * rows
 
-    stats = lax.dynamic_slice(stats, (first, 0), (rows, 2))
-    own_inv = stats[:, 1:]
-    own_normed = (x_in.astype(F32) - stats[:, :1]) * own_inv
+    half = n_gx // 2
+    marks = jnp.where(lax.axis_index("yh") == first // (rows * half), own, peer)
+    marks = marks.reshape(half, rows, -1)[:, :, 2 * hid :]
+    marks = lax.dynamic_index_in_dim(marks, lax.axis_index("gx") % half, keepdims=False)
+    own_mean, own_inv = column(marks, 1)[:, None], column(marks, 2)[:, None]
+    own_normed = (x_in.astype(F32) - own_mean) * own_inv
     d_x = own_inv * (d_z * gain - scaled_sum - own_normed * cross_sum)
     return (d_x.astype(BF), d_w_up, d_w_down, d_gain)
 

time: 207 us -> 203 us (0.981)
  starting transfers between devices: 58 us -> 74 us
  blocking collectives: 70.6 us -> 58 us
  waiting for transfers between devices: 38.9 us -> 31 us
    ppermute x9, starting transfers between devices: 37.5 us -> 55.5 us  [swap(): lax.ppermute(value, axis, [(i, i ^ bits) for i in range(lax.axis_size(axi...]
    all_to_all x1, blocking collectives: 42.9 us -> 29.8 us  [exchange(): return lax.all_to_all(blocks, axis, 0, 0, tiled=True)]
    all_gather x1, waiting for transfers between devices: 5.67 us -> 0.21 us  [body(): down_full = lax.all_gather(w_down, GY, axis=0, tiled=True)]
    all_to_all x4, starting transfers between devices: 20.5 us -> 18.4 us  [exchange(): return lax.all_to_all(blocks, axis, 0, 0, tiled=True)]
  transfers between devices with their start and end apart: 14 -> 14, of which waited for: 8 -> 7; matrix products, arithmetic and copies ran while one was open for 3% -> 4% of each run, Pallas kernels for 0% -> 0%
where the time goes in v9:
time: 203 us; the launch traced here: 202 us
  starting transfers between devices  74 us (36%)
  blocking collectives  58 us (29%)
  waiting for transfers between devices  31 us (15%)
  between operations  14.4 us (7%)
  Pallas kernels  9.24 us (5%)
  local copies, waits for them, and re-layouts  7.9 us (4%)
  other arithmetic  7.58 us (4%)
    ppermute x9, starting transfers between devices, swap(): lax.ppermute(value, axis, [(i, i ^ bits) for i in range(lax.axis_size(axi...  55.5 us
    all_to_all x1, blocking collectives, exchange(): return lax.all_to_all(blocks, axis, 0, 0, tiled=True)  29.8 us
    all_gather x1, blocking collectives, body(): lax.all_gather(jnp.concatenate([x_in, d_out], axis=1), 'gx', axis=0, tile...  28.2 us
    all_to_all x4, starting transfers between devices, exchange(): return lax.all_to_all(blocks, axis, 0, 0, tiled=True)  18.4 us
    all_to_all x4, waiting for transfers between devices, exchange(): return lax.all_to_all(blocks, axis, 0, 0, tiled=True)  17.5 us
    ppermute x9, waiting for transfers between devices, swap(): lax.ppermute(value, axis, [(i, i ^ bits) for i in range(lax.axis_size(axi...  12.7 us
    pallas_call x4, Pallas kernels, local_call(): pl.pallas_call(kernel, out_shape=out, in_specs=specs, out_specs=jax.tree....  9.24 us
  transfers between devices with their start and end apart: 14, of which 7 were waited for; matrix products, arithmetic and copies ran while one was open for 4% of the time, Pallas kernels for 0%

profile of v9, /device:TPU:1, one launch (start us, length us, event | category | flops | bytes accessed | tf_op | source)
XLA Modules:
  0.0 202.4 jit_solution(3637668738959658992)
XLA Ops:
  7.2 0.7 all-gather.2.cloned.1.call-update
  7.9 1.8 broadcast_in_dim.12
  9.7 5.4 %all-to-all-start = ((bf16[4,80,896]{2,1,0:T(8,128)(2,1)}), bf16[4,80,896]{2,1,0:T(8,128)(2,1)S(1)}, u32[]{:S(2)}, u32[]{:S(2)}) async-start(bf16[4,80,896]{2,1,0:T(8,128)(2,1)} %broadcast_in_dim.12), calls=%async_computation | async-start | bytes 1146880 | tf_op jit(solution)/shard_map/all_to_all | solution.py:21
  15.2 28.2 %all_gather.6.both_ref = bf16[384,1280]{1,0:T(8,128)(2,1)S(1)} all-gather(bf16[48,1280]{1,0:T(8,128)(2,1)S(1)} %pad_maximum_fusion.1), channel_id=1, replica_groups=mesh['gx'=8,'yl'=4,'co'=2,'yh'=2,'xx'=4] {'gx'}, dimensions={0}, use_global_device_ids=true | all-gather | bytes 1105920 | tf_op jit(solution)/shard_map/all_gather | solution.py:191
  43.4 7.5 %collective-permute-start = (bf16[4,80,896]{2,1,0:T(8,128)(2,1)S(1)}, bf16[4,80,896]{2,1,0:T(8,128)(2,1)S(1)}, u32[]{:S(2)}, u32[]{:S(2)}) collective-permute-start(bf16[4,80,896]{2,1,0:T(8,128)(2,1)S(1)} %all-to-all-done), channel_id=1, source_target_pairs={{0,8},{8,0},{1,9},{9,1},{2,10},{10,2},{3,11},{11,3},{4,12},{12,4},... | collective-permute-start | bytes 1720328 | tf_op jit(solution)/shard_map/ppermute | solution.py:49
  51.0 0.1 convert_reduce_fusion.2
  51.1 0.3 fusion.3
  51.5 0.2 copy.24
  51.8 0.8 collective-permute-done
  52.7 0.1 pad_maximum_fusion
  52.8 0.3 convolution_reduce_fusion
  53.4 0.2 all-gather.2.cloned.1.call-done.down_ref
  53.6 1.3 copy-done
  54.8 1.4 shard_map.84
  56.2 29.8 %all_to_all.25 = bf16[8,48,1920]{2,1,0:T(8,128)(2,1)S(1)} all-to-all(bf16[8,48,1920]{2,1,0:T(8,128)(2,1)S(1)} %shard_map.84), channel_id=1, replica_groups=mesh['gx'=8,'yl'=4,'co'=2,'yh'=2,'xx'=4] {'yh','xx'}, dimensions={0} | all-to-all | bytes 2949120 | tf_op jit(solution)/shard_map/all_to_all | solution.py:21
  86.0 0.2 convert_reduce_fusion.6
  86.3 0.8 copy-done.1
  87.8 1.5 convert_reduce_fusion
  89.3 0.2 multiply_convert_fusion
  89.6 0.2 multiply_reduce_fusion
  90.0 0.9 broadcast_in_dim.14
  90.9 3.5 %all-to-all-start.2 = ((bf16[4,48,1920]{2,1,0:T(8,128)(2,1)}), bf16[4,48,1920]{2,1,0:T(8,128)(2,1)S(1)}, u32[]{:S(2)}, u32[]{:S(2)}) async-start(bf16[4,48,1920]{2,1,0:T(8,128)(2,1)} %broadcast_in_dim.14), calls=%async_computation.2 | async-start | bytes 1474560 | tf_op jit(solution)/shard_map/all_to_all | solution.py:21
  94.4 2.1 %collective-permute-start.1 = (bf16[48,1920]{1,0:T(8,128)(2,1)S(1)}, bf16[48,1920]{1,0:T(8,128)(2,1)S(1)}, u32[]{:S(2)}, u32[]{:S(2)}) collective-permute-start(bf16[48,1920]{1,0:T(8,128)(2,1)S(1)} %fusion.5), channel_id=1, source_target_pairs={{0,4},{4,0},{1,5},{5,1},{2,6},{6,2},{3,7},{7,3},{8,12},{12,8},{9,1... | collective-permute-start | bytes 552968 | tf_op jit(solution)/shard_map/ppermute | solution.py:49
  96.5 8.1 %collective-permute-done.1 = bf16[48,1920]{1,0:T(8,128)(2,1)S(1)} collective-permute-done((bf16[48,1920]{1,0:T(8,128)(2,1)S(1)}, bf16[48,1920]{1,0:T(8,128)(2,1)S(1)}, u32[]{:S(2)}, u32[]{:S(2)}) %collective-permute-start.1) | collective-permute-done | bytes 184352 | tf_op jit(solution)/shard_map/ppermute | solution.py:49
  104.6 0.9 broadcast_in_dim.15
  105.5 4.2 %all-to-all-start.3 = ((bf16[4,48,1920]{2,1,0:T(8,128)(2,1)}), bf16[4,48,1920]{2,1,0:T(8,128)(2,1)}, u32[]{:S(2)}, u32[]{:S(2)}) async-start(bf16[4,48,1920]{2,1,0:T(8,128)(2,1)} %broadcast_in_dim.15), calls=%async_computation.3 | async-start | bytes 1474560 | tf_op jit(solution)/shard_map/all_to_all | solution.py:21
  109.8 0.9 convert_reduce_fusion.7
  110.8 9.1 %all-to-all-done.3 = bf16[4,48,1920]{2,1,0:T(8,128)(2,1)} async-done(((bf16[4,48,1920]{2,1,0:T(8,128)(2,1)}), bf16[4,48,1920]{2,1,0:T(8,128)(2,1)}, u32[]{:S(2)}, u32[]{:S(2)}) %all-to-all-start.3) | async-done | bytes 737312 | tf_op jit(solution)/shard_map/all_to_all | solution.py:21
  119.9 3.0 %shard_map.85 = (bf16[8,56,768]{2,1,0:T(8,128)(2,1)}, bf16[384,640]{1,0:T(8,128)(2,1)S(1)}) custom-call(s32[2]{0:T(128)S(1)} %pad_add_fusion.place_ref, bf16[192,1920]{1,0:T(8,128)(2,1)S(1)} %bitcast.69, bf16[192,1920]{1,0:T(8,128)(2,1)} %bitcast.21.peer_ref, bf16[384,1280]{1,0:T(8,128)(2,1)S(1)} %all_gather.6.both_ref, bf16[640,896]{1,0:T(8,128)(2,1)S(1)} %bitcast.68, ...), custom_call_target="tpu_custom_call" | custom-call | tf_op jit(solution)/shard_map/pallas_call | solution.py:67
  122.9 4.1 %shard_map.86 = (bf16[4,1120,128]{2,1,0:T(8,128)(2,1)S(1)}, bf16[4,1120,128]{2,1,0:T(8,128)(2,1)}) custom-call(s32[2]{0:T(128)S(1)} %pad_add_fusion.place_ref, bf16[192,1920]{1,0:T(8,128)(2,1)S(1)} %bitcast.70, bf16[192,1920]{1,0:T(8,128)(2,1)} %bitcast.21.peer_ref, bf16[384,1280]{1,0:T(8,128)(2,1)S(1)} %all_gather.6.both_ref, ...), custom_call_target="tpu_custom_call" | custom-call | tf_op jit(solution)/shard_map/pallas_call | solution.py:67
  127.0 23.6 %collective-permute-start.2 = (bf16[4,1120,128]{2,1,0:T(8,128)(2,1)}, bf16[4,1120,128]{2,1,0:T(8,128)(2,1)}, u32[]{:S(2)}, u32[]{:S(2)}) collective-permute-start(bf16[4,1120,128]{2,1,0:T(8,128)(2,1)} %get-tuple-element.21), channel_id=1, source_target_pairs={{0,8},{8,0},{1,9},{9,1},{2,10},{10,2},{3,11},{11,3},{4,12},{12,4},... | collective-permute-start | bytes 3440648 | tf_op jit(solution)/shard_map/ppermute | solution.py:49
  150.5 5.3 %all-to-all-start.4 = ((bf16[8,56,768]{2,1,0:T(8,128)(2,1)}), bf16[8,56,768]{2,1,0:T(8,128)(2,1)S(1)}, u32[]{:S(2)}, u32[]{:S(2)}) async-start(bf16[8,56,768]{2,1,0:T(8,128)(2,1)} %get-tuple-element.18), calls=%async_computation.4 | async-start | bytes 1376256 | tf_op jit(solution)/shard_map/all_to_all | solution.py:21
  155.8 0.8 slice.145
  156.6 0.2 convert_reduce_fusion.10
  156.8 1.6 add_convert_fusion
  158.5 3.5 %collective-permute-start.5 = (bf16[1120,128]{1,0:T(8,128)(2,1)S(1)}, bf16[1120,128]{1,0:T(8,128)(2,1)S(1)}, u32[]{:S(2)}, u32[]{:S(2)}) collective-permute-start(bf16[1120,128]{1,0:T(8,128)(2,1)S(1)} %get-tuple-element.40), channel_id=1, source_target_pairs={{0,48},{16,32},{32,16},{48,0},{1,49},{17,33},{33,17},{49,1},{2,50}... | collective-permute-start | bytes 860168 | tf_op jit(solution)/shard_map/ppermute | solution.py:49
  162.0 4.7 %collective-permute-start.4 = (bf16[1120,128]{1,0:T(8,128)(2,1)S(1)}, bf16[1120,128]{1,0:T(8,128)(2,1)S(1)}, u32[]{:S(2)}, u32[]{:S(2)}) collective-permute-start(bf16[1120,128]{1,0:T(8,128)(2,1)S(1)} %get-tuple-element.41), channel_id=1, source_target_pairs={{0,32},{16,48},{32,0},{48,16},{1,33},{17,49},{33,1},{49,17},{2,34}... | collective-permute-start | bytes 860168 | tf_op jit(solution)/shard_map/ppermute | solution.py:49
  166.7 2.2 %collective-permute-start.3 = (bf16[1120,128]{1,0:T(8,128)(2,1)S(1)}, bf16[1120,128]{1,0:T(8,128)(2,1)S(1)}, u32[]{:S(2)}, u32[]{:S(2)}) collective-permute-start(bf16[1120,128]{1,0:T(8,128)(2,1)S(1)} %get-tuple-element.42), channel_id=1, source_target_pairs={{0,16},{16,0},{32,48},{48,32},{1,17},{17,1},{33,49},{49,33},{2,18}... | collective-permute-start | bytes 860168 | tf_op jit(solution)/shard_map/ppermute | solution.py:49
  168.9 8.4 %all-to-all-done.4 = bf16[8,56,768]{2,1,0:T(8,128)(2,1)S(1)} async-done(((bf16[8,56,768]{2,1,0:T(8,128)(2,1)}), bf16[8,56,768]{2,1,0:T(8,128)(2,1)S(1)}, u32[]{:S(2)}, u32[]{:S(2)}) %all-to-all-start.4) | async-done | bytes 688160 | tf_op jit(solution)/shard_map/all_to_all | solution.py:21
  177.3 1.9 collective-permute-start.6
  179.3 0.2 slice_reduce_fusion.1
  179.5 2.2 %collective-permute-done.6 = f32[640]{0:T(1024)S(1)} collective-permute-done((f32[640]{0:T(1024)S(1)}, f32[640]{0:T(1024)S(1)}, u32[]{:S(2)}, u32[]{:S(2)}) %collective-permute-start.6) | collective-permute-done | bytes 2592 | tf_op jit(solution)/shard_map/ppermute | solution.py:49
  181.7 6.3 %collective-permute-start.7 = (f32[640]{0:T(1024)S(1)}, f32[640]{0:T(1024)S(1)}, u32[]{:S(2)}, u32[]{:S(2)}) collective-permute-start(f32[640]{0:T(1024)S(1)} %add.146), channel_id=1, source_target_pairs={{0,32},{16,48},{32,0},{48,16},{1,33},{17,49},{33,1},{49,17},{2,34}... | collective-permute-start | bytes 7688 | tf_op jit(solution)/shard_map/ppermute | solution.py:49
  188.0 1.5 collective-permute-done.7
  189.5 3.8 %collective-permute-start.8 = (f32[640]{0:T(1024)S(1)}, f32[640]{0:T(1024)S(1)}, u32[]{:S(2)}, u32[]{:S(2)}) collective-permute-start(f32[640]{0:T(1024)S(1)} %add.147), channel_id=1, source_target_pairs={{0,8},{8,0},{1,9},{9,1},{2,10},{10,2},{3,11},{11,3},{4,12},{12,4},... | collective-permute-start | bytes 7688 | tf_op jit(solution)/shard_map/ppermute | solution.py:49
  193.3 0.7 multiply_convert_fusion.1
  194.1 0.6 add.148
  194.7 0.8 shard_map.87
  (71 shorter events, 2.0 us)
Async XLA Ops:
  7.2 8.0 %copy-start.4 = (f32[640]{0:T(1024)S(1)}, f32[640]{0:T(1024)}, u32[]{:S(2)}) copy-start(f32[640]{0:T(1024)} %param.6) | copy-start | bytes 7684
  7.2 8.0 %copy-start.2 = (bf16[48,640]{1,0:T(8,128)(2,1)S(1)}, bf16[48,640]{1,0:T(8,128)(2,1)}, u32[]{:S(2)}) copy-start(bf16[48,640]{1,0:T(8,128)(2,1)} %param.5) | copy-start | bytes 184324
  7.2 8.0 %copy-start.6 = (bf16[48,640]{1,0:T(8,128)(2,1)S(1)}, bf16[48,640]{1,0:T(8,128)(2,1)}, u32[]{:S(2)}) copy-start(bf16[48,640]{1,0:T(8,128)(2,1)} %param.9) | copy-start | bytes 184324
  7.2 46.4 %all-gather.2.cloned.1.call-start = ((), (), s32[]{:S(2)}) async-start(), calls=%async_computation.5 | async-start | bytes 1290240 | tf_op jit(solution)/shard_map/all_gather | solution.py:189
  9.7 33.7 %all-to-all-start = ((bf16[4,80,896]{2,1,0:T(8,128)(2,1)}), bf16[4,80,896]{2,1,0:T(8,128)(2,1)S(1)}, u32[]{:S(2)}, u32[]{:S(2)}) async-start(bf16[4,80,896]{2,1,0:T(8,128)(2,1)} %broadcast_in_dim.12), calls=%async_computation | async-start | bytes 1146880 | tf_op jit(solution)/shard_map/all_to_all | solution.py:21
  43.4 9.1 %collective-permute-start = (bf16[4,80,896]{2,1,0:T(8,128)(2,1)S(1)}, bf16[4,80,896]{2,1,0:T(8,128)(2,1)S(1)}, u32[]{:S(2)}, u32[]{:S(2)}) collective-permute-start(bf16[4,80,896]{2,1,0:T(8,128)(2,1)S(1)} %all-to-all-done), channel_id=1, source_target_pairs={{0,8},{8,0},{1,9},{9,1},{2,10},{10,2},{3,11},{11,3},{4,12},{12,4},... | collective-permute-start | bytes 1720328 | tf_op jit(solution)/shard_map/ppermute | solution.py:49
  53.6 1.3 copy-start
  86.0 1.1 copy-start.1
  90.9 13.7 %all-to-all-start.2 = ((bf16[4,48,1920]{2,1,0:T(8,128)(2,1)}), bf16[4,48,1920]{2,1,0:T(8,128)(2,1)S(1)}, u32[]{:S(2)}, u32[]{:S(2)}) async-start(bf16[4,48,1920]{2,1,0:T(8,128)(2,1)} %broadcast_in_dim.14), calls=%async_computation.2 | async-start | bytes 1474560 | tf_op jit(solution)/shard_map/all_to_all | solution.py:21
  94.4 10.2 %collective-permute-start.1 = (bf16[48,1920]{1,0:T(8,128)(2,1)S(1)}, bf16[48,1920]{1,0:T(8,128)(2,1)S(1)}, u32[]{:S(2)}, u32[]{:S(2)}) collective-permute-start(bf16[48,1920]{1,0:T(8,128)(2,1)S(1)} %fusion.5), channel_id=1, source_target_pairs={{0,4},{4,0},{1,5},{5,1},{2,6},{6,2},{3,7},{7,3},{8,12},{12,8},{9,1... | collective-permute-start | bytes 552968 | tf_op jit(solution)/shard_map/ppermute | solution.py:49
  105.5 14.3 %all-to-all-start.3 = ((bf16[4,48,1920]{2,1,0:T(8,128)(2,1)}), bf16[4,48,1920]{2,1,0:T(8,128)(2,1)}, u32[]{:S(2)}, u32[]{:S(2)}) async-start(bf16[4,48,1920]{2,1,0:T(8,128)(2,1)} %broadcast_in_dim.15), calls=%async_computation.3 | async-start | bytes 1474560 | tf_op jit(solution)/shard_map/all_to_all | solution.py:21
  127.0 29.9 %collective-permute-start.2 = (bf16[4,1120,128]{2,1,0:T(8,128)(2,1)}, bf16[4,1120,128]{2,1,0:T(8,128)(2,1)}, u32[]{:S(2)}, u32[]{:S(2)}) collective-permute-start(bf16[4,1120,128]{2,1,0:T(8,128)(2,1)} %get-tuple-element.21), channel_id=1, source_target_pairs={{0,8},{8,0},{1,9},{9,1},{2,10},{10,2},{3,11},{11,3},{4,12},{12,4},... | collective-permute-start | bytes 3440648 | tf_op jit(solution)/shard_map/ppermute | solution.py:49
  150.5 26.8 %all-to-all-start.4 = ((bf16[8,56,768]{2,1,0:T(8,128)(2,1)}), bf16[8,56,768]{2,1,0:T(8,128)(2,1)S(1)}, u32[]{:S(2)}, u32[]{:S(2)}) async-start(bf16[8,56,768]{2,1,0:T(8,128)(2,1)} %get-tuple-element.18), calls=%async_computation.4 | async-start | bytes 1376256 | tf_op jit(solution)/shard_map/all_to_all | solution.py:21
  158.4 34.9 %copy-start.3 = (bf16[48,640]{1,0:T(8,128)(2,1)S(1)}, bf16[48,640]{1,0:T(8,128)(2,1)}, u32[]{:S(2)}) copy-start(bf16[48,640]{1,0:T(8,128)(2,1)} %param.5) | copy-start | bytes 184324
  158.4 34.9 %copy-start.5 = (f32[640]{0:T(1024)S(1)}, f32[640]{0:T(1024)}, u32[]{:S(2)}) copy-start(f32[640]{0:T(1024)} %param.6) | copy-start | bytes 7684
  158.5 36.2 %collective-permute-start.5 = (bf16[1120,128]{1,0:T(8,128)(2,1)S(1)}, bf16[1120,128]{1,0:T(8,128)(2,1)S(1)}, u32[]{:S(2)}, u32[]{:S(2)}) collective-permute-start(bf16[1120,128]{1,0:T(8,128)(2,1)S(1)} %get-tuple-element.40), channel_id=1, source_target_pairs={{0,48},{16,32},{32,16},{48,0},{1,49},{17,33},{33,17},{49,1},{2,50}... | collective-permute-start | bytes 860168 | tf_op jit(solution)/shard_map/ppermute | solution.py:49
  162.0 32.7 %collective-permute-start.4 = (bf16[1120,128]{1,0:T(8,128)(2,1)S(1)}, bf16[1120,128]{1,0:T(8,128)(2,1)S(1)}, u32[]{:S(2)}, u32[]{:S(2)}) collective-permute-start(bf16[1120,128]{1,0:T(8,128)(2,1)S(1)} %get-tuple-element.41), channel_id=1, source_target_pairs={{0,32},{16,48},{32,0},{48,16},{1,33},{17,49},{33,1},{49,17},{2,34}... | collective-permute-start | bytes 860168 | tf_op jit(solution)/shard_map/ppermute | solution.py:49
  166.7 28.0 %collective-permute-start.3 = (bf16[1120,128]{1,0:T(8,128)(2,1)S(1)}, bf16[1120,128]{1,0:T(8,128)(2,1)S(1)}, u32[]{:S(2)}, u32[]{:S(2)}) collective-permute-start(bf16[1120,128]{1,0:T(8,128)(2,1)S(1)} %get-tuple-element.42), channel_id=1, source_target_pairs={{0,16},{16,0},{32,48},{48,32},{1,17},{17,1},{33,49},{49,33},{2,18}... | collective-permute-start | bytes 860168 | tf_op jit(solution)/shard_map/ppermute | solution.py:49
  177.3 4.4 %collective-permute-start.6 = (f32[640]{0:T(1024)S(1)}, f32[640]{0:T(1024)S(1)}, u32[]{:S(2)}, u32[]{:S(2)}) collective-permute-start(f32[640]{0:T(1024)S(1)} %convert_reduce_fusion.8), channel_id=1, source_target_pairs={{0,16},{16,0},{32,48},{48,32},{1,17},{17,1},{33,49},{49,33},{2,18}... | collective-permute-start | bytes 7688 | tf_op jit(solution)/shard_map/ppermute | solution.py:49
  181.7 7.8 %collective-permute-start.7 = (f32[640]{0:T(1024)S(1)}, f32[640]{0:T(1024)S(1)}, u32[]{:S(2)}, u32[]{:S(2)}) collective-permute-start(f32[640]{0:T(1024)S(1)} %add.146), channel_id=1, source_target_pairs={{0,32},{16,48},{32,0},{48,16},{1,33},{17,49},{33,1},{49,17},{2,34}... | collective-permute-start | bytes 7688 | tf_op jit(solution)/shard_map/ppermute | solution.py:49
  189.5 4.6 %collective-permute-start.8 = (f32[640]{0:T(1024)S(1)}, f32[640]{0:T(1024)S(1)}, u32[]{:S(2)}, u32[]{:S(2)}) collective-permute-start(f32[640]{0:T(1024)S(1)} %add.147), channel_id=1, source_target_pairs={{0,8},{8,0},{1,9},{9,1},{2,10},{10,2},{3,11},{11,3},{4,12},{12,4},... | collective-permute-start | bytes 7688 | tf_op jit(solution)/shard_map/ppermute | solution.py:49
Sparse Core Ops, SparseCore 0:
  10.1 43.4 all-gather.1

commit v10 on v9

--- a/solution.py
+++ b/solution.py
@@ -139,15 +139,13 @@
 
 
 def grads_kernel(
-    place_ref, own_ref, peer_ref, both_ref, z_ref, keep_ref, give_ref, down_ref, up_ref
+    place_ref, own_ref, peer_ref, both_ref, z_ref, keep_ref, give_ref, down_ref, up_ref, all_ref
 ):
     hid, local = down_ref.shape
-    down, up = 0.0, 0.0
     for ref, _, span in halves(place_ref[1], own_ref, peer_ref):
-        down = down + dot(ref[:, :hid], both_ref[span, local:], (0, 0))
-        up = up + dot(z_ref[span, :], ref[:, hid : 2 * hid], (0, 0))
-    down_ref[...] = down.astype(BF)
-    up_ref[...] = up.astype(BF)
+        all_ref[span, :] = ref[:, : 2 * hid]
+    down_ref[...] = dot(all_ref[:, :hid], both_ref[:, local:], (0, 0)).astype(BF)
+    up_ref[...] = dot(z_ref[...], all_ref[:, hid:], (0, 0)).astype(BF)
     core = place_ref[0]
     n = keep_ref.shape[0]
     for ref, which in ((keep_ref, core), (give_ref, 1 - core)):
@@ -257,7 +255,7 @@
         grads_kernel,
         (jax.ShapeDtypeStruct((n_yl, packed, LANES), BF),) * 2,
         *(place, own, peer, both, z),
-        scratch=(pltpu.VMEM((hid, local), BF), pltpu.VMEM((local, hid), BF)),
+        scratch=[pltpu.VMEM(v, BF) for v in ((hid, local), (local, hid), (all_rows, 2 * hid))],
         scalar=True,
     )
     grads = (keep.astype(F32) + other_core(give).astype(F32)).astype(BF)
@@ -286,6 +284,7 @@
     first = lax.axis_index("gx") * rows
 
     half = n_gx // 2
+    own, peer, d_z = lax.optimization_barrier((own, peer, d_z))
     marks = jnp.where(lax.axis_index("yh") == first // (rows * half), own, peer)
     marks = marks.reshape(half, rows, -1)[:, :, 2 * hid :]
     marks = lax.dynamic_index_in_dim(marks, lax.axis_index("gx") % half, keepdims=False)

time: 203 us -> 203 us (level)
  no operation moved by 1% of the time
where the time goes in v10:
time: 203 us; the launch traced here: 202 us
  starting transfers between devices  73.9 us (36%)
  blocking collectives  58 us (29%)
  waiting for transfers between devices  30.9 us (15%)
  between operations  14.4 us (7%)
  Pallas kernels  9.19 us (5%)
  local copies, waits for them, and re-layouts  7.98 us (4%)
  other arithmetic  7.66 us (4%)
    ppermute x9, starting transfers between devices, swap(): lax.ppermute(value, axis, [(i, i ^ bits) for i in range(lax.axis_size(axi...  55.5 us
    all_to_all x1, blocking collectives, exchange(): return lax.all_to_all(blocks, axis, 0, 0, tiled=True)  29.8 us
    all_gather x1, blocking collectives, body(): lax.all_gather(jnp.concatenate([x_in, d_out], axis=1), 'gx', axis=0, tile...  28.2 us
    all_to_all x4, starting transfers between devices, exchange(): return lax.all_to_all(blocks, axis, 0, 0, tiled=True)  18.4 us
    all_to_all x4, waiting for transfers between devices, exchange(): return lax.all_to_all(blocks, axis, 0, 0, tiled=True)  17.7 us
    ppermute x9, waiting for transfers between devices, swap(): lax.ppermute(value, axis, [(i, i ^ bits) for i in range(lax.axis_size(axi...  12.3 us
    pallas_call x4, Pallas kernels, local_call(): pl.pallas_call(kernel, out_shape=out, in_specs=specs, out_specs=jax.tree....  9.19 us
  transfers between devices with their start and end apart: 14, of which 7 were waited for; matrix products, arithmetic and copies ran while one was open for 4% of the time, Pallas kernels for 0%

profile of v10, /device:TPU:1, one launch (start us, length us, event | category | flops | bytes accessed | tf_op | source)
XLA Modules:
  0.0 202.3 jit_solution(272836302344781078)
XLA Ops:
  7.2 0.7 all-gather.2.cloned.1.call-update
  7.9 1.8 broadcast_in_dim.12
  9.7 5.4 %all-to-all-start = ((bf16[4,80,896]{2,1,0:T(8,128)(2,1)}), bf16[4,80,896]{2,1,0:T(8,128)(2,1)S(1)}, u32[]{:S(2)}, u32[]{:S(2)}) async-start(bf16[4,80,896]{2,1,0:T(8,128)(2,1)} %broadcast_in_dim.12), calls=%async_computation | async-start | bytes 1146880 | tf_op jit(solution)/shard_map/all_to_all | solution.py:21
  15.2 28.2 %all_gather.6.both_ref = bf16[384,1280]{1,0:T(8,128)(2,1)S(1)} all-gather(bf16[48,1280]{1,0:T(8,128)(2,1)S(1)} %pad_maximum_fusion.1), channel_id=1, replica_groups=mesh['gx'=8,'yl'=4,'co'=2,'yh'=2,'xx'=4] {'gx'}, dimensions={0}, use_global_device_ids=true | all-gather | bytes 1105920 | tf_op jit(solution)/shard_map/all_gather | solution.py:189
  43.4 7.5 %collective-permute-start = (bf16[4,80,896]{2,1,0:T(8,128)(2,1)S(1)}, bf16[4,80,896]{2,1,0:T(8,128)(2,1)S(1)}, u32[]{:S(2)}, u32[]{:S(2)}) collective-permute-start(bf16[4,80,896]{2,1,0:T(8,128)(2,1)S(1)} %all-to-all-done), channel_id=1, source_target_pairs={{0,8},{8,0},{1,9},{9,1},{2,10},{10,2},{3,11},{11,3},{4,12},{12,4},... | collective-permute-start | bytes 1720328 | tf_op jit(solution)/shard_map/ppermute | solution.py:49
  51.0 0.1 convert_reduce_fusion.2
  51.1 0.3 fusion.3
  51.5 0.2 copy.24
  51.8 0.8 collective-permute-done
  52.7 0.1 pad_maximum_fusion
  52.8 0.3 convolution_reduce_fusion
  53.4 0.2 all-gather.2.cloned.1.call-done.down_ref
  53.6 1.3 copy-done
  54.8 1.4 shard_map.84
  56.2 29.8 %all_to_all.25 = bf16[8,48,1920]{2,1,0:T(8,128)(2,1)S(1)} all-to-all(bf16[8,48,1920]{2,1,0:T(8,128)(2,1)S(1)} %shard_map.84), channel_id=1, replica_groups=mesh['gx'=8,'yl'=4,'co'=2,'yh'=2,'xx'=4] {'yh','xx'}, dimensions={0} | all-to-all | bytes 2949120 | tf_op jit(solution)/shard_map/all_to_all | solution.py:21
  86.0 0.2 convert_reduce_fusion.6
  86.3 0.8 copy-done.1
  87.8 1.5 convert_reduce_fusion
  89.3 0.2 multiply_convert_fusion
  89.6 0.2 multiply_reduce_fusion
  90.0 0.9 broadcast_in_dim.14
  90.9 3.5 %all-to-all-start.2 = ((bf16[4,48,1920]{2,1,0:T(8,128)(2,1)}), bf16[4,48,1920]{2,1,0:T(8,128)(2,1)S(1)}, u32[]{:S(2)}, u32[]{:S(2)}) async-start(bf16[4,48,1920]{2,1,0:T(8,128)(2,1)} %broadcast_in_dim.14), calls=%async_computation.2 | async-start | bytes 1474560 | tf_op jit(solution)/shard_map/all_to_all | solution.py:21
  94.4 2.1 %collective-permute-start.1 = (bf16[48,1920]{1,0:T(8,128)(2,1)S(1)}, bf16[48,1920]{1,0:T(8,128)(2,1)S(1)}, u32[]{:S(2)}, u32[]{:S(2)}) collective-permute-start(bf16[48,1920]{1,0:T(8,128)(2,1)S(1)} %fusion.5), channel_id=1, source_target_pairs={{0,4},{4,0},{1,5},{5,1},{2,6},{6,2},{3,7},{7,3},{8,12},{12,8},{9,1... | collective-permute-start | bytes 552968 | tf_op jit(solution)/shard_map/ppermute | solution.py:49
  96.5 8.1 %collective-permute-done.1 = bf16[48,1920]{1,0:T(8,128)(2,1)S(1)} collective-permute-done((bf16[48,1920]{1,0:T(8,128)(2,1)S(1)}, bf16[48,1920]{1,0:T(8,128)(2,1)S(1)}, u32[]{:S(2)}, u32[]{:S(2)}) %collective-permute-start.1) | collective-permute-done | bytes 184352 | tf_op jit(solution)/shard_map/ppermute | solution.py:49
  104.6 0.9 broadcast_in_dim.15
  105.5 4.2 %all-to-all-start.3 = ((bf16[4,48,1920]{2,1,0:T(8,128)(2,1)}), bf16[4,48,1920]{2,1,0:T(8,128)(2,1)}, u32[]{:S(2)}, u32[]{:S(2)}) async-start(bf16[4,48,1920]{2,1,0:T(8,128)(2,1)} %broadcast_in_dim.15), calls=%async_computation.3 | async-start | bytes 1474560 | tf_op jit(solution)/shard_map/all_to_all | solution.py:21
  109.8 0.9 convert_reduce_fusion.7
  110.8 9.1 %all-to-all-done.3 = bf16[4,48,1920]{2,1,0:T(8,128)(2,1)} async-done(((bf16[4,48,1920]{2,1,0:T(8,128)(2,1)}), bf16[4,48,1920]{2,1,0:T(8,128)(2,1)}, u32[]{:S(2)}, u32[]{:S(2)}) %all-to-all-start.3) | async-done | bytes 737312 | tf_op jit(solution)/shard_map/all_to_all | solution.py:21
  119.9 3.0 %shard_map.85 = (bf16[8,56,768]{2,1,0:T(8,128)(2,1)}, bf16[384,640]{1,0:T(8,128)(2,1)S(1)}) custom-call(s32[2]{0:T(128)S(1)} %pad_add_fusion.place_ref, bf16[192,1920]{1,0:T(8,128)(2,1)S(1)} %bitcast.70, bf16[192,1920]{1,0:T(8,128)(2,1)} %bitcast.18.peer_ref, bf16[384,1280]{1,0:T(8,128)(2,1)S(1)} %all_gather.6.both_ref, bf16[640,896]{1,0:T(8,128)(2,1)S(1)} %bitcast.69, ...), custom_call_target="tpu_custom_call" | custom-call | tf_op jit(solution)/shard_map/pallas_call | solution.py:67
  122.9 4.0 %shard_map.86 = (bf16[4,1120,128]{2,1,0:T(8,128)(2,1)S(1)}, bf16[4,1120,128]{2,1,0:T(8,128)(2,1)}) custom-call(s32[2]{0:T(128)S(1)} %pad_add_fusion.place_ref, bf16[192,1920]{1,0:T(8,128)(2,1)S(1)} %bitcast.71, bf16[192,1920]{1,0:T(8,128)(2,1)} %bitcast.18.peer_ref, bf16[384,1280]{1,0:T(8,128)(2,1)S(1)} %all_gather.6.both_ref, ...), custom_call_target="tpu_custom_call" | custom-call | tf_op jit(solution)/shard_map/pallas_call | solution.py:67
  126.9 23.5 %collective-permute-start.2 = (bf16[4,1120,128]{2,1,0:T(8,128)(2,1)}, bf16[4,1120,128]{2,1,0:T(8,128)(2,1)}, u32[]{:S(2)}, u32[]{:S(2)}) collective-permute-start(bf16[4,1120,128]{2,1,0:T(8,128)(2,1)} %get-tuple-element.27), channel_id=1, source_target_pairs={{0,8},{8,0},{1,9},{9,1},{2,10},{10,2},{3,11},{11,3},{4,12},{12,4},... | collective-permute-start | bytes 3440648 | tf_op jit(solution)/shard_map/ppermute | solution.py:49
  150.4 5.3 %all-to-all-start.4 = ((bf16[8,56,768]{2,1,0:T(8,128)(2,1)}), bf16[8,56,768]{2,1,0:T(8,128)(2,1)S(1)}, u32[]{:S(2)}, u32[]{:S(2)}) async-start(bf16[8,56,768]{2,1,0:T(8,128)(2,1)} %get-tuple-element.21), calls=%async_computation.4 | async-start | bytes 1376256 | tf_op jit(solution)/shard_map/all_to_all | solution.py:21
  155.7 1.6 add_convert_fusion
  157.3 1.0 dynamic-slice_bitcast_fusion
  158.3 3.5 %collective-permute-start.5 = (bf16[1120,128]{1,0:T(8,128)(2,1)}, bf16[1120,128]{1,0:T(8,128)(2,1)S(1)}, u32[]{:S(2)}, u32[]{:S(2)}) collective-permute-start(bf16[1120,128]{1,0:T(8,128)(2,1)} %get-tuple-element.46), channel_id=1, source_target_pairs={{0,48},{16,32},{32,16},{48,0},{1,49},{17,33},{33,17},{49,1},{2,50}... | collective-permute-start | bytes 860168 | tf_op jit(solution)/shard_map/ppermute | solution.py:49
  161.8 4.7 %collective-permute-start.4 = (bf16[1120,128]{1,0:T(8,128)(2,1)}, bf16[1120,128]{1,0:T(8,128)(2,1)S(1)}, u32[]{:S(2)}, u32[]{:S(2)}) collective-permute-start(bf16[1120,128]{1,0:T(8,128)(2,1)} %get-tuple-element.47), channel_id=1, source_target_pairs={{0,32},{16,48},{32,0},{48,16},{1,33},{17,49},{33,1},{49,17},{2,34}... | collective-permute-start | bytes 860168 | tf_op jit(solution)/shard_map/ppermute | solution.py:49
  166.4 2.2 %collective-permute-start.3 = (bf16[1120,128]{1,0:T(8,128)(2,1)}, bf16[1120,128]{1,0:T(8,128)(2,1)S(1)}, u32[]{:S(2)}, u32[]{:S(2)}) collective-permute-start(bf16[1120,128]{1,0:T(8,128)(2,1)} %get-tuple-element.48), channel_id=1, source_target_pairs={{0,16},{16,0},{32,48},{48,32},{1,17},{17,1},{33,49},{49,33},{2,18}... | collective-permute-start | bytes 860168 | tf_op jit(solution)/shard_map/ppermute | solution.py:49
  168.6 8.6 %all-to-all-done.4 = bf16[8,56,768]{2,1,0:T(8,128)(2,1)S(1)} async-done(((bf16[8,56,768]{2,1,0:T(8,128)(2,1)}), bf16[8,56,768]{2,1,0:T(8,128)(2,1)S(1)}, u32[]{:S(2)}, u32[]{:S(2)}) %all-to-all-start.4) | async-done | bytes 688160 | tf_op jit(solution)/shard_map/all_to_all | solution.py:21
  177.3 1.9 collective-permute-start.6
  179.2 0.2 slice_reduce_fusion.1
  179.6 2.0 collective-permute-done.6
  181.6 6.3 %collective-permute-start.7 = (f32[640]{0:T(1024)S(1)}, f32[640]{0:T(1024)S(1)}, u32[]{:S(2)}, u32[]{:S(2)}) collective-permute-start(f32[640]{0:T(1024)S(1)} %add.146), channel_id=1, source_target_pairs={{0,32},{16,48},{32,0},{48,16},{1,33},{17,49},{33,1},{49,17},{2,34}... | collective-permute-start | bytes 7688 | tf_op jit(solution)/shard_map/ppermute | solution.py:49
  187.9 0.2 convert_reduce_fusion.10
  188.1 1.4 collective-permute-done.7
  189.5 3.8 %collective-permute-start.8 = (f32[640]{0:T(1024)S(1)}, f32[640]{0:T(1024)S(1)}, u32[]{:S(2)}, u32[]{:S(2)}) collective-permute-start(f32[640]{0:T(1024)S(1)} %add.147), channel_id=1, source_target_pairs={{0,8},{8,0},{1,9},{9,1},{2,10},{10,2},{3,11},{11,3},{4,12},{12,4},... | collective-permute-start | bytes 7688 | tf_op jit(solution)/shard_map/ppermute | solution.py:49
  193.3 0.7 multiply_convert_fusion.1
  194.1 0.6 add.148
  194.7 0.8 shard_map.87
  (71 shorter events, 2.0 us)
Async XLA Ops:
  7.2 8.0 %copy-start.4 = (f32[640]{0:T(1024)S(1)}, f32[640]{0:T(1024)}, u32[]{:S(2)}) copy-start(f32[640]{0:T(1024)} %param.6) | copy-start | bytes 7684
  7.2 8.0 %copy-start.2 = (bf16[48,640]{1,0:T(8,128)(2,1)S(1)}, bf16[48,640]{1,0:T(8,128)(2,1)}, u32[]{:S(2)}) copy-start(bf16[48,640]{1,0:T(8,128)(2,1)} %param.5) | copy-start | bytes 184324
  7.2 8.0 %copy-start.6 = (bf16[48,640]{1,0:T(8,128)(2,1)S(1)}, bf16[48,640]{1,0:T(8,128)(2,1)}, u32[]{:S(2)}) copy-start(bf16[48,640]{1,0:T(8,128)(2,1)} %param.9) | copy-start | bytes 184324
  7.2 46.4 %all-gather.2.cloned.1.call-start = ((), (), s32[]{:S(2)}) async-start(), calls=%async_computation.5 | async-start | bytes 1290240 | tf_op jit(solution)/shard_map/all_gather | solution.py:187
  9.7 33.7 %all-to-all-start = ((bf16[4,80,896]{2,1,0:T(8,128)(2,1)}), bf16[4,80,896]{2,1,0:T(8,128)(2,1)S(1)}, u32[]{:S(2)}, u32[]{:S(2)}) async-start(bf16[4,80,896]{2,1,0:T(8,128)(2,1)} %broadcast_in_dim.12), calls=%async_computation | async-start | bytes 1146880 | tf_op jit(solution)/shard_map/all_to_all | solution.py:21
  43.4 9.1 %collective-permute-start = (bf16[4,80,896]{2,1,0:T(8,128)(2,1)S(1)}, bf16[4,80,896]{2,1,0:T(8,128)(2,1)S(1)}, u32[]{:S(2)}, u32[]{:S(2)}) collective-permute-start(bf16[4,80,896]{2,1,0:T(8,128)(2,1)S(1)} %all-to-all-done), channel_id=1, source_target_pairs={{0,8},{8,0},{1,9},{9,1},{2,10},{10,2},{3,11},{11,3},{4,12},{12,4},... | collective-permute-start | bytes 1720328 | tf_op jit(solution)/shard_map/ppermute | solution.py:49
  53.6 1.3 copy-start
  86.0 1.1 copy-start.1
  90.9 13.7 %all-to-all-start.2 = ((bf16[4,48,1920]{2,1,0:T(8,128)(2,1)}), bf16[4,48,1920]{2,1,0:T(8,128)(2,1)S(1)}, u32[]{:S(2)}, u32[]{:S(2)}) async-start(bf16[4,48,1920]{2,1,0:T(8,128)(2,1)} %broadcast_in_dim.14), calls=%async_computation.2 | async-start | bytes 1474560 | tf_op jit(solution)/shard_map/all_to_all | solution.py:21
  94.4 10.2 %collective-permute-start.1 = (bf16[48,1920]{1,0:T(8,128)(2,1)S(1)}, bf16[48,1920]{1,0:T(8,128)(2,1)S(1)}, u32[]{:S(2)}, u32[]{:S(2)}) collective-permute-start(bf16[48,1920]{1,0:T(8,128)(2,1)S(1)} %fusion.5), channel_id=1, source_target_pairs={{0,4},{4,0},{1,5},{5,1},{2,6},{6,2},{3,7},{7,3},{8,12},{12,8},{9,1... | collective-permute-start | bytes 552968 | tf_op jit(solution)/shard_map/ppermute | solution.py:49
  105.5 14.3 %all-to-all-start.3 = ((bf16[4,48,1920]{2,1,0:T(8,128)(2,1)}), bf16[4,48,1920]{2,1,0:T(8,128)(2,1)}, u32[]{:S(2)}, u32[]{:S(2)}) async-start(bf16[4,48,1920]{2,1,0:T(8,128)(2,1)} %broadcast_in_dim.15), calls=%async_computation.3 | async-start | bytes 1474560 | tf_op jit(solution)/shard_map/all_to_all | solution.py:21
  126.9 28.8 %collective-permute-start.2 = (bf16[4,1120,128]{2,1,0:T(8,128)(2,1)}, bf16[4,1120,128]{2,1,0:T(8,128)(2,1)}, u32[]{:S(2)}, u32[]{:S(2)}) collective-permute-start(bf16[4,1120,128]{2,1,0:T(8,128)(2,1)} %get-tuple-element.27), channel_id=1, source_target_pairs={{0,8},{8,0},{1,9},{9,1},{2,10},{10,2},{3,11},{11,3},{4,12},{12,4},... | collective-permute-start | bytes 3440648 | tf_op jit(solution)/shard_map/ppermute | solution.py:49
  150.4 26.8 %all-to-all-start.4 = ((bf16[8,56,768]{2,1,0:T(8,128)(2,1)}), bf16[8,56,768]{2,1,0:T(8,128)(2,1)S(1)}, u32[]{:S(2)}, u32[]{:S(2)}) async-start(bf16[8,56,768]{2,1,0:T(8,128)(2,1)} %get-tuple-element.21), calls=%async_computation.4 | async-start | bytes 1376256 | tf_op jit(solution)/shard_map/all_to_all | solution.py:21
  158.3 36.4 %collective-permute-start.5 = (bf16[1120,128]{1,0:T(8,128)(2,1)}, bf16[1120,128]{1,0:T(8,128)(2,1)S(1)}, u32[]{:S(2)}, u32[]{:S(2)}) collective-permute-start(bf16[1120,128]{1,0:T(8,128)(2,1)} %get-tuple-element.46), channel_id=1, source_target_pairs={{0,48},{16,32},{32,16},{48,0},{1,49},{17,33},{33,17},{49,1},{2,50}... | collective-permute-start | bytes 860168 | tf_op jit(solution)/shard_map/ppermute | solution.py:49
  161.8 32.9 %collective-permute-start.4 = (bf16[1120,128]{1,0:T(8,128)(2,1)}, bf16[1120,128]{1,0:T(8,128)(2,1)S(1)}, u32[]{:S(2)}, u32[]{:S(2)}) collective-permute-start(bf16[1120,128]{1,0:T(8,128)(2,1)} %get-tuple-element.47), channel_id=1, source_target_pairs={{0,32},{16,48},{32,0},{48,16},{1,33},{17,49},{33,1},{49,17},{2,34}... | collective-permute-start | bytes 860168 | tf_op jit(solution)/shard_map/ppermute | solution.py:49
  166.4 28.2 %collective-permute-start.3 = (bf16[1120,128]{1,0:T(8,128)(2,1)}, bf16[1120,128]{1,0:T(8,128)(2,1)S(1)}, u32[]{:S(2)}, u32[]{:S(2)}) collective-permute-start(bf16[1120,128]{1,0:T(8,128)(2,1)} %get-tuple-element.48), channel_id=1, source_target_pairs={{0,16},{16,0},{32,48},{48,32},{1,17},{17,1},{33,49},{49,33},{2,18}... | collective-permute-start | bytes 860168 | tf_op jit(solution)/shard_map/ppermute | solution.py:49
  177.3 4.4 %collective-permute-start.6 = (f32[640]{0:T(1024)S(1)}, f32[640]{0:T(1024)S(1)}, u32[]{:S(2)}, u32[]{:S(2)}) collective-permute-start(f32[640]{0:T(1024)S(1)} %convert_reduce_fusion.8), channel_id=1, source_target_pairs={{0,16},{16,0},{32,48},{48,32},{1,17},{17,1},{33,49},{49,33},{2,18}... | collective-permute-start | bytes 7688 | tf_op jit(solution)/shard_map/ppermute | solution.py:49
  179.5 13.8 %copy-start.3 = (bf16[48,640]{1,0:T(8,128)(2,1)S(1)}, bf16[48,640]{1,0:T(8,128)(2,1)}, u32[]{:S(2)}) copy-start(bf16[48,640]{1,0:T(8,128)(2,1)} %param.5) | copy-start | bytes 184324
  179.5 13.8 %copy-start.5 = (f32[640]{0:T(1024)S(1)}, f32[640]{0:T(1024)}, u32[]{:S(2)}) copy-start(f32[640]{0:T(1024)} %param.6) | copy-start | bytes 7684
  181.6 7.9 %collective-permute-start.7 = (f32[640]{0:T(1024)S(1)}, f32[640]{0:T(1024)S(1)}, u32[]{:S(2)}, u32[]{:S(2)}) collective-permute-start(f32[640]{0:T(1024)S(1)} %add.146), channel_id=1, source_target_pairs={{0,32},{16,48},{32,0},{48,16},{1,33},{17,49},{33,1},{49,17},{2,34}... | collective-permute-start | bytes 7688 | tf_op jit(solution)/shard_map/ppermute | solution.py:49
  189.5 4.6 %collective-permute-start.8 = (f32[640]{0:T(1024)S(1)}, f32[640]{0:T(1024)S(1)}, u32[]{:S(2)}, u32[]{:S(2)}) collective-permute-start(f32[640]{0:T(1024)S(1)} %add.147), channel_id=1, source_target_pairs={{0,8},{8,0},{1,9},{9,1},{2,10},{10,2},{3,11},{11,3},{4,12},{12,4},... | collective-permute-start | bytes 7688 | tf_op jit(solution)/shard_map/ppermute | solution.py:49
Sparse Core Ops, SparseCore 0:
  10.1 43.4 all-gather.1

commit v11 on v10

--- a/solution.py
+++ b/solution.py
@@ -234,9 +234,15 @@
     marks = jnp.pad(marks, ((0, 0), (0, LANES - marks.shape[1])))
     acts = jnp.concatenate([act_f.astype(BF), d_hidden, marks], axis=1)
     peer = swap(acts, "yh", 1)
-    own = spread(acts, "xx")
-    own, peer = lax.optimization_barrier((own, peer))
-    own, peer = (v.reshape(all_rows // 2, -1) for v in (own, spread(peer, "xx")))
+    got1 = swap(acts, "xx", 1)
+    got2 = swap(acts, "xx", 2)
+    got3 = swap(acts, "xx", 3)
+    spot = lax.axis_index("xx")
+    got = jnp.stack([acts, got1, got2, got3])
+    own = jnp.concatenate(
+        [lax.dynamic_index_in_dim(got, spot ^ i, keepdims=False) for i in range(got.shape[0])]
+    )
+    peer = spread(peer, "xx").reshape(all_rows // 2, -1)
 
     place = jnp.stack([lax.axis_index("co"), lax.axis_index("yh")])
     tail, z = local_call(

time: 203 us -> 209 us (1.030)
  blocking collectives: 58 us -> 28.2 us
  waiting for transfers between devices: 30.9 us -> 46.3 us
  starting transfers between devices: 73.9 us -> 87.8 us
  other arithmetic: 7.66 us -> 14.5 us
    all_to_all x1 -> x0, blocking collectives: 29.8 us -> none  [exchange(): return lax.all_to_all(blocks, axis, 0, 0, tiled=True)]
    all_to_all x4, waiting for transfers between devices: 17.7 us -> 38.6 us  [exchange(): return lax.all_to_all(blocks, axis, 0, 0, tiled=True)]
    ppermute x9 -> x12, starting transfers between devices: 55.5 us -> 64.1 us  [swap(): lax.ppermute(value, axis, [(i, i ^ bits) for i in range(lax.axis_size(axi...]
    ppermute x9 -> x12, waiting for transfers between devices: 12.3 us -> 6.82 us  [swap(): lax.ppermute(value, axis, [(i, i ^ bits) for i in range(lax.axis_size(axi...]
    all_to_all x4, starting transfers between devices: 18.4 us -> 23.7 us  [exchange(): return lax.all_to_all(blocks, axis, 0, 0, tiled=True)]
  transfers between devices with their start and end apart: 14 -> 17, of which waited for: 7 -> 9; matrix products, arithmetic and copies ran while one was open for 4% -> 7% of each run, Pallas kernels for 0% -> 0%
where the time goes in v11:
time: 209 us; the launch traced here: 208 us
  starting transfers between devices  87.8 us (42%)
  waiting for transfers between devices  46.3 us (22%)
  blocking collectives  28.2 us (13%)
  other arithmetic  14.5 us (7%)
  between operations  14.5 us (7%)
  local copies, waits for them, and re-layouts  8.33 us (4%)
  Pallas kernels  8.03 us (4%)
    ppermute x12, starting transfers between devices, swap(): lax.ppermute(value, axis, [(i, i ^ bits) for i in range(lax.axis_size(axi...  64.1 us
    all_to_all x4, waiting for transfers between devices, exchange(): return lax.all_to_all(blocks, axis, 0, 0, tiled=True)  38.6 us
    all_gather x1, blocking collectives, body(): lax.all_gather(jnp.concatenate([x_in, d_out], axis=1), 'gx', axis=0, tile...  28.2 us
    all_to_all x4, starting transfers between devices, exchange(): return lax.all_to_all(blocks, axis, 0, 0, tiled=True)  23.7 us
    pallas_call x4, Pallas kernels, local_call(): pl.pallas_call(kernel, out_shape=out, in_specs=specs, out_specs=jax.tree....  8.03 us
    ppermute x12, waiting for transfers between devices, swap(): lax.ppermute(value, axis, [(i, i ^ bits) for i in range(lax.axis_size(axi...  6.82 us
  transfers between devices with their start and end apart: 17, of which 9 were waited for; matrix products, arithmetic and copies ran while one was open for 7% of the time, Pallas kernels for 0%

profile of v11, /device:TPU:1, one launch (start us, length us, event | category | flops | bytes accessed | tf_op | source)
XLA Modules:
  0.0 207.9 jit_solution(10160959932076675812)
XLA Ops:
  7.2 0.7 all-gather.2.cloned.1.call-update
  7.9 1.8 broadcast_in_dim.10
  9.7 5.4 %all-to-all-start = ((bf16[4,80,896]{2,1,0:T(8,128)(2,1)}), bf16[4,80,896]{2,1,0:T(8,128)(2,1)S(1)}, u32[]{:S(2)}, u32[]{:S(2)}) async-start(bf16[4,80,896]{2,1,0:T(8,128)(2,1)} %broadcast_in_dim.10), calls=%async_computation | async-start | bytes 1146880 | tf_op jit(solution)/shard_map/all_to_all | solution.py:21
  15.2 28.2 %all_gather.6.both_ref = bf16[384,1280]{1,0:T(8,128)(2,1)S(1)} all-gather(bf16[48,1280]{1,0:T(8,128)(2,1)S(1)} %pad_maximum_fusion.3), channel_id=1, replica_groups=mesh['gx'=8,'yl'=4,'co'=2,'yh'=2,'xx'=4] {'gx'}, dimensions={0}, use_global_device_ids=true | all-gather | bytes 1105920 | tf_op jit(solution)/shard_map/all_gather | solution.py:189
  43.4 7.5 %collective-permute-start = (bf16[4,80,896]{2,1,0:T(8,128)(2,1)S(1)}, bf16[4,80,896]{2,1,0:T(8,128)(2,1)S(1)}, u32[]{:S(2)}, u32[]{:S(2)}) collective-permute-start(bf16[4,80,896]{2,1,0:T(8,128)(2,1)S(1)} %all-to-all-done), channel_id=1, source_target_pairs={{0,8},{8,0},{1,9},{9,1},{2,10},{10,2},{3,11},{11,3},{4,12},{12,4},... | collective-permute-start | bytes 1720328 | tf_op jit(solution)/shard_map/ppermute | solution.py:49
  51.1 0.3 fusion.3
  51.7 0.8 collective-permute-done
  53.6 1.3 copy-done.4
  54.8 1.4 shard_map.84
  56.2 1.1 copy-done.3
  57.3 7.9 %all-to-all-start.1 = ((bf16[8,48,1920]{2,1,0:T(8,128)(2,1)}), bf16[8,48,1920]{2,1,0:T(8,128)(2,1)}, u32[]{:S(2)}, u32[]{:S(2)}) async-start(bf16[8,48,1920]{2,1,0:T(8,128)(2,1)} %copy-done.3), calls=%async_computation.1 | async-start | bytes 2949120 | tf_op jit(solution)/shard_map/all_to_all | solution.py:21
  65.3 20.7 %all-to-all-done.1 = bf16[8,48,1920]{2,1,0:T(8,128)(2,1)} async-done(((bf16[8,48,1920]{2,1,0:T(8,128)(2,1)}), bf16[8,48,1920]{2,1,0:T(8,128)(2,1)}, u32[]{:S(2)}, u32[]{:S(2)}) %all-to-all-start.1) | async-done | bytes 1474592 | tf_op jit(solution)/shard_map/all_to_all | solution.py:21
  86.0 1.2 convert_reduce_fusion.6
  87.3 0.9 fusion.12
  88.9 1.5 convert_reduce_fusion
  91.0 4.3 %collective-permute-start.3 = (bf16[48,1920]{1,0:T(8,128)(2,1)S(1)}, bf16[48,1920]{1,0:T(8,128)(2,1)}, u32[]{:S(2)}, u32[]{:S(2)}) collective-permute-start(bf16[48,1920]{1,0:T(8,128)(2,1)S(1)} %get-tuple-element.55), channel_id=1, source_target_pairs={{0,3},{1,2},{2,1},{3,0},{4,7},{5,6},{6,5},{7,4},{8,11},{9,10},{10,... | collective-permute-start | bytes 552968 | tf_op jit(solution)/shard_map/ppermute | solution.py:49
  95.4 2.5 %collective-permute-start.2 = (bf16[48,1920]{1,0:T(8,128)(2,1)S(1)}, bf16[48,1920]{1,0:T(8,128)(2,1)}, u32[]{:S(2)}, u32[]{:S(2)}) collective-permute-start(bf16[48,1920]{1,0:T(8,128)(2,1)S(1)} %get-tuple-element.55), channel_id=1, source_target_pairs={{0,2},{1,3},{2,0},{3,1},{4,6},{5,7},{6,4},{7,5},{8,10},{9,11},{10,... | collective-permute-start | bytes 552968 | tf_op jit(solution)/shard_map/ppermute | solution.py:49
  97.8 2.2 %collective-permute-start.1 = (bf16[48,1920]{1,0:T(8,128)(2,1)S(1)}, bf16[48,1920]{1,0:T(8,128)(2,1)}, u32[]{:S(2)}, u32[]{:S(2)}) collective-permute-start(bf16[48,1920]{1,0:T(8,128)(2,1)S(1)} %get-tuple-element.55), channel_id=1, source_target_pairs={{0,1},{1,0},{2,3},{3,2},{4,5},{5,4},{6,7},{7,6},{8,9},{9,8},{10,11... | collective-permute-start | bytes 552968 | tf_op jit(solution)/shard_map/ppermute | solution.py:49
  100.0 5.8 %collective-permute-start.4 = (bf16[48,1920]{1,0:T(8,128)(2,1)S(1)}, bf16[48,1920]{1,0:T(8,128)(2,1)S(1)}, u32[]{:S(2)}, u32[]{:S(2)}) collective-permute-start(bf16[48,1920]{1,0:T(8,128)(2,1)S(1)} %get-tuple-element.55), channel_id=1, source_target_pairs={{0,4},{4,0},{1,5},{5,1},{2,6},{6,2},{3,7},{7,3},{8,12},{12,8},{9,1... | collective-permute-start | bytes 552968 | tf_op jit(solution)/shard_map/ppermute | solution.py:49
  105.8 0.9 convert_reduce_fusion.7
  106.8 3.4 %collective-permute-done.4 = bf16[48,1920]{1,0:T(8,128)(2,1)S(1)} collective-permute-done((bf16[48,1920]{1,0:T(8,128)(2,1)S(1)}, bf16[48,1920]{1,0:T(8,128)(2,1)S(1)}, u32[]{:S(2)}, u32[]{:S(2)}) %collective-permute-start.4) | collective-permute-done | bytes 184352 | tf_op jit(solution)/shard_map/ppermute | solution.py:49
  110.2 0.9 broadcast_in_dim.12
  111.1 4.0 %all-to-all-start.2 = ((bf16[4,48,1920]{2,1,0:T(8,128)(2,1)}), bf16[4,48,1920]{2,1,0:T(8,128)(2,1)S(1)}, u32[]{:S(2)}, u32[]{:S(2)}) async-start(bf16[4,48,1920]{2,1,0:T(8,128)(2,1)} %broadcast_in_dim.12), calls=%async_computation.2 | async-start | bytes 1474560 | tf_op jit(solution)/shard_map/all_to_all | solution.py:21
  115.1 1.2 pad_maximum_fusion.1
  116.4 0.9 pad_maximum_fusion.2.own_ref
  117.4 7.9 %all-to-all-done.2 = bf16[4,48,1920]{2,1,0:T(8,128)(2,1)S(1)} async-done(((bf16[4,48,1920]{2,1,0:T(8,128)(2,1)}), bf16[4,48,1920]{2,1,0:T(8,128)(2,1)S(1)}, u32[]{:S(2)}, u32[]{:S(2)}) %all-to-all-start.2) | async-done | bytes 737312 | tf_op jit(solution)/shard_map/all_to_all | solution.py:21
  125.3 1.1 copy-done
  126.4 2.4 %shard_map.85 = (bf16[8,56,768]{2,1,0:T(8,128)(2,1)}, bf16[384,640]{1,0:T(8,128)(2,1)S(1)}) custom-call(s32[2]{0:T(128)S(1)} %pad_add_fusion.place_ref, bf16[192,1920]{1,0:T(8,128)(2,1)S(1)} %copy-done, bf16[192,1920]{1,0:T(8,128)(2,1)S(1)} %bitcast.82, bf16[384,1280]{1,0:T(8,128)(2,1)S(1)} %all_gather.6.both_ref, bf16[640,896]{1,0:T(8,128)(2,1)S(1)} %bitcast.81, ...), custom_call_target="tpu_custom_call" | custom-call | tf_op jit(solution)/shard_map/pallas_call | solution.py:67
  128.8 3.4 %shard_map.86 = (bf16[4,1120,128]{2,1,0:T(8,128)(2,1)S(1)}, bf16[4,1120,128]{2,1,0:T(8,128)(2,1)}) custom-call(s32[2]{0:T(128)S(1)} %pad_add_fusion.place_ref, bf16[192,1920]{1,0:T(8,128)(2,1)S(1)} %copy-done.1, bf16[192,1920]{1,0:T(8,128)(2,1)S(1)} %bitcast.83, bf16[384,1280]{1,0:T(8,128)(2,1)S(1)} %all_gather.6.both_ref, ...), custom_call_target="tpu_custom_call" | custom-call | tf_op jit(solution)/shard_map/pallas_call | solution.py:67
  132.3 23.0 %collective-permute-start.5 = (bf16[4,1120,128]{2,1,0:T(8,128)(2,1)}, bf16[4,1120,128]{2,1,0:T(8,128)(2,1)}, u32[]{:S(2)}, u32[]{:S(2)}) collective-permute-start(bf16[4,1120,128]{2,1,0:T(8,128)(2,1)} %get-tuple-element.23), channel_id=1, source_target_pairs={{0,8},{8,0},{1,9},{9,1},{2,10},{10,2},{3,11},{11,3},{4,12},{12,4},... | collective-permute-start | bytes 3440648 | tf_op jit(solution)/shard_map/ppermute | solution.py:49
  155.3 6.4 %all-to-all-start.3 = ((bf16[8,56,768]{2,1,0:T(8,128)(2,1)}), bf16[8,56,768]{2,1,0:T(8,128)(2,1)}, u32[]{:S(2)}, u32[]{:S(2)}) async-start(bf16[8,56,768]{2,1,0:T(8,128)(2,1)} %get-tuple-element.17), calls=%async_computation.3 | async-start | bytes 1376256 | tf_op jit(solution)/shard_map/all_to_all | solution.py:21
  161.7 1.6 add_convert_fusion
  163.3 0.8 dynamic-slice_bitcast_fusion
  164.1 2.5 %collective-permute-start.8 = (bf16[1120,128]{1,0:T(8,128)(2,1)}, bf16[1120,128]{1,0:T(8,128)(2,1)S(1)}, u32[]{:S(2)}, u32[]{:S(2)}) collective-permute-start(bf16[1120,128]{1,0:T(8,128)(2,1)} %get-tuple-element.42), channel_id=1, source_target_pairs={{0,48},{16,32},{32,16},{48,0},{1,49},{17,33},{33,17},{49,1},{2,50}... | collective-permute-start | bytes 860168 | tf_op jit(solution)/shard_map/ppermute | solution.py:49
  166.6 3.4 %collective-permute-start.7 = (bf16[1120,128]{1,0:T(8,128)(2,1)S(1)}, bf16[1120,128]{1,0:T(8,128)(2,1)S(1)}, u32[]{:S(2)}, u32[]{:S(2)}) collective-permute-start(bf16[1120,128]{1,0:T(8,128)(2,1)S(1)} %get-tuple-element.43), channel_id=1, source_target_pairs={{0,32},{16,48},{32,0},{48,16},{1,33},{17,49},{33,1},{49,17},{2,34}... | collective-permute-start | bytes 860168 | tf_op jit(solution)/shard_map/ppermute | solution.py:49
  169.9 3.4 %collective-permute-start.6 = (bf16[1120,128]{1,0:T(8,128)(2,1)S(1)}, bf16[1120,128]{1,0:T(8,128)(2,1)S(1)}, u32[]{:S(2)}, u32[]{:S(2)}) collective-permute-start(bf16[1120,128]{1,0:T(8,128)(2,1)S(1)} %get-tuple-element.44), channel_id=1, source_target_pairs={{0,16},{16,0},{32,48},{48,32},{1,17},{17,1},{33,49},{49,33},{2,18}... | collective-permute-start | bytes 860168 | tf_op jit(solution)/shard_map/ppermute | solution.py:49
  173.4 9.9 %all-to-all-done.3 = bf16[8,56,768]{2,1,0:T(8,128)(2,1)} async-done(((bf16[8,56,768]{2,1,0:T(8,128)(2,1)}), bf16[8,56,768]{2,1,0:T(8,128)(2,1)}, u32[]{:S(2)}, u32[]{:S(2)}) %all-to-all-start.3) | async-done | bytes 688160 | tf_op jit(solution)/shard_map/all_to_all | solution.py:21
  183.3 0.9 convert_reduce_fusion.8
  184.2 1.9 collective-permute-start.9
  186.2 0.9 convert_reduce_fusion.4
  187.3 1.1 convert_reduce_fusion.3
  188.6 0.7 collective-permute-done.9
  189.3 3.2 %collective-permute-start.10 = (f32[640]{0:T(1024)S(1)}, f32[640]{0:T(1024)S(1)}, u32[]{:S(2)}, u32[]{:S(2)}) collective-permute-start(f32[640]{0:T(1024)S(1)} %add.163), channel_id=1, source_target_pairs={{0,32},{16,48},{32,0},{48,16},{1,33},{17,49},{33,1},{49,17},{2,34}... | collective-permute-start | bytes 7688 | tf_op jit(solution)/shard_map/ppermute | solution.py:49
  192.7 1.8 collective-permute-done.10
  194.5 4.3 %collective-permute-start.11 = (f32[640]{0:T(1024)S(1)}, f32[640]{0:T(1024)S(1)}, u32[]{:S(2)}, u32[]{:S(2)}) collective-permute-start(f32[640]{0:T(1024)S(1)} %add.164), channel_id=1, source_target_pairs={{0,8},{8,0},{1,9},{9,1},{2,10},{10,2},{3,11},{11,3},{4,12},{12,4},... | collective-permute-start | bytes 7688 | tf_op jit(solution)/shard_map/ppermute | solution.py:49
  198.9 0.7 multiply_convert_fusion.1
  199.7 0.6 add.165
  200.3 0.8 shard_map.87
  (80 shorter events, 3.6 us)
Async XLA Ops:
  7.2 8.0 %copy-start.6 = (f32[640]{0:T(1024)S(1)}, f32[640]{0:T(1024)}, u32[]{:S(2)}) copy-start(f32[640]{0:T(1024)} %param.6) | copy-start | bytes 7684
  7.2 8.0 %copy-start.5 = (bf16[48,640]{1,0:T(8,128)(2,1)S(1)}, bf16[48,640]{1,0:T(8,128)(2,1)}, u32[]{:S(2)}) copy-start(bf16[48,640]{1,0:T(8,128)(2,1)} %param.5) | copy-start | bytes 184324
  7.2 8.0 %copy-start.7 = (bf16[48,640]{1,0:T(8,128)(2,1)S(1)}, bf16[48,640]{1,0:T(8,128)(2,1)}, u32[]{:S(2)}) copy-start(bf16[48,640]{1,0:T(8,128)(2,1)} %param.9) | copy-start | bytes 184324
  7.2 46.4 %all-gather.2.cloned.1.call-start = ((), (), s32[]{:S(2)}) async-start(), calls=%async_computation.4 | async-start | bytes 1290240 | tf_op jit(solution)/shard_map/all_gather | solution.py:187
  9.7 33.7 %all-to-all-start = ((bf16[4,80,896]{2,1,0:T(8,128)(2,1)}), bf16[4,80,896]{2,1,0:T(8,128)(2,1)S(1)}, u32[]{:S(2)}, u32[]{:S(2)}) async-start(bf16[4,80,896]{2,1,0:T(8,128)(2,1)} %broadcast_in_dim.10), calls=%async_computation | async-start | bytes 1146880 | tf_op jit(solution)/shard_map/all_to_all | solution.py:21
  43.4 9.1 %collective-permute-start = (bf16[4,80,896]{2,1,0:T(8,128)(2,1)S(1)}, bf16[4,80,896]{2,1,0:T(8,128)(2,1)S(1)}, u32[]{:S(2)}, u32[]{:S(2)}) collective-permute-start(bf16[4,80,896]{2,1,0:T(8,128)(2,1)S(1)} %all-to-all-done), channel_id=1, source_target_pairs={{0,8},{8,0},{1,9},{9,1},{2,10},{10,2},{3,11},{11,3},{4,12},{12,4},... | collective-permute-start | bytes 1720328 | tf_op jit(solution)/shard_map/ppermute | solution.py:49
  53.6 1.3 copy-start.4
  56.2 1.1 copy-start.3
  57.3 28.7 %all-to-all-start.1 = ((bf16[8,48,1920]{2,1,0:T(8,128)(2,1)}), bf16[8,48,1920]{2,1,0:T(8,128)(2,1)}, u32[]{:S(2)}, u32[]{:S(2)}) async-start(bf16[8,48,1920]{2,1,0:T(8,128)(2,1)} %copy-done.3), calls=%async_computation.1 | async-start | bytes 2949120 | tf_op jit(solution)/shard_map/all_to_all | solution.py:21
  91.0 24.1 %collective-permute-start.3 = (bf16[48,1920]{1,0:T(8,128)(2,1)S(1)}, bf16[48,1920]{1,0:T(8,128)(2,1)}, u32[]{:S(2)}, u32[]{:S(2)}) collective-permute-start(bf16[48,1920]{1,0:T(8,128)(2,1)S(1)} %get-tuple-element.55), channel_id=1, source_target_pairs={{0,3},{1,2},{2,1},{3,0},{4,7},{5,6},{6,5},{7,4},{8,11},{9,10},{10,... | collective-permute-start | bytes 552968 | tf_op jit(solution)/shard_map/ppermute | solution.py:49
  95.4 19.8 %collective-permute-start.2 = (bf16[48,1920]{1,0:T(8,128)(2,1)S(1)}, bf16[48,1920]{1,0:T(8,128)(2,1)}, u32[]{:S(2)}, u32[]{:S(2)}) collective-permute-start(bf16[48,1920]{1,0:T(8,128)(2,1)S(1)} %get-tuple-element.55), channel_id=1, source_target_pairs={{0,2},{1,3},{2,0},{3,1},{4,6},{5,7},{6,4},{7,5},{8,10},{9,11},{10,... | collective-permute-start | bytes 552968 | tf_op jit(solution)/shard_map/ppermute | solution.py:49
  97.8 17.3 %collective-permute-start.1 = (bf16[48,1920]{1,0:T(8,128)(2,1)S(1)}, bf16[48,1920]{1,0:T(8,128)(2,1)}, u32[]{:S(2)}, u32[]{:S(2)}) collective-permute-start(bf16[48,1920]{1,0:T(8,128)(2,1)S(1)} %get-tuple-element.55), channel_id=1, source_target_pairs={{0,1},{1,0},{2,3},{3,2},{4,5},{5,4},{6,7},{7,6},{8,9},{9,8},{10,11... | collective-permute-start | bytes 552968 | tf_op jit(solution)/shard_map/ppermute | solution.py:49
  100.0 10.2 %collective-permute-start.4 = (bf16[48,1920]{1,0:T(8,128)(2,1)S(1)}, bf16[48,1920]{1,0:T(8,128)(2,1)S(1)}, u32[]{:S(2)}, u32[]{:S(2)}) collective-permute-start(bf16[48,1920]{1,0:T(8,128)(2,1)S(1)} %get-tuple-element.55), channel_id=1, source_target_pairs={{0,4},{4,0},{1,5},{5,1},{2,6},{6,2},{3,7},{7,3},{8,12},{12,8},{9,1... | collective-permute-start | bytes 552968 | tf_op jit(solution)/shard_map/ppermute | solution.py:49
  111.1 14.1 %all-to-all-start.2 = ((bf16[4,48,1920]{2,1,0:T(8,128)(2,1)}), bf16[4,48,1920]{2,1,0:T(8,128)(2,1)S(1)}, u32[]{:S(2)}, u32[]{:S(2)}) async-start(bf16[4,48,1920]{2,1,0:T(8,128)(2,1)} %broadcast_in_dim.12), calls=%async_computation.2 | async-start | bytes 1474560 | tf_op jit(solution)/shard_map/all_to_all | solution.py:21
  125.3 1.1 copy-start
  126.4 2.4 %copy-start.1 = (bf16[192,1920]{1,0:T(8,128)(2,1)S(1)}, bf16[192,1920]{1,0:T(8,128)(2,1)}, u32[]{:S(2)}) copy-start(bf16[192,1920]{1,0:T(8,128)(2,1)} %pad_maximum_fusion.2.own_ref) | copy-start | bytes 2211844
  132.3 29.4 %collective-permute-start.5 = (bf16[4,1120,128]{2,1,0:T(8,128)(2,1)}, bf16[4,1120,128]{2,1,0:T(8,128)(2,1)}, u32[]{:S(2)}, u32[]{:S(2)}) collective-permute-start(bf16[4,1120,128]{2,1,0:T(8,128)(2,1)} %get-tuple-element.23), channel_id=1, source_target_pairs={{0,8},{8,0},{1,9},{9,1},{2,10},{10,2},{3,11},{11,3},{4,12},{12,4},... | collective-permute-start | bytes 3440648 | tf_op jit(solution)/shard_map/ppermute | solution.py:49
  155.3 28.0 %all-to-all-start.3 = ((bf16[8,56,768]{2,1,0:T(8,128)(2,1)}), bf16[8,56,768]{2,1,0:T(8,128)(2,1)}, u32[]{:S(2)}, u32[]{:S(2)}) async-start(bf16[8,56,768]{2,1,0:T(8,128)(2,1)} %get-tuple-element.17), calls=%async_computation.3 | async-start | bytes 1376256 | tf_op jit(solution)/shard_map/all_to_all | solution.py:21
  163.3 25.1 %copy-start.2 = (bf16[192,1920]{1,0:T(8,128)(2,1)S(1)}, bf16[192,1920]{1,0:T(8,128)(2,1)}, u32[]{:S(2)}) copy-start(bf16[192,1920]{1,0:T(8,128)(2,1)} %pad_maximum_fusion.2.own_ref) | copy-start | bytes 2211844
  164.1 36.2 %collective-permute-start.8 = (bf16[1120,128]{1,0:T(8,128)(2,1)}, bf16[1120,128]{1,0:T(8,128)(2,1)S(1)}, u32[]{:S(2)}, u32[]{:S(2)}) collective-permute-start(bf16[1120,128]{1,0:T(8,128)(2,1)} %get-tuple-element.42), channel_id=1, source_target_pairs={{0,48},{16,32},{32,16},{48,0},{1,49},{17,33},{33,17},{49,1},{2,50}... | collective-permute-start | bytes 860168 | tf_op jit(solution)/shard_map/ppermute | solution.py:49
  166.6 33.7 %collective-permute-start.7 = (bf16[1120,128]{1,0:T(8,128)(2,1)S(1)}, bf16[1120,128]{1,0:T(8,128)(2,1)S(1)}, u32[]{:S(2)}, u32[]{:S(2)}) collective-permute-start(bf16[1120,128]{1,0:T(8,128)(2,1)S(1)} %get-tuple-element.43), channel_id=1, source_target_pairs={{0,32},{16,48},{32,0},{48,16},{1,33},{17,49},{33,1},{49,17},{2,34}... | collective-permute-start | bytes 860168 | tf_op jit(solution)/shard_map/ppermute | solution.py:49
  169.9 30.3 %collective-permute-start.6 = (bf16[1120,128]{1,0:T(8,128)(2,1)S(1)}, bf16[1120,128]{1,0:T(8,128)(2,1)S(1)}, u32[]{:S(2)}, u32[]{:S(2)}) collective-permute-start(bf16[1120,128]{1,0:T(8,128)(2,1)S(1)} %get-tuple-element.44), channel_id=1, source_target_pairs={{0,16},{16,0},{32,48},{48,32},{1,17},{17,1},{33,49},{49,33},{2,18}... | collective-permute-start | bytes 860168 | tf_op jit(solution)/shard_map/ppermute | solution.py:49
  184.2 5.0 %collective-permute-start.9 = (f32[640]{0:T(1024)S(1)}, f32[640]{0:T(1024)S(1)}, u32[]{:S(2)}, u32[]{:S(2)}) collective-permute-start(f32[640]{0:T(1024)S(1)} %convert_reduce_fusion.8), channel_id=1, source_target_pairs={{0,16},{16,0},{32,48},{48,32},{1,17},{17,1},{33,49},{49,33},{2,18}... | collective-permute-start | bytes 7688 | tf_op jit(solution)/shard_map/ppermute | solution.py:49
  189.3 5.2 %collective-permute-start.10 = (f32[640]{0:T(1024)S(1)}, f32[640]{0:T(1024)S(1)}, u32[]{:S(2)}, u32[]{:S(2)}) collective-permute-start(f32[640]{0:T(1024)S(1)} %add.163), channel_id=1, source_target_pairs={{0,32},{16,48},{32,0},{48,16},{1,33},{17,49},{33,1},{49,17},{2,34}... | collective-permute-start | bytes 7688 | tf_op jit(solution)/shard_map/ppermute | solution.py:49
  194.5 5.1 %collective-permute-start.11 = (f32[640]{0:T(1024)S(1)}, f32[640]{0:T(1024)S(1)}, u32[]{:S(2)}, u32[]{:S(2)}) collective-permute-start(f32[640]{0:T(1024)S(1)} %add.164), channel_id=1, source_target_pairs={{0,8},{8,0},{1,9},{9,1},{2,10},{10,2},{3,11},{11,3},{4,12},{12,4},... | collective-permute-start | bytes 7688 | tf_op jit(solution)/shard_map/ppermute | solution.py:49
Sparse Core Ops, SparseCore 0:
  10.1 43.4 all-gather.1
